TPU v7x, 32 devices: a whole 2x2x4 slice. The times are simulated.
32 devices in a mesh: rows: 16 (over z, x, core), cols: 2 (over y).
Axes of the slice: x: 2, y: 2, z: 4, core: 2. Of those that a mesh axis runs over, the one named last changes fastest.
Arguments:
- slab: float32 [131072, 512], P('rows', 'cols')
- sign_bits: int32 [131072], P('rows'), may hold values from 0 to 1
- block_mask: int32 [1024], P('rows'), may hold values 0 or 1
- sample_rows: int32 [2048], P('rows'), may hold values from 0 to 8191, as said below
Outputs:
- sketch_rows: float32 [2048, 512], P('rows', 'cols')
- r_factor: float32 [512, 512], P(None, 'cols')
Inputs may be any that keep to these rules, and one draw needn't show every extreme that they name: `sample_rows`: each block of 128 entries names rows of the matching index of rows, as numbers below 8192; rows may repeat.
All inputs are finite; a program needn't handle non-finite values. No bound on the sum of `block_mask` on one device may be relied on, other than what follows from the above.
Results may differ from a plain program's by a relative error of at most 0.00016.
Values sent between devices are 32-bit elements; how exact they have to be, the bound alone decides.
No kernel may reach another device: no remote copies, remote signals or barrier semaphores. Data moves between devices by JAX's collectives and lax.ppermute only.
A program may use at most 64 MiB of HBM per device.

v0:
```python
import math

import jax
import jax.numpy as jnp
from jax import lax
from jax.sharding import PartitionSpec as P


def swapped(value, axis, bit):
    return lax.ppermute(value, axis, [(i, i ^ 1 << bit) for i in range(lax.axis_size(axis))])


def bit_parity(values, bit_total):
    total = jnp.zeros(values.shape, jnp.int32)
    for position in range(bit_total):
        total = total + jnp.bitwise_and(jnp.right_shift(values, position), 1)
    return jnp.bitwise_and(total, 1)


def sylvester(order_size):
    counter = jnp.arange(order_size, dtype=jnp.int32)
    common = jnp.bitwise_and(counter[:, None], counter[None, :])
    parity = bit_parity(common, max(order_size.bit_length(), 1))
    return (1 - 2 * parity).astype(jnp.float32)


def local_mix(scaled):
    block_count = scaled.shape[0]
    block_rows = scaled.shape[1]
    first_pass = jnp.einsum(
        "jb,rbc->rjc", sylvester(block_rows), scaled, precision=lax.Precision.HIGHEST
    )
    return jnp.einsum(
        "ir,rjc->ijc", sylvester(block_count), first_pass, precision=lax.Precision.HIGHEST
    )


def body(slab, sign_bits, block_mask, sample_rows):
    row_count, panel_width = slab.shape
    groups = lax.axis_size("rows")
    block_count = block_mask.shape[0]
    block_rows = row_count // block_count
    norm_scale = 1.0 / math.sqrt(row_count * groups)
    sign_values = (2 * sign_bits - 1).astype(jnp.float32)
    mask_values = block_mask.astype(jnp.float32)
    scaled = slab.reshape(block_count, block_rows, panel_width) * sign_values.reshape(
        block_count, block_rows, 1
    )
    scaled = scaled * mask_values.reshape(block_count, 1, 1)
    mixed_rows = local_mix(scaled).reshape(row_count, panel_width)
    pick_count = sample_rows.shape[0]
    device = lax.axis_index("rows")
    for bit_level in range(groups.bit_length() - 1):
        partner = swapped(mixed_rows, "rows", bit_level)
        high_bit = jnp.bitwise_and(jnp.right_shift(device, bit_level), 1)
        mixed_rows = jnp.where(high_bit == 0, mixed_rows + partner, partner - mixed_rows)
    sketch = jnp.take(mixed_rows, sample_rows, axis=0) * norm_scale
    full_rows = lax.all_gather(sketch, "cols", axis=1, tiled=True)
    panel_index = lax.axis_index("cols")
    local_gram = jnp.einsum("sa,sb->ab", full_rows, full_rows, precision=lax.Precision.HIGHEST)
    gram_matrix = lax.psum(local_gram, "rows")
    gram_matrix = gram_matrix / (pick_count * groups)
    lower_factor = jnp.linalg.cholesky(gram_matrix)
    upper_factor = lower_factor.T
    r_panel = lax.dynamic_slice_in_dim(upper_factor, panel_index * panel_width, panel_width, 1)
    return (sketch, r_panel)


def solution(mesh):
    in_specs = (P("rows", "cols"), P("rows"), P("rows"), P("rows"))
    out_specs = (P("rows", "cols"), P(None, "cols"))
    return jax.shard_map(body, mesh=mesh, in_specs=in_specs, out_specs=out_specs, check_vma=False)
```

profile of v0, /device:TPU:0, one launch (start us, length us, event | category | flops | bytes accessed | tf_op | source)
XLA Modules:
  0.0 1039.1 jit_solution(15961802083530760773)
XLA Ops:
  8.6 19.1 %fusion.2 = f32[64,256,128]{2,1,0:T(8,128)} fusion(f32[64,128,256]{2,1,0:T(8,128)} %bitcast.40, f32[64]{0:T(128)S(1)} %convert_element_type.14, f32[64,128]{1,0:T(8,128)S(1)} %convert_bitcast_fusion), kind=kOutput, calls=%fused_computation.7 | convolution fusion | flops 3225878528 | bytes 16810240 | tf_op jit(solution)/shard_map/jb,rbc->rjc/dot_general | solution.py:30
  27.8 9.2 copy.13
  36.9 10.2 fusion
  47.2 8.1 copy.9
  55.7 13.1 %collective-permute-done = f32[8192,256]{1,0:T(8,128)} collective-permute-done((f32[8192,256]{1,0:T(8,128)}, f32[8192,256]{1,0:T(8,128)}, u32[]{:S(2)}, u32[]{:S(2)}) %collective-permute-start) | collective-permute-done | bytes 8388640 | tf_op jit(solution)/shard_map/ppermute | solution.py:10
  68.8 10.1 subtract_select_fusion.3
  78.9 2.9 collective-permute-start.1
  81.7 181.1 %collective-permute-done.1 = f32[8192,256]{1,0:T(8,128)} collective-permute-done((f32[8192,256]{1,0:T(8,128)}, f32[8192,256]{1,0:T(8,128)}, u32[]{:S(2)}, u32[]{:S(2)}) %collective-permute-start.1) | collective-permute-done | bytes 8388640 | tf_op jit(solution)/shard_map/ppermute | solution.py:10
  262.8 10.1 subtract_select_fusion.2
  274.7 180.5 %collective-permute-done.2 = f32[8192,256]{1,0:T(8,128)} collective-permute-done((f32[8192,256]{1,0:T(8,128)}, f32[8192,256]{1,0:T(8,128)}, u32[]{:S(2)}, u32[]{:S(2)}) %collective-permute-start.2) | collective-permute-done | bytes 8388640 | tf_op jit(solution)/shard_map/ppermute | solution.py:10
  455.2 10.1 subtract_select_fusion.1
  465.3 2.5 collective-permute-start.3
  467.8 359.5 %collective-permute-done.3 = f32[8192,256]{1,0:T(8,128)} collective-permute-done((f32[8192,256]{1,0:T(8,128)}, f32[8192,256]{1,0:T(8,128)}, u32[]{:S(2)}, u32[]{:S(2)}) %collective-permute-start.3) | collective-permute-done | bytes 8388640 | tf_op jit(solution)/shard_map/ppermute | solution.py:10
  827.3 10.1 subtract_select_fusion
  837.4 4.1 gather_fusion
  841.6 5.9 all_gather.3
  849.6 94.7 %all-reduce.3.cloned.1.call-done = f32[512,512]{0,1:T(8,128)} async-done(((f32[512,512]{0,1:T(8,128)}), f32[512,512]{0,1:T(8,128)}) %all-reduce.3.cloned.1.call-update) | async-done | bytes 1048592 | tf_op jit(solution)/shard_map/psum | solution.py:61
  947.4 11.7 %cholesky.104 = f32[128,128]{1,0:T(8,128)S(1)} custom-call(f32[128,128]{1,0:T(8,128)S(1)} %cholesky.266), custom_call_target="Cholesky" | custom-call | tf_op jit(solution)/shard_map/jit(cholesky)/cholesky | solution.py:63
  959.3 9.8 custom-call.27
  969.7 12.0 %cholesky.217 = f32[128,128]{1,0:T(8,128)S(1)} custom-call(f32[128,128]{1,0:T(8,128)S(1)} %cholesky.270), custom_call_target="Cholesky" | custom-call | tf_op jit(solution)/shard_map/jit(cholesky)/cholesky | solution.py:63
  981.7 9.8 custom-call.28
  992.2 11.7 %cholesky.238 = f32[128,128]{1,0:T(8,128)S(1)} custom-call(f32[128,128]{1,0:T(8,128)S(1)} %cholesky.275), custom_call_target="Cholesky" | custom-call | tf_op jit(solution)/shard_map/jit(cholesky)/cholesky | solution.py:63
  1004.7 9.8 custom-call.29
  1015.1 11.7 %cholesky.255 = f32[128,128]{1,0:T(8,128)S(1)} custom-call(f32[128,128]{1,0:T(8,128)S(1)} %convolution_subtract_fusion.2), custom_call_target="Cholesky" | custom-call | tf_op jit(solution)/shard_map/jit(cholesky)/cholesky | solution.py:63
  (37 shorter events, 14.3 us)
Async XLA Ops:
  7.2 937.1 %all-reduce.3.cloned.1.call-start = ((), (), s32[]{:S(2)}) async-start(), calls=%async_computation | async-start | bytes 2097152 | tf_op jit(solution)/shard_map/psum | solution.py:61
  55.2 13.6 %collective-permute-start = (f32[8192,256]{1,0:T(8,128)}, f32[8192,256]{1,0:T(8,128)}, u32[]{:S(2)}, u32[]{:S(2)}) collective-permute-start(f32[8192,256]{1,0:T(8,128)} %bitcast.5), channel_id=1, source_target_pairs={{0,2},{2,0},{4,6},{6,4},{8,10},{10,8},{12,14},{14,12},{16,18},{18,... | collective-permute-start | bytes 25165832 | tf_op jit(solution)/shard_map/ppermute | solution.py:10
  78.9 183.9 %collective-permute-start.1 = (f32[8192,256]{1,0:T(8,128)}, f32[8192,256]{1,0:T(8,128)}, u32[]{:S(2)}, u32[]{:S(2)}) collective-permute-start(f32[8192,256]{1,0:T(8,128)} %subtract_select_fusion.3), channel_id=1, source_target_pairs={{0,4},{2,6},{4,0},{6,2},{8,12},{10,14},{12,8},{14,10},{16,20},{18,... | collective-permute-start | bytes 25165832 | tf_op jit(solution)/shard_map/ppermute | solution.py:10
  272.9 182.3 %collective-permute-start.2 = (f32[8192,256]{1,0:T(8,128)}, f32[8192,256]{1,0:T(8,128)}, u32[]{:S(2)}, u32[]{:S(2)}) collective-permute-start(f32[8192,256]{1,0:T(8,128)} %subtract_select_fusion.2), channel_id=1, source_target_pairs={{0,8},{2,10},{4,12},{6,14},{8,0},{10,2},{12,4},{14,6},{16,24},{18,... | collective-permute-start | bytes 25165832 | tf_op jit(solution)/shard_map/ppermute | solution.py:10
  274.7 193.1 %copy-start.1 = (s32[128]{0:T(128)S(1)}, s32[128]{0:T(128)}, u32[]{:S(2)}) copy-start(s32[128]{0:T(128)} %param.7) | copy-start | bytes 1540
  465.3 362.1 %collective-permute-start.3 = (f32[8192,256]{1,0:T(8,128)}, f32[8192,256]{1,0:T(8,128)}, u32[]{:S(2)}, u32[]{:S(2)}) collective-permute-start(f32[8192,256]{1,0:T(8,128)} %subtract_select_fusion.1), channel_id=1, source_target_pairs={{0,16},{2,18},{4,20},{6,22},{8,24},{10,26},{12,28},{14,30},{16,0},... | collective-permute-start | bytes 25165832 | tf_op jit(solution)/shard_map/ppermute | solution.py:10
  841.6 190.2 %copy-start = (f32[128,256]{1,0:T(8,128)}, f32[128,256]{1,0:T(8,128)S(1)}, u32[]{:S(2)}) copy-start(f32[128,256]{1,0:T(8,128)S(1)} %select_multiply_fusion) | copy-start | bytes 393220
Sparse Core Ops, SparseCore 0:
  849.7 94.5 all-reduce.2
where the time goes:
time: 1050 us; the launch traced here: 1040 us
  waiting for transfers between devices  829 us (79%)
  other arithmetic  123 us (12%)
  matrix products  33.3 us (3%)
  local copies, waits for them, and re-layouts  22.9 us (2%)
  between operations  17.2 us (2%)
    ppermute x4, waiting for transfers between devices, swapped(): lax.ppermute(value, axis, [(i, i ^ 1 << bit) for i in range(lax.axis_size...  734 us
    psum x1, waiting for transfers between devices, body(): gram_matrix = lax.psum(local_gram, 'rows')  94.7 us
    another operation x14, other arithmetic, body(): lower_factor = jnp.linalg.cholesky(gram_matrix)  78.7 us
    select_n x4, other arithmetic, body(): jnp.where(high_bit == 0, mixed_rows + partner, partner - mixed_rows)  40.3 us
  transfers between devices with their start and end apart: 5, of which 5 were waited for; matrix products, arithmetic and copies ran while one was open for 0% of the time, Pallas kernels for 0%

commit v1 on v0

v1 whole, which is shorter than its diff:
```python
import functools
import math

import jax
import jax.numpy as jnp
from jax import lax
from jax.experimental import pallas as pl
from jax.experimental.pallas import tpu as pltpu
from jax.sharding import PartitionSpec as P

TILE = 256
LANES = 128


def swapped(value, axis, bit):
    return lax.ppermute(value, axis, [(i, i ^ 1 << bit) for i in range(lax.axis_size(axis))])


def parity_sign(common):
    for shift in (16, 8, 4, 2, 1):
        common = common ^ (common >> shift)
    return 1 - 2 * (common & 1)


def butterfly(parts):
    stride = 1
    while stride < len(parts):
        for at in range(len(parts)):
            if at & stride == 0:
                low, high = parts[at], parts[at + stride]
                parts[at], parts[at + stride] = low + high, low - high
        stride *= 2
    return parts


def split_two(value):
    high = value.astype(jnp.bfloat16)
    low = (value - high.astype(jnp.float32)).astype(jnp.bfloat16)
    return high, low


def mix_kernel(mask_ref, pick_ref, slab_ref, sign_ref, send_ref, keep_ref, had_ref, mixed_ref,
               *, inner, outer, pick_count, groups, norm_scale):
    step = pl.program_id(0)
    width = slab_ref.shape[1]

    @pl.when(step == 0)
    def _():
        row = lax.broadcasted_iota(jnp.int32, (TILE, TILE), 0)
        col = lax.broadcasted_iota(jnp.int32, (TILE, TILE), 1)
        had_ref[...] = parity_sign(row & col).astype(jnp.float32).astype(jnp.bfloat16)

    parts = []
    per_tile = TILE // LANES
    for block in range(inner):
        signed = []
        for half in range(per_tile):
            at = block * per_tile + half
            mask = mask_ref[step * inner * per_tile + at]
            sign = (2 * sign_ref[at:at + 1, :] - 1) * mask
            sign = sign.astype(jnp.float32).astype(jnp.bfloat16)
            signed.append(had_ref[:, half * LANES:(half + 1) * LANES] * sign)
        left = jnp.concatenate(signed, axis=1)
        high, low = split_two(slab_ref[block * TILE:(block + 1) * TILE, :])
        mixed = jnp.dot(left, high, preferred_element_type=jnp.float32)
        mixed += jnp.dot(left, low, preferred_element_type=jnp.float32)
        parts.append(mixed)
    parts = butterfly(parts)
    for block in range(inner):
        at = pl.multiple_of((step * inner + block) * TILE, TILE)
        mixed_ref[pl.ds(at, TILE), :] = parts[block]

    @pl.when(step == outer - 1)
    def _():
        span = inner * TILE
        chunk = 8

        @pl.loop(0, span // chunk)
        def _(part):
            base = pl.multiple_of(part * chunk, chunk)
            values = [mixed_ref[pl.ds(base + group * span, chunk), :] for group in range(outer)]
            values = butterfly(values)
            for group in range(outer):
                mixed_ref[pl.ds(base + group * span, chunk), :] = values[group]

        device = lax.axis_index("rows")
        for out_ref, low_bit in ((keep_ref, 0), (send_ref, 1)):
            @pl.loop(0, groups // 2)
            def _(pair):
                owner = device ^ (2 * pair + low_bit)
                scale = parity_sign(owner & device).astype(jnp.float32) * norm_scale
                first = owner * pick_count

                @pl.loop(0, pick_count // 8)
                def _(octet):
                    rows = []
                    for sub in range(8):
                        index = pick_ref[first + octet * 8 + sub]
                        rows.append(mixed_ref[pl.ds(index, 1), :])
                    out_at = pl.multiple_of(pair * pick_count + octet * 8, 8)
                    out_ref[pl.ds(out_at, 8), :] = jnp.concatenate(rows, axis=0) * scale


def mix_and_pick(slab, sign_bits, block_mask, picks, groups):
    row_count, width = slab.shape
    pick_count = picks.shape[0] // groups
    inner = 4
    outer = row_count // (TILE * inner)
    norm_scale = 1.0 / math.sqrt(row_count * groups)
    half = jax.ShapeDtypeStruct((groups // 2 * pick_count, width), jnp.float32)
    span = inner * TILE
    return pl.pallas_call(
        functools.partial(mix_kernel, inner=inner, outer=outer, pick_count=pick_count,
                          groups=groups, norm_scale=norm_scale),
        grid=(outer,),
        in_specs=[
            pl.BlockSpec(memory_space=pltpu.SMEM),
            pl.BlockSpec(memory_space=pltpu.SMEM),
            pl.BlockSpec((span, width), lambda i: (i, 0)),
            pl.BlockSpec((span // LANES, LANES), lambda i: (i, 0)),
        ],
        out_specs=[pl.BlockSpec(half.shape, lambda i: (0, 0))] * 2,
        out_shape=[half, half],
        scratch_shapes=[
            pltpu.VMEM((TILE, TILE), jnp.bfloat16),
            pltpu.VMEM((row_count, width), jnp.float32),
        ],
        compiler_params=pltpu.CompilerParams(
            dimension_semantics=("arbitrary",), vmem_limit_bytes=48 << 20),
    )(block_mask, picks, slab, sign_bits.reshape(row_count // LANES, LANES))


def gather_rows(value, groups):
    device = lax.axis_index("rows")
    for bit in range(groups.bit_length() - 1):
        other = swapped(value, "rows", bit)
        high_bit = (device >> bit) & 1
        value = jnp.where(high_bit == 0, jnp.concatenate([value, other]), jnp.concatenate([other, value]))
    return value


def body(slab, sign_bits, block_mask, sample_rows):
    panel_width = slab.shape[1]
    groups = lax.axis_size("rows")
    bits = groups.bit_length() - 1
    pick_count = sample_rows.shape[0]
    picks = gather_rows(sample_rows, groups)
    send, keep = mix_and_pick(slab, sign_bits, block_mask, picks, groups)
    sketch = keep + swapped(send, "rows", 0)
    for bit in range(1, bits):
        parts = sketch.reshape(-1, 2, pick_count, panel_width)
        sketch = (parts[:, 0] + swapped(parts[:, 1].reshape(-1, panel_width), "rows", bit).reshape(parts[:, 0].shape))
        sketch = sketch.reshape(-1, panel_width)
    full_rows = lax.all_gather(sketch, "cols", axis=1, tiled=True)
    panel_index = lax.axis_index("cols")
    gram_matrix = jnp.einsum("sa,sb->ab", full_rows, full_rows, precision=lax.Precision.HIGHEST)
    for bit in range(bits):
        gram_matrix = gram_matrix + swapped(gram_matrix, "rows", bit)
    gram_matrix = gram_matrix / (pick_count * groups)
    lower_factor = jnp.linalg.cholesky(gram_matrix)
    upper_factor = lower_factor.T
    r_panel = lax.dynamic_slice_in_dim(upper_factor, panel_index * panel_width, panel_width, 1)
    return (sketch, r_panel)


def solution(mesh):
    in_specs = (P("rows", "cols"), P("rows"), P("rows"), P("rows"))
    out_specs = (P("rows", "cols"), P(None, "cols"))
    return jax.shard_map(body, mesh=mesh, in_specs=in_specs, out_specs=out_specs, check_vma=False)
```

time: 1050 us -> 258 us (0.25); the launches traced: 1040 us -> 258 us
  waiting for transfers between devices: 829 us -> 126 us
  other arithmetic: 123 us -> 80.7 us
  matrix products: 33.3 us -> 2.9 us
  local copies, waits for them, and re-layouts: 22.9 us -> 3.02 us
  Pallas kernels: 0 us -> 16.4 us
  between operations: 17.2 us -> 3.4 us
  starting transfers between devices: 7.7 us -> 20 us
    ppermute x4 -> x12, waiting for transfers between devices: 734 us -> 126 us  [swapped(): lax.ppermute(value, axis, [(i, i ^ 1 << bit) for i in range(lax.axis_size...]
    psum x1 -> x0, waiting for transfers between devices: 94.7 us -> none  [body(): gram_matrix = lax.psum(local_gram, 'rows')]
    select_n x5 -> x4, other arithmetic: 40.3 us -> 0.76 us  [gather_rows(): jnp.where(high_bit == 0, jnp.concatenate([value, other]), jnp.concatenate...]
    dot_general x2 -> x0, matrix products: 29.4 us -> none  [the longest x1 19.1 us: local_mix(): jnp.einsum('jb,rbc->rjc', sylvester(block_rows), scaled, precision=lax.Pr...]
    dot_general x2 -> x0, local copies, waits for them, and re-layouts: 17.2 us -> none  [the longest x1 9.17 us: local_mix(): jnp.einsum('jb,rbc->rjc', sylvester(block_rows), scaled, precision=lax.Pr...]
    pallas_call x0 -> x1, Pallas kernels: none -> 16.4 us  [mix_and_pick(): pl.pallas_call(functools.partial(mix_kernel, inner=inner, outer=outer, pi...]
    ppermute x4 -> x12, starting transfers between devices: 7.67 us -> 20 us  [swapped(): lax.ppermute(value, axis, [(i, i ^ 1 << bit) for i in range(lax.axis_size...]
  transfers between devices with their start and end apart: 5 -> 12, of which waited for: 5 -> 12; matrix products, arithmetic and copies ran while one was open for 0% -> 0% of each run, Pallas kernels for 0% -> 0%
where the time goes in v1:
time: 258 us
  waiting for transfers between devices  126 us (49%)
  other arithmetic  80.7 us (31%)
  starting transfers between devices  20 us (8%)
  Pallas kernels  16.4 us (6%)
  blocking collectives  5.64 us (2%)
  between operations  3.4 us (1%)
  local copies, waits for them, and re-layouts  3.02 us (1%)
  matrix products  2.9 us (1%)
    ppermute x12, waiting for transfers between devices, swapped(): lax.ppermute(value, axis, [(i, i ^ 1 << bit) for i in range(lax.axis_size...  126 us
    another operation x14, other arithmetic, body(): lower_factor = jnp.linalg.cholesky(gram_matrix)  78.6 us
    ppermute x12, starting transfers between devices, swapped(): lax.ppermute(value, axis, [(i, i ^ 1 << bit) for i in range(lax.axis_size...  20 us
    pallas_call x1, Pallas kernels, mix_and_pick(): pl.pallas_call(functools.partial(mix_kernel, inner=inner, outer=outer, pi...  16.4 us
    all_gather x1, blocking collectives, body(): full_rows = lax.all_gather(sketch, 'cols', axis=1, tiled=True)  5.64 us
  transfers between devices with their start and end apart: 12, of which 12 were waited for; matrix products, arithmetic and copies ran while one was open for 0% of the time, Pallas kernels for 0%

profile of v1, /device:TPU:0, one launch (start us, length us, event | category | flops | bytes accessed | tf_op | source)
XLA Modules:
  0.0 257.7 jit_solution(4578895490166034115)
XLA Ops:
  2.8 2.8 %collective-permute-start.1 = (s32[256]{0:T(256)S(1)}, s32[256]{0:T(256)S(1)}, u32[]{:S(2)}, u32[]{:S(2)}) collective-permute-start(s32[256]{0:T(256)S(1)} %add_select_fusion.3), channel_id=1, source_target_pairs={{0,4},{2,6},{4,0},{6,2},{8,12},{10,14},{12,8},{14,10},{16,20},{18,... | collective-permute-start | bytes 3080 | tf_op jit(solution)/shard_map/ppermute | solution.py:16
  7.2 2.1 collective-permute-start.2
  10.9 3.0 %collective-permute-start.3 = (s32[1024]{0:T(1024)S(1)}, s32[1024]{0:T(1024)S(1)}, u32[]{:S(2)}, u32[]{:S(2)}) collective-permute-start(s32[1024]{0:T(1024)S(1)} %add_select_fusion.1), channel_id=1, source_target_pairs={{0,16},{2,18},{4,20},{6,22},{8,24},{10,26},{12,28},{14,30},{16,0},... | collective-permute-start | bytes 12296 | tf_op jit(solution)/shard_map/ppermute | solution.py:16
  16.9 16.4 %shard_map.59 = (f32[1024,256]{1,0:T(8,128)S(1)}, f32[1024,256]{1,0:T(8,128)S(1)}) custom-call(s32[64]{0:T(128)S(1)} %copy-done.1, s32[2048]{0:T(1024)S(1)} %add_select_fusion.pick_ref, f32[8192,256]{1,0:T(8,128)} %slab_ref.1, s32[64,128]{1,0:T(8,128)S(1)} %bitcast.47), custom_call_target="tpu_custom_call" | custom-call | tf_op jit(solution)/shard_map/pallas_call | solution.py:112
  33.4 2.6 %collective-permute-done.4 = f32[1024,256]{1,0:T(8,128)S(1)} collective-permute-done((f32[1024,256]{1,0:T(8,128)S(1)}, f32[1024,256]{1,0:T(8,128)S(1)}, u32[]{:S(2)}, u32[]{:S(2)}) %collective-permute-start.4) | collective-permute-done | bytes 1048608 | tf_op jit(solution)/shard_map/ppermute | solution.py:16
  36.3 1.9 collective-permute-start.5
  38.2 12.2 %collective-permute-done.5 = f32[512,256]{1,0:T(8,128)S(1)} collective-permute-done((f32[512,256]{1,0:T(8,128)S(1)}, f32[512,256]{1,0:T(8,128)S(1)}, u32[]{:S(2)}, u32[]{:S(2)}) %collective-permute-start.5) | collective-permute-done | bytes 524320 | tf_op jit(solution)/shard_map/ppermute | solution.py:16
  50.5 1.9 collective-permute-start.6
  52.4 5.8 %collective-permute-done.6 = f32[256,256]{1,0:T(8,128)S(1)} collective-permute-done((f32[256,256]{1,0:T(8,128)S(1)}, f32[256,256]{1,0:T(8,128)S(1)}, u32[]{:S(2)}, u32[]{:S(2)}) %collective-permute-start.6) | collective-permute-done | bytes 262176 | tf_op jit(solution)/shard_map/ppermute | solution.py:16
  58.2 2.8 %collective-permute-start.7 = (f32[128,256]{1,0:T(8,128)S(1)}, f32[128,256]{1,0:T(8,128)S(1)}, u32[]{:S(2)}, u32[]{:S(2)}) collective-permute-start(f32[128,256]{1,0:T(8,128)S(1)} %slice_bitcast_fusion.1), channel_id=1, source_target_pairs={{0,16},{2,18},{4,20},{6,22},{8,24},{10,26},{12,28},{14,30},{16,0},... | collective-permute-start | bytes 393224 | tf_op jit(solution)/shard_map/ppermute | solution.py:16
  61.1 4.9 %collective-permute-done.7 = f32[128,256]{1,0:T(8,128)S(1)} collective-permute-done((f32[128,256]{1,0:T(8,128)S(1)}, f32[128,256]{1,0:T(8,128)S(1)}, u32[]{:S(2)}, u32[]{:S(2)}) %collective-permute-start.7) | collective-permute-done | bytes 131104 | tf_op jit(solution)/shard_map/ppermute | solution.py:16
  66.0 5.6 %all_gather.3 = f32[128,512]{1,0:T(8,128)S(1)} all-gather(f32[128,256]{1,0:T(8,128)S(1)} %fusion.10), channel_id=1, replica_groups=mesh['rows'=16,'cols'=2] {'cols'}, dimensions={1}, use_global_device_ids=true | all-gather | bytes 393216 | tf_op jit(solution)/shard_map/all_gather | solution.py:154
  72.7 2.6 %collective-permute-done.8 = f32[512,512]{0,1:T(8,128)S(1)} collective-permute-done((f32[512,512]{0,1:T(8,128)S(1)}, f32[512,512]{0,1:T(8,128)S(1)}, u32[]{:S(2)}, u32[]{:S(2)}) %collective-permute-start.8) | collective-permute-done | bytes 1048608 | tf_op jit(solution)/shard_map/ppermute | solution.py:16
  77.2 23.7 %collective-permute-done.9 = f32[512,512]{0,1:T(8,128)S(1)} collective-permute-done((f32[512,512]{0,1:T(8,128)S(1)}, f32[512,512]{0,1:T(8,128)S(1)}, u32[]{:S(2)}, u32[]{:S(2)}) %collective-permute-start.9) | collective-permute-done | bytes 1048608 | tf_op jit(solution)/shard_map/ppermute | solution.py:16
  101.8 23.7 %collective-permute-done.10 = f32[512,512]{0,1:T(8,128)S(1)} collective-permute-done((f32[512,512]{0,1:T(8,128)S(1)}, f32[512,512]{0,1:T(8,128)S(1)}, u32[]{:S(2)}, u32[]{:S(2)}) %collective-permute-start.10) | collective-permute-done | bytes 1048608 | tf_op jit(solution)/shard_map/ppermute | solution.py:16
  125.7 2.4 collective-permute-start.11
  128.1 44.5 %collective-permute-done.11 = f32[512,512]{0,1:T(8,128)S(1)} collective-permute-done((f32[512,512]{0,1:T(8,128)S(1)}, f32[512,512]{0,1:T(8,128)S(1)}, u32[]{:S(2)}, u32[]{:S(2)}) %collective-permute-start.11) | collective-permute-done | bytes 1048608 | tf_op jit(solution)/shard_map/ppermute | solution.py:16
  173.4 11.7 %cholesky.104 = f32[128,128]{1,0:T(8,128)S(1)} custom-call(f32[128,128]{1,0:T(8,128)S(1)} %cholesky.266), custom_call_target="Cholesky" | custom-call | tf_op jit(solution)/shard_map/jit(cholesky)/cholesky | solution.py:160
  185.2 9.8 %custom-call.27 = f32[1,128,128]{1,2,0:T(8,128)S(1)} custom-call(f32[1,128,128]{2,1,0:T(8,128)S(1)} %get-tuple-element.21), custom_call_target="InvertDiagBlocksLowerTriangular" | custom-call | tf_op jit(solution)/shard_map/jit(cholesky)/cholesky | solution.py:160
  195.8 11.8 %cholesky.217 = f32[128,128]{1,0:T(8,128)S(1)} custom-call(f32[128,128]{1,0:T(8,128)S(1)} %cholesky.270), custom_call_target="Cholesky" | custom-call | tf_op jit(solution)/shard_map/jit(cholesky)/cholesky | solution.py:160
  207.7 9.8 %custom-call.28 = f32[1,128,128]{1,2,0:T(8,128)S(1)} custom-call(f32[1,128,128]{2,1,0:T(8,128)S(1)} %get-tuple-element.18), custom_call_target="InvertDiagBlocksLowerTriangular" | custom-call | tf_op jit(solution)/shard_map/jit(cholesky)/cholesky | solution.py:160
  218.2 11.7 %cholesky.238 = f32[128,128]{1,0:T(8,128)S(1)} custom-call(f32[128,128]{1,0:T(8,128)S(1)} %cholesky.275), custom_call_target="Cholesky" | custom-call | tf_op jit(solution)/shard_map/jit(cholesky)/cholesky | solution.py:160
  230.6 9.8 %custom-call.29 = f32[1,128,128]{1,2,0:T(8,128)S(1)} custom-call(f32[1,128,128]{2,1,0:T(8,128)S(1)} %get-tuple-element.15), custom_call_target="InvertDiagBlocksLowerTriangular" | custom-call | tf_op jit(solution)/shard_map/jit(cholesky)/cholesky | solution.py:160
  241.0 11.7 %cholesky.255 = f32[128,128]{1,0:T(8,128)S(1)} custom-call(f32[128,128]{1,0:T(8,128)S(1)} %convolution_subtract_fusion.2), custom_call_target="Cholesky" | custom-call | tf_op jit(solution)/shard_map/jit(cholesky)/cholesky | solution.py:160
  (52 shorter events, 18.9 us)
Async XLA Ops:
  0.6 1.5 collective-permute-start
  2.8 4.3 %collective-permute-start.1 = (s32[256]{0:T(256)S(1)}, s32[256]{0:T(256)S(1)}, u32[]{:S(2)}, u32[]{:S(2)}) collective-permute-start(s32[256]{0:T(256)S(1)} %add_select_fusion.3), channel_id=1, source_target_pairs={{0,4},{2,6},{4,0},{6,2},{8,12},{10,14},{12,8},{14,10},{16,20},{18,... | collective-permute-start | bytes 3080 | tf_op jit(solution)/shard_map/ppermute | solution.py:16
  7.2 3.7 %collective-permute-start.2 = (s32[512]{0:T(512)S(1)}, s32[512]{0:T(512)S(1)}, u32[]{:S(2)}, u32[]{:S(2)}) collective-permute-start(s32[512]{0:T(512)S(1)} %add_select_fusion.2), channel_id=1, source_target_pairs={{0,8},{2,10},{4,12},{6,14},{8,0},{10,2},{12,4},{14,6},{16,24},{18,... | collective-permute-start | bytes 6152 | tf_op jit(solution)/shard_map/ppermute | solution.py:16
  10.9 4.6 %collective-permute-start.3 = (s32[1024]{0:T(1024)S(1)}, s32[1024]{0:T(1024)S(1)}, u32[]{:S(2)}, u32[]{:S(2)}) collective-permute-start(s32[1024]{0:T(1024)S(1)} %add_select_fusion.1), channel_id=1, source_target_pairs={{0,16},{2,18},{4,20},{6,22},{8,24},{10,26},{12,28},{14,30},{16,0},... | collective-permute-start | bytes 12296 | tf_op jit(solution)/shard_map/ppermute | solution.py:16
  15.5 0.8 copy-start
  16.2 0.7 copy-start.1
  33.3 2.7 %collective-permute-start.4 = (f32[1024,256]{1,0:T(8,128)S(1)}, f32[1024,256]{1,0:T(8,128)S(1)}, u32[]{:S(2)}, u32[]{:S(2)}) collective-permute-start(f32[1024,256]{1,0:T(8,128)S(1)} %get-tuple-element.5), channel_id=1, source_target_pairs={{0,2},{2,0},{4,6},{6,4},{8,10},{10,8},{12,14},{14,12},{16,18},{18,... | collective-permute-start | bytes 3145736 | tf_op jit(solution)/shard_map/ppermute | solution.py:16
  36.3 14.1 %collective-permute-start.5 = (f32[512,256]{1,0:T(8,128)S(1)}, f32[512,256]{1,0:T(8,128)S(1)}, u32[]{:S(2)}, u32[]{:S(2)}) collective-permute-start(f32[512,256]{1,0:T(8,128)S(1)} %bitcast.51), channel_id=1, source_target_pairs={{0,4},{2,6},{4,0},{6,2},{8,12},{10,14},{12,8},{14,10},{16,20},{18,... | collective-permute-start | bytes 1572872 | tf_op jit(solution)/shard_map/ppermute | solution.py:16
  50.5 7.7 %collective-permute-start.6 = (f32[256,256]{1,0:T(8,128)S(1)}, f32[256,256]{1,0:T(8,128)S(1)}, u32[]{:S(2)}, u32[]{:S(2)}) collective-permute-start(f32[256,256]{1,0:T(8,128)S(1)} %bitcast.53), channel_id=1, source_target_pairs={{0,8},{2,10},{4,12},{6,14},{8,0},{10,2},{12,4},{14,6},{16,24},{18,... | collective-permute-start | bytes 786440 | tf_op jit(solution)/shard_map/ppermute | solution.py:16
  58.2 7.7 %collective-permute-start.7 = (f32[128,256]{1,0:T(8,128)S(1)}, f32[128,256]{1,0:T(8,128)S(1)}, u32[]{:S(2)}, u32[]{:S(2)}) collective-permute-start(f32[128,256]{1,0:T(8,128)S(1)} %slice_bitcast_fusion.1), channel_id=1, source_target_pairs={{0,16},{2,18},{4,20},{6,22},{8,24},{10,26},{12,28},{14,30},{16,0},... | collective-permute-start | bytes 393224 | tf_op jit(solution)/shard_map/ppermute | solution.py:16
  65.9 107.5 %copy-start.2 = (f32[128,256]{1,0:T(8,128)}, f32[128,256]{1,0:T(8,128)S(1)}, u32[]{:S(2)}) copy-start(f32[128,256]{1,0:T(8,128)S(1)} %fusion.10) | copy-start | bytes 393220
  72.6 2.7 %collective-permute-start.8 = (f32[512,512]{0,1:T(8,128)S(1)}, f32[512,512]{0,1:T(8,128)S(1)}, u32[]{:S(2)}, u32[]{:S(2)}) collective-permute-start(f32[512,512]{0,1:T(8,128)S(1)} %fusion.17), channel_id=1, source_target_pairs={{0,2},{2,0},{4,6},{6,4},{8,10},{10,8},{12,14},{14,12},{16,18},{18,... | collective-permute-start | bytes 3145736 | tf_op jit(solution)/shard_map/ppermute | solution.py:16
  75.6 25.3 %collective-permute-start.9 = (f32[512,512]{0,1:T(8,128)S(1)}, f32[512,512]{0,1:T(8,128)S(1)}, u32[]{:S(2)}, u32[]{:S(2)}) collective-permute-start(f32[512,512]{0,1:T(8,128)S(1)} %add.78), channel_id=1, source_target_pairs={{0,4},{2,6},{4,0},{6,2},{8,12},{10,14},{12,8},{14,10},{16,20},{18,... | collective-permute-start | bytes 3145736 | tf_op jit(solution)/shard_map/ppermute | solution.py:16
  101.0 24.4 %collective-permute-start.10 = (f32[512,512]{0,1:T(8,128)S(1)}, f32[512,512]{0,1:T(8,128)S(1)}, u32[]{:S(2)}, u32[]{:S(2)}) collective-permute-start(f32[512,512]{0,1:T(8,128)S(1)} %add.79), channel_id=1, source_target_pairs={{0,8},{2,10},{4,12},{6,14},{8,0},{10,2},{12,4},{14,6},{16,24},{18,... | collective-permute-start | bytes 3145736 | tf_op jit(solution)/shard_map/ppermute | solution.py:16
  125.7 46.9 %collective-permute-start.11 = (f32[512,512]{0,1:T(8,128)S(1)}, f32[512,512]{0,1:T(8,128)S(1)}, u32[]{:S(2)}, u32[]{:S(2)}) collective-permute-start(f32[512,512]{0,1:T(8,128)S(1)} %add.80), channel_id=1, source_target_pairs={{0,16},{2,18},{4,20},{6,22},{8,24},{10,26},{12,28},{14,30},{16,0},... | collective-permute-start | bytes 3145736 | tf_op jit(solution)/shard_map/ppermute | solution.py:16

commit v2 on v1

--- a/solution.py
+++ b/solution.py
@@ -10,6 +10,7 @@
 
 TILE = 256
 LANES = 128
+SUB = 8
 
 
 def swapped(value, axis, bit):
@@ -39,7 +40,7 @@
     return high, low
 
 
-def mix_kernel(mask_ref, pick_ref, slab_ref, sign_ref, send_ref, keep_ref, had_ref, mixed_ref,
+def mix_kernel(mask_ref, pick_ref, slab_ref, sign_ref, keep_ref, send_ref, had_ref, mixed_ref,
                *, inner, outer, pick_count, groups, norm_scale):
     step = pl.program_id(0)
     width = slab_ref.shape[1]
@@ -130,6 +131,132 @@
     )(block_mask, picks, slab, sign_bits.reshape(row_count // LANES, LANES))
 
 
+def gram_kernel(full_ref, keep_ref, send_ref, gram_ref, *, strips, scale):
+    total = full_ref.shape[1]
+    height = LANES // strips
+    mine = lax.axis_index("rows") & (strips - 1)
+    block = 0
+    for upper in range(total // LANES):
+        left = full_ref[:, upper * LANES:(upper + 1) * LANES]
+        rows = lax.dot_general(left, full_ref[:, upper * LANES:], (((0,), (0,)), ((), ())),
+                               precision=lax.Precision.HIGHEST, preferred_element_type=jnp.float32)
+        gram_ref[:, :total - upper * LANES] = rows * scale
+        for right in range(upper, total // LANES):
+            at = (right - upper) * LANES
+            for low_bit, out_ref in ((0, keep_ref), (1, send_ref)):
+                for half in range(strips // 2):
+                    strip = pl.multiple_of(((low_bit + 2 * half) ^ mine) * height, height)
+                    out_ref[half, block * height:(block + 1) * height, :] = gram_ref[
+                        pl.ds(strip, height), at:at + LANES]
+            block += 1
+
+
+def partial_gram(full_rows, strips, scale):
+    total = full_rows.shape[1]
+    tiles = total // LANES
+    half = jax.ShapeDtypeStruct(
+        (strips // 2, tiles * (tiles + 1) // 2 * (LANES // strips), LANES), jnp.float32)
+    return pl.pallas_call(
+        functools.partial(gram_kernel, strips=strips, scale=scale),
+        out_shape=[half, half],
+        scratch_shapes=[pltpu.VMEM((LANES, total), jnp.float32)],
+        compiler_params=pltpu.CompilerParams(vmem_limit_bytes=48 << 20),
+    )(full_rows)
+
+
+def lane_splat(value, lane):
+    return jnp.broadcast_to(value[:, lane:lane + 1], (value.shape[0], LANES))
+
+
+def row_splat(value, row):
+    return jnp.broadcast_to(value[row:row + 1, :], value.shape)
+
+
+def factor_tile(tile):
+    done = []
+    copies = tile[0].shape[1] // LANES
+    sub_row = lax.broadcasted_iota(jnp.int32, tile[0].shape, 0)
+
+    def widen(value):
+        return jnp.concatenate([value] * copies, axis=1)
+
+    for at in range(len(tile)):
+        lead = tile[at]
+        columns = [lane_splat(lead[:, :LANES], SUB * at + j) for j in range(SUB)]
+        pivot = {(i, j): row_splat(columns[j], i) for j in range(SUB) for i in range(j + 1)}
+        below = [[lane_splat(tile[u][:, :LANES], SUB * at + j) for j in range(SUB)]
+                 for u in range(at + 1, len(tile))]
+        rows = [row_splat(lead, m) for m in range(SUB)]
+        panel = jnp.zeros_like(lead)
+        for m in range(SUB):
+            inverse = lax.rsqrt(pivot[m, m])
+            for j in range(m + 1, SUB):
+                pivot[m, j] = pivot[m, j] * inverse
+            for i in range(m + 1, SUB):
+                for j in range(i, SUB):
+                    pivot[i, j] = pivot[i, j] - pivot[m, i] * pivot[m, j]
+            rows[m] = rows[m] * widen(inverse)
+            for j in range(m + 1, SUB):
+                rows[j] = rows[j] - widen(pivot[m, j]) * rows[m]
+            panel = jnp.where(sub_row == m, rows[m], panel)
+            for u, column in enumerate(below):
+                column[m] = column[m] * inverse
+                for j in range(m + 1, SUB):
+                    column[j] = column[j] - pivot[m, j] * column[m]
+                tile[at + 1 + u] = tile[at + 1 + u] - widen(column[m]) * rows[m]
+        done.append(panel)
+    return done
+
+
+def factor_kernel(even_ref, odd_ref, out_ref, gram_ref, factor_ref, *, strips):
+    total = gram_ref.shape[0]
+    tiles = total // LANES
+    height = LANES // strips
+    mine = lax.axis_index("rows") & (strips - 1)
+    block = 0
+    for upper in range(tiles):
+        for right in range(upper, tiles):
+            for low_bit, in_ref in ((0, even_ref), (1, odd_ref)):
+                for half in range(strips // 2):
+                    strip = pl.multiple_of(((low_bit + 2 * half) ^ mine) * height, height)
+                    gram_ref[pl.ds(upper * LANES + strip, height), right * LANES:(right + 1) * LANES] = in_ref[
+                        half, block * height:(block + 1) * height, :]
+            block += 1
+    factor_ref[...] = jnp.zeros_like(factor_ref)
+    row = lax.broadcasted_iota(jnp.int32, (LANES, LANES), 0)
+    col = lax.broadcasted_iota(jnp.int32, (LANES, LANES), 1)
+    identity = (row == col).astype(jnp.float32)
+    for at in range(tiles):
+        here = slice(at * LANES, (at + 1) * LANES)
+        diagonal = jnp.concatenate([gram_ref[here, here], identity], axis=1)
+        slabs = [diagonal[SUB * t:SUB * t + SUB] for t in range(LANES // SUB)]
+        factored = jnp.concatenate(factor_tile(slabs), axis=0)
+        factor_ref[here, here] = jnp.where(col >= row, factored[:, :LANES], 0.0)
+        if at < tiles - 1:
+            rest = (at + 1) * LANES
+            panel = jnp.dot(factored[:, LANES:], gram_ref[here, rest:], precision=lax.Precision.HIGHEST,
+                            preferred_element_type=jnp.float32)
+            factor_ref[here, rest:] = panel
+            for below in range(at + 1, tiles):
+                skip = (below - at - 1) * LANES
+                gram_ref[below * LANES:(below + 1) * LANES, below * LANES:] -= lax.dot_general(
+                    panel[:, skip:skip + LANES], panel[:, skip:], (((0,), (0,)), ((), ())),
+                    precision=lax.Precision.HIGHEST, preferred_element_type=jnp.float32)
+    width = out_ref.shape[1]
+    first = pl.multiple_of(lax.axis_index("cols") * width, width)
+    out_ref[...] = factor_ref[:, pl.ds(first, width)]
+
+
+def factor_panel(even, odd, total, width):
+    strips = 2 * even.shape[0]
+    return pl.pallas_call(
+        functools.partial(factor_kernel, strips=strips),
+        out_shape=jax.ShapeDtypeStruct((total, width), jnp.float32),
+        scratch_shapes=[pltpu.VMEM((total, total), jnp.float32)] * 2,
+        compiler_params=pltpu.CompilerParams(vmem_limit_bytes=48 << 20),
+    )(even, odd)
+
+
 def gather_rows(value, groups):
     device = lax.axis_index("rows")
     for bit in range(groups.bit_length() - 1):
@@ -145,21 +272,20 @@
     bits = groups.bit_length() - 1
     pick_count = sample_rows.shape[0]
     picks = gather_rows(sample_rows, groups)
-    send, keep = mix_and_pick(slab, sign_bits, block_mask, picks, groups)
+    keep, send = mix_and_pick(slab, sign_bits, block_mask, picks, groups)
     sketch = keep + swapped(send, "rows", 0)
     for bit in range(1, bits):
         parts = sketch.reshape(-1, 2, pick_count, panel_width)
         sketch = (parts[:, 0] + swapped(parts[:, 1].reshape(-1, panel_width), "rows", bit).reshape(parts[:, 0].shape))
         sketch = sketch.reshape(-1, panel_width)
     full_rows = lax.all_gather(sketch, "cols", axis=1, tiled=True)
-    panel_index = lax.axis_index("cols")
-    gram_matrix = jnp.einsum("sa,sb->ab", full_rows, full_rows, precision=lax.Precision.HIGHEST)
-    for bit in range(bits):
-        gram_matrix = gram_matrix + swapped(gram_matrix, "rows", bit)
-    gram_matrix = gram_matrix / (pick_count * groups)
-    lower_factor = jnp.linalg.cholesky(gram_matrix)
-    upper_factor = lower_factor.T
-    r_panel = lax.dynamic_slice_in_dim(upper_factor, panel_index * panel_width, panel_width, 1)
+    keep, send = partial_gram(full_rows, 4, 1.0 / (pick_count * groups))
+    gram = keep + swapped(send, "rows", 0)
+    gram = gram[:1] + swapped(gram[1:], "rows", 1)
+    for bit in range(2, bits):
+        gram = gram + swapped(gram, "rows", bit)
+    gram = jnp.concatenate([gram, swapped(gram, "rows", 1)])
+    r_panel = factor_panel(gram, swapped(gram, "rows", 0), full_rows.shape[1], panel_width)
     return (sketch, r_panel)
 
 

time: 258 us -> 121 us (0.47)
  other arithmetic: 80.7 us -> 1.14 us
  waiting for transfers between devices: 126 us -> 54.1 us
  Pallas kernels: 16.4 us -> 36.2 us
  matrix products: 2.9 us -> 0 us
  between operations: 3.4 us -> 0.75 us
    another operation x14 -> x0, other arithmetic: 78.6 us -> none  [body(): lower_factor = jnp.linalg.cholesky(gram_matrix)]
    ppermute x12 -> x14, waiting for transfers between devices: 126 us -> 54.1 us  [swapped(): lax.ppermute(value, axis, [(i, i ^ 1 << bit) for i in range(lax.axis_size...]
    pallas_call x0 -> x2, Pallas kernels: none -> 19.8 us  [the longest x1 19 us: factor_panel(): pl.pallas_call(functools.partial(factor_kernel, strips=strips), out_shape...]
    ppermute x12 -> x14, starting transfers between devices: 20 us -> 21.7 us  [swapped(): lax.ppermute(value, axis, [(i, i ^ 1 << bit) for i in range(lax.axis_size...]
  transfers between devices with their start and end apart: 12 -> 14, of which waited for: 12 -> 14; matrix products, arithmetic and copies ran while one was open for 0% -> 0% of each run, Pallas kernels for 0% -> 0%
where the time goes in v2:
time: 121 us
  waiting for transfers between devices  54.1 us (45%)
  Pallas kernels  36.2 us (30%)
  starting transfers between devices  21.7 us (18%)
  blocking collectives  5.64 us (5%)
  local copies, waits for them, and re-layouts  1.56 us (1%)
    ppermute x14, waiting for transfers between devices, swapped(): lax.ppermute(value, axis, [(i, i ^ 1 << bit) for i in range(lax.axis_size...  54.1 us
    ppermute x14, starting transfers between devices, swapped(): lax.ppermute(value, axis, [(i, i ^ 1 << bit) for i in range(lax.axis_size...  21.7 us
    pallas_call x1, Pallas kernels, factor_panel(): pl.pallas_call(functools.partial(factor_kernel, strips=strips), out_shape...  19 us
    pallas_call x1, Pallas kernels, mix_and_pick(): pl.pallas_call(functools.partial(mix_kernel, inner=inner, outer=outer, pi...  16.4 us
    all_gather x1, blocking collectives, body(): full_rows = lax.all_gather(sketch, 'cols', axis=1, tiled=True)  5.64 us
  transfers between devices with their start and end apart: 14, of which 14 were waited for; matrix products, arithmetic and copies ran while one was open for 0% of the time, Pallas kernels for 0%

profile of v2, /device:TPU:0, one launch (start us, length us, event | category | flops | bytes accessed | tf_op | source)
XLA Modules:
  0.0 121.1 jit_solution(13796447295997825543)
XLA Ops:
  2.8 2.8 %collective-permute-start.1 = (s32[256]{0:T(256)S(1)}, s32[256]{0:T(256)S(1)}, u32[]{:S(2)}, u32[]{:S(2)}) collective-permute-start(s32[256]{0:T(256)S(1)} %add_select_fusion.3), channel_id=1, source_target_pairs={{0,4},{2,6},{4,0},{6,2},{8,12},{10,14},{12,8},{14,10},{16,20},{18,... | collective-permute-start | bytes 3080 | tf_op jit(solution)/shard_map/ppermute | solution.py:17
  7.2 2.1 %collective-permute-start.2 = (s32[512]{0:T(512)S(1)}, s32[512]{0:T(512)S(1)}, u32[]{:S(2)}, u32[]{:S(2)}) collective-permute-start(s32[512]{0:T(512)S(1)} %add_select_fusion.2), channel_id=1, source_target_pairs={{0,8},{2,10},{4,12},{6,14},{8,0},{10,2},{12,4},{14,6},{16,24},{18,... | collective-permute-start | bytes 6152 | tf_op jit(solution)/shard_map/ppermute | solution.py:17
  9.3 1.6 %collective-permute-done.2 = s32[512]{0:T(512)S(1)} collective-permute-done((s32[512]{0:T(512)S(1)}, s32[512]{0:T(512)S(1)}, u32[]{:S(2)}, u32[]{:S(2)}) %collective-permute-start.2) | collective-permute-done | bytes 2080 | tf_op jit(solution)/shard_map/ppermute | solution.py:17
  10.9 3.0 %collective-permute-start.3 = (s32[1024]{0:T(1024)S(1)}, s32[1024]{0:T(1024)S(1)}, u32[]{:S(2)}, u32[]{:S(2)}) collective-permute-start(s32[1024]{0:T(1024)S(1)} %add_select_fusion.1), channel_id=1, source_target_pairs={{0,16},{2,18},{4,20},{6,22},{8,24},{10,26},{12,28},{14,30},{16,0},... | collective-permute-start | bytes 12296 | tf_op jit(solution)/shard_map/ppermute | solution.py:17
  13.9 1.6 %collective-permute-done.3 = s32[1024]{0:T(1024)S(1)} collective-permute-done((s32[1024]{0:T(1024)S(1)}, s32[1024]{0:T(1024)S(1)}, u32[]{:S(2)}, u32[]{:S(2)}) %collective-permute-start.3) | collective-permute-done | bytes 4128 | tf_op jit(solution)/shard_map/ppermute | solution.py:17
  16.9 16.4 %shard_map.59 = (f32[1024,256]{1,0:T(8,128)S(1)}, f32[1024,256]{1,0:T(8,128)S(1)}) custom-call(s32[64]{0:T(128)S(1)} %copy-done.1, s32[2048]{0:T(1024)S(1)} %add_select_fusion.pick_ref, f32[8192,256]{1,0:T(8,128)} %slab_ref.1, s32[64,128]{1,0:T(8,128)S(1)} %bitcast.23), custom_call_target="tpu_custom_call" | custom-call | tf_op jit(solution)/shard_map/pallas_call | solution.py:113
  33.4 2.6 %collective-permute-done.4 = f32[1024,256]{1,0:T(8,128)S(1)} collective-permute-done((f32[1024,256]{1,0:T(8,128)S(1)}, f32[1024,256]{1,0:T(8,128)S(1)}, u32[]{:S(2)}, u32[]{:S(2)}) %collective-permute-start.4) | collective-permute-done | bytes 1048608 | tf_op jit(solution)/shard_map/ppermute | solution.py:17
  36.3 1.9 %collective-permute-start.5 = (f32[512,256]{1,0:T(8,128)S(1)}, f32[512,256]{1,0:T(8,128)S(1)}, u32[]{:S(2)}, u32[]{:S(2)}) collective-permute-start(f32[512,256]{1,0:T(8,128)S(1)} %bitcast.27), channel_id=1, source_target_pairs={{0,4},{2,6},{4,0},{6,2},{8,12},{10,14},{12,8},{14,10},{16,20},{18,... | collective-permute-start | bytes 1572872 | tf_op jit(solution)/shard_map/ppermute | solution.py:17
  38.2 12.2 %collective-permute-done.5 = f32[512,256]{1,0:T(8,128)S(1)} collective-permute-done((f32[512,256]{1,0:T(8,128)S(1)}, f32[512,256]{1,0:T(8,128)S(1)}, u32[]{:S(2)}, u32[]{:S(2)}) %collective-permute-start.5) | collective-permute-done | bytes 524320 | tf_op jit(solution)/shard_map/ppermute | solution.py:17
  50.5 1.9 %collective-permute-start.6 = (f32[256,256]{1,0:T(8,128)S(1)}, f32[256,256]{1,0:T(8,128)S(1)}, u32[]{:S(2)}, u32[]{:S(2)}) collective-permute-start(f32[256,256]{1,0:T(8,128)S(1)} %bitcast.29), channel_id=1, source_target_pairs={{0,8},{2,10},{4,12},{6,14},{8,0},{10,2},{12,4},{14,6},{16,24},{18,... | collective-permute-start | bytes 786440 | tf_op jit(solution)/shard_map/ppermute | solution.py:17
  52.4 5.8 %collective-permute-done.6 = f32[256,256]{1,0:T(8,128)S(1)} collective-permute-done((f32[256,256]{1,0:T(8,128)S(1)}, f32[256,256]{1,0:T(8,128)S(1)}, u32[]{:S(2)}, u32[]{:S(2)}) %collective-permute-start.6) | collective-permute-done | bytes 262176 | tf_op jit(solution)/shard_map/ppermute | solution.py:17
  58.2 2.8 %collective-permute-start.7 = (f32[128,256]{1,0:T(8,128)S(1)}, f32[128,256]{1,0:T(8,128)S(1)}, u32[]{:S(2)}, u32[]{:S(2)}) collective-permute-start(f32[128,256]{1,0:T(8,128)S(1)} %slice_bitcast_fusion.1), channel_id=1, source_target_pairs={{0,16},{2,18},{4,20},{6,22},{8,24},{10,26},{12,28},{14,30},{16,0},... | collective-permute-start | bytes 393224 | tf_op jit(solution)/shard_map/ppermute | solution.py:17
  61.1 4.9 %collective-permute-done.7 = f32[128,256]{1,0:T(8,128)S(1)} collective-permute-done((f32[128,256]{1,0:T(8,128)S(1)}, f32[128,256]{1,0:T(8,128)S(1)}, u32[]{:S(2)}, u32[]{:S(2)}) %collective-permute-start.7) | collective-permute-done | bytes 131104 | tf_op jit(solution)/shard_map/ppermute | solution.py:17
  66.0 5.6 %all_gather.3.full_ref = f32[128,512]{1,0:T(8,128)S(1)} all-gather(f32[128,256]{1,0:T(8,128)S(1)} %fusion.1), channel_id=1, replica_groups=mesh['rows'=16,'cols'=2] {'cols'}, dimensions={1}, use_global_device_ids=true | all-gather | bytes 393216 | tf_op jit(solution)/shard_map/all_gather | solution.py:281
  72.5 1.6 %collective-permute-done.8 = f32[2,320,128]{2,1,0:T(8,128)S(1)} collective-permute-done((f32[2,320,128]{2,1,0:T(8,128)S(1)}, f32[2,320,128]{2,1,0:T(8,128)S(1)}, u32[]{:S(2)}, u32[]{:S(2)}) %collective-permute-start.8) | collective-permute-done | bytes 327712 | tf_op jit(solution)/shard_map/ppermute | solution.py:17
  74.1 1.6 %collective-permute-start.9 = (f32[1,320,128]{2,1,0:T(8,128)S(1)}, f32[1,320,128]{2,1,0:T(8,128)S(1)}, u32[]{:S(2)}, u32[]{:S(2)}) collective-permute-start(f32[1,320,128]{2,1,0:T(8,128)S(1)} %slice.39), channel_id=1, source_target_pairs={{0,4},{2,6},{4,0},{6,2},{8,12},{10,14},{12,8},{14,10},{16,20},{18,... | collective-permute-start | bytes 491528 | tf_op jit(solution)/shard_map/ppermute | solution.py:17
  75.8 4.7 %collective-permute-done.9 = f32[1,320,128]{2,1,0:T(8,128)S(1)} collective-permute-done((f32[1,320,128]{2,1,0:T(8,128)S(1)}, f32[1,320,128]{2,1,0:T(8,128)S(1)}, u32[]{:S(2)}, u32[]{:S(2)}) %collective-permute-start.9) | collective-permute-done | bytes 163872 | tf_op jit(solution)/shard_map/ppermute | solution.py:17
  81.3 4.7 %collective-permute-done.10 = f32[1,320,128]{2,1,0:T(8,128)S(1)} collective-permute-done((f32[1,320,128]{2,1,0:T(8,128)S(1)}, f32[1,320,128]{2,1,0:T(8,128)S(1)}, u32[]{:S(2)}, u32[]{:S(2)}) %collective-permute-start.10) | collective-permute-done | bytes 163872 | tf_op jit(solution)/shard_map/ppermute | solution.py:17
  86.0 2.4 %collective-permute-start.11 = (f32[1,320,128]{2,1,0:T(8,128)S(1)}, f32[1,320,128]{2,1,0:T(8,128)S(1)}, u32[]{:S(2)}, u32[]{:S(2)}) collective-permute-start(f32[1,320,128]{2,1,0:T(8,128)S(1)} %add.39), channel_id=1, source_target_pairs={{0,16},{2,18},{4,20},{6,22},{8,24},{10,26},{12,28},{14,30},{16,0},... | collective-permute-start | bytes 491528 | tf_op jit(solution)/shard_map/ppermute | solution.py:17
  88.4 6.6 %collective-permute-done.11 = f32[1,320,128]{2,1,0:T(8,128)S(1)} collective-permute-done((f32[1,320,128]{2,1,0:T(8,128)S(1)}, f32[1,320,128]{2,1,0:T(8,128)S(1)}, u32[]{:S(2)}, u32[]{:S(2)}) %collective-permute-start.11) | collective-permute-done | bytes 163872 | tf_op jit(solution)/shard_map/ppermute | solution.py:17
  95.0 1.6 %collective-permute-start.12 = (f32[1,320,128]{2,1,0:T(8,128)S(1)}, f32[1,320,128]{2,1,0:T(8,128)S(1)}, u32[]{:S(2)}, u32[]{:S(2)}) collective-permute-start(f32[1,320,128]{2,1,0:T(8,128)S(1)} %add.40), channel_id=1, source_target_pairs={{0,4},{2,6},{4,0},{6,2},{8,12},{10,14},{12,8},{14,10},{16,20},{18,... | collective-permute-start | bytes 491528 | tf_op jit(solution)/shard_map/ppermute | solution.py:17
  96.6 3.8 %collective-permute-done.12 = f32[1,320,128]{2,1,0:T(8,128)S(1)} collective-permute-done((f32[1,320,128]{2,1,0:T(8,128)S(1)}, f32[1,320,128]{2,1,0:T(8,128)S(1)}, u32[]{:S(2)}, u32[]{:S(2)}) %collective-permute-start.12) | collective-permute-done | bytes 163872 | tf_op jit(solution)/shard_map/ppermute | solution.py:17
  100.5 1.6 %collective-permute-done.13.odd_ref = f32[2,320,128]{2,1,0:T(8,128)S(1)} collective-permute-done((f32[2,320,128]{2,1,0:T(8,128)S(1)}, f32[2,320,128]{2,1,0:T(8,128)S(1)}, u32[]{:S(2)}, u32[]{:S(2)}) %collective-permute-start.13) | collective-permute-done | bytes 327712 | tf_op jit(solution)/shard_map/ppermute | solution.py:17
  102.1 19.0 %shard_map.61 = f32[512,256]{1,0:T(8,128)} custom-call(f32[2,320,128]{2,1,0:T(8,128)S(1)} %pad_maximum_fusion.even_ref, f32[2,320,128]{2,1,0:T(8,128)S(1)} %collective-permute-done.13.odd_ref), custom_call_target="tpu_custom_call" | custom-call | tf_op jit(solution)/shard_map/pallas_call | solution.py:252
  (31 shorter events, 7.5 us)
Async XLA Ops:
  0.6 1.5 %collective-permute-start = (s32[128]{0:T(128)}, s32[128]{0:T(128)S(1)}, u32[]{:S(2)}, u32[]{:S(2)}) collective-permute-start(s32[128]{0:T(128)} %param.7), channel_id=1, source_target_pairs={{0,2},{2,0},{4,6},{6,4},{8,10},{10,8},{12,14},{14,12},{16,18},{18,... | collective-permute-start | bytes 1544 | tf_op jit(solution)/shard_map/ppermute | solution.py:17
  2.8 4.3 %collective-permute-start.1 = (s32[256]{0:T(256)S(1)}, s32[256]{0:T(256)S(1)}, u32[]{:S(2)}, u32[]{:S(2)}) collective-permute-start(s32[256]{0:T(256)S(1)} %add_select_fusion.3), channel_id=1, source_target_pairs={{0,4},{2,6},{4,0},{6,2},{8,12},{10,14},{12,8},{14,10},{16,20},{18,... | collective-permute-start | bytes 3080 | tf_op jit(solution)/shard_map/ppermute | solution.py:17
  7.2 3.7 %collective-permute-start.2 = (s32[512]{0:T(512)S(1)}, s32[512]{0:T(512)S(1)}, u32[]{:S(2)}, u32[]{:S(2)}) collective-permute-start(s32[512]{0:T(512)S(1)} %add_select_fusion.2), channel_id=1, source_target_pairs={{0,8},{2,10},{4,12},{6,14},{8,0},{10,2},{12,4},{14,6},{16,24},{18,... | collective-permute-start | bytes 6152 | tf_op jit(solution)/shard_map/ppermute | solution.py:17
  10.9 4.6 %collective-permute-start.3 = (s32[1024]{0:T(1024)S(1)}, s32[1024]{0:T(1024)S(1)}, u32[]{:S(2)}, u32[]{:S(2)}) collective-permute-start(s32[1024]{0:T(1024)S(1)} %add_select_fusion.1), channel_id=1, source_target_pairs={{0,16},{2,18},{4,20},{6,22},{8,24},{10,26},{12,28},{14,30},{16,0},... | collective-permute-start | bytes 12296 | tf_op jit(solution)/shard_map/ppermute | solution.py:17
  15.5 0.8 copy-start
  16.2 0.7 copy-start.1
  33.3 2.7 %collective-permute-start.4 = (f32[1024,256]{1,0:T(8,128)S(1)}, f32[1024,256]{1,0:T(8,128)S(1)}, u32[]{:S(2)}, u32[]{:S(2)}) collective-permute-start(f32[1024,256]{1,0:T(8,128)S(1)} %get-tuple-element.7), channel_id=1, source_target_pairs={{0,2},{2,0},{4,6},{6,4},{8,10},{10,8},{12,14},{14,12},{16,18},{18,... | collective-permute-start | bytes 3145736 | tf_op jit(solution)/shard_map/ppermute | solution.py:17
  36.3 14.1 %collective-permute-start.5 = (f32[512,256]{1,0:T(8,128)S(1)}, f32[512,256]{1,0:T(8,128)S(1)}, u32[]{:S(2)}, u32[]{:S(2)}) collective-permute-start(f32[512,256]{1,0:T(8,128)S(1)} %bitcast.27), channel_id=1, source_target_pairs={{0,4},{2,6},{4,0},{6,2},{8,12},{10,14},{12,8},{14,10},{16,20},{18,... | collective-permute-start | bytes 1572872 | tf_op jit(solution)/shard_map/ppermute | solution.py:17
  50.5 7.7 %collective-permute-start.6 = (f32[256,256]{1,0:T(8,128)S(1)}, f32[256,256]{1,0:T(8,128)S(1)}, u32[]{:S(2)}, u32[]{:S(2)}) collective-permute-start(f32[256,256]{1,0:T(8,128)S(1)} %bitcast.29), channel_id=1, source_target_pairs={{0,8},{2,10},{4,12},{6,14},{8,0},{10,2},{12,4},{14,6},{16,24},{18,... | collective-permute-start | bytes 786440 | tf_op jit(solution)/shard_map/ppermute | solution.py:17
  58.2 7.7 %collective-permute-start.7 = (f32[128,256]{1,0:T(8,128)S(1)}, f32[128,256]{1,0:T(8,128)S(1)}, u32[]{:S(2)}, u32[]{:S(2)}) collective-permute-start(f32[128,256]{1,0:T(8,128)S(1)} %slice_bitcast_fusion.1), channel_id=1, source_target_pairs={{0,16},{2,18},{4,20},{6,22},{8,24},{10,26},{12,28},{14,30},{16,0},... | collective-permute-start | bytes 393224 | tf_op jit(solution)/shard_map/ppermute | solution.py:17
  65.9 55.2 %copy-start.2 = (f32[128,256]{1,0:T(8,128)}, f32[128,256]{1,0:T(8,128)S(1)}, u32[]{:S(2)}) copy-start(f32[128,256]{1,0:T(8,128)S(1)} %fusion.1) | copy-start | bytes 393220
  72.4 1.7 %collective-permute-start.8 = (f32[2,320,128]{2,1,0:T(8,128)S(1)}, f32[2,320,128]{2,1,0:T(8,128)S(1)}, u32[]{:S(2)}, u32[]{:S(2)}) collective-permute-start(f32[2,320,128]{2,1,0:T(8,128)S(1)} %get-tuple-element.9), channel_id=1, source_target_pairs={{0,2},{2,0},{4,6},{6,4},{8,10},{10,8},{12,14},{14,12},{16,18},{18,... | collective-permute-start | bytes 983048 | tf_op jit(solution)/shard_map/ppermute | solution.py:17
  74.1 6.3 %collective-permute-start.9 = (f32[1,320,128]{2,1,0:T(8,128)S(1)}, f32[1,320,128]{2,1,0:T(8,128)S(1)}, u32[]{:S(2)}, u32[]{:S(2)}) collective-permute-start(f32[1,320,128]{2,1,0:T(8,128)S(1)} %slice.39), channel_id=1, source_target_pairs={{0,4},{2,6},{4,0},{6,2},{8,12},{10,14},{12,8},{14,10},{16,20},{18,... | collective-permute-start | bytes 491528 | tf_op jit(solution)/shard_map/ppermute | solution.py:17
  80.5 5.5 %collective-permute-start.10 = (f32[1,320,128]{2,1,0:T(8,128)S(1)}, f32[1,320,128]{2,1,0:T(8,128)S(1)}, u32[]{:S(2)}, u32[]{:S(2)}) collective-permute-start(f32[1,320,128]{2,1,0:T(8,128)S(1)} %slice_add_fusion), channel_id=1, source_target_pairs={{0,8},{2,10},{4,12},{6,14},{8,0},{10,2},{12,4},{14,6},{16,24},{18,... | collective-permute-start | bytes 491528 | tf_op jit(solution)/shard_map/ppermute | solution.py:17
  86.0 9.0 %collective-permute-start.11 = (f32[1,320,128]{2,1,0:T(8,128)S(1)}, f32[1,320,128]{2,1,0:T(8,128)S(1)}, u32[]{:S(2)}, u32[]{:S(2)}) collective-permute-start(f32[1,320,128]{2,1,0:T(8,128)S(1)} %add.39), channel_id=1, source_target_pairs={{0,16},{2,18},{4,20},{6,22},{8,24},{10,26},{12,28},{14,30},{16,0},... | collective-permute-start | bytes 491528 | tf_op jit(solution)/shard_map/ppermute | solution.py:17
  95.0 5.4 %collective-permute-start.12 = (f32[1,320,128]{2,1,0:T(8,128)S(1)}, f32[1,320,128]{2,1,0:T(8,128)S(1)}, u32[]{:S(2)}, u32[]{:S(2)}) collective-permute-start(f32[1,320,128]{2,1,0:T(8,128)S(1)} %add.40), channel_id=1, source_target_pairs={{0,4},{2,6},{4,0},{6,2},{8,12},{10,14},{12,8},{14,10},{16,20},{18,... | collective-permute-start | bytes 491528 | tf_op jit(solution)/shard_map/ppermute | solution.py:17
  100.4 1.7 %collective-permute-start.13 = (f32[2,320,128]{2,1,0:T(8,128)S(1)}, f32[2,320,128]{2,1,0:T(8,128)S(1)}, u32[]{:S(2)}, u32[]{:S(2)}) collective-permute-start(f32[2,320,128]{2,1,0:T(8,128)S(1)} %pad_maximum_fusion.even_ref), channel_id=1, source_target_pairs={{0,2},{2,0},{4,6},{6,4},{8,10},{10,8},{12,14},{14,12},{16,18},{18,... | collective-permute-start | bytes 983048 | tf_op jit(solution)/shard_map/ppermute | solution.py:17

commit v3 on v2

v3 whole, which is shorter than its diff:
```python
import functools
import math

import jax
import jax.numpy as jnp
from jax import lax
from jax.experimental import pallas as pl
from jax.experimental.pallas import tpu as pltpu
from jax.sharding import PartitionSpec as P

TILE = 256
LANES = 128
SUB = 8


def swapped(value, axis, bit):
    return lax.ppermute(value, axis, [(i, i ^ 1 << bit) for i in range(lax.axis_size(axis))])


def parity_sign(common):
    for shift in (16, 8, 4, 2, 1):
        common = common ^ (common >> shift)
    return 1 - 2 * (common & 1)


def butterfly(parts):
    stride = 1
    while stride < len(parts):
        for at in range(len(parts)):
            if at & stride == 0:
                low, high = parts[at], parts[at + stride]
                parts[at], parts[at + stride] = low + high, low - high
        stride *= 2
    return parts


def split_two(value):
    high = value.astype(jnp.bfloat16)
    low = (value - high.astype(jnp.float32)).astype(jnp.bfloat16)
    return high, low


def mix_kernel(slab_ref, sign_ref, mask_ref, *refs, first, earlier):
    joined = refs[:earlier]
    out_ref, had_ref, buf_ref, bits_ref, flags_ref, sems = refs[earlier:]
    rows = buf_ref.shape[0]
    chunks = sems.shape[0] - 2
    span = rows // chunks
    per_tile = TILE // LANES

    def fetch(part):
        return pltpu.make_async_copy(slab_ref.at[pl.ds(first + part * span, span), :],
                                     buf_ref.at[pl.ds(part * span, span), :], sems.at[part])

    bits_copy = pltpu.make_async_copy(sign_ref, bits_ref, sems.at[chunks])
    flags_copy = pltpu.make_async_copy(mask_ref, flags_ref, sems.at[chunks + 1])
    bits_copy.start()
    flags_copy.start()
    for part in range(chunks):
        fetch(part).start()
    row = lax.broadcasted_iota(jnp.int32, (TILE, TILE), 0)
    col = lax.broadcasted_iota(jnp.int32, (TILE, TILE), 1)
    had_ref[...] = parity_sign(row & col).astype(jnp.float32).astype(jnp.bfloat16)
    bits_copy.wait()
    flags_copy.wait()
    base_out = out_ref.shape[0] - rows
    tiles = span // TILE
    for part in range(chunks):
        fetch(part).wait()
        mixed = []
        for block in range(part * tiles, (part + 1) * tiles):
            signed = []
            for half in range(per_tile):
                at = first // LANES + block * per_tile + half
                sign = (2 * bits_ref[at:at + 1, :] - 1) * flags_ref[at]
                sign = sign.astype(jnp.float32).astype(jnp.bfloat16)
                signed.append(had_ref[:, half * LANES:(half + 1) * LANES] * sign)
            left = jnp.concatenate(signed * 2, axis=1)
            right = jnp.concatenate(split_two(buf_ref[block * TILE:(block + 1) * TILE, :]), axis=0)
            mixed.append(jnp.dot(left, right, preferred_element_type=jnp.float32))
        mixed = butterfly(mixed)
        for block in range(tiles):
            at = base_out + (part * tiles + block) * TILE
            out_ref[at:at + TILE, :] = mixed[block]

    @pl.loop(0, span // SUB // 4)
    def _(part):
        for eighth in range(4):
            base = pl.multiple_of(part * 4 * SUB, 4 * SUB) + eighth * SUB
            values = butterfly([out_ref[pl.ds(base_out + base + at * span, SUB), :] for at in range(chunks)])
            for at in range(chunks):
                out_ref[pl.ds(base_out + base + at * span, SUB), :] = values[at]

    if earlier:
        @pl.loop(0, rows // SUB // 8)
        def _(part):
            for eighth in range(8):
                base = pl.multiple_of(part * 8 * SUB, 8 * SUB) + eighth * SUB
                values = [ref[pl.ds(base, SUB), :] for ref in joined]
                values = butterfly(values + [out_ref[pl.ds(base_out + base, SUB), :]])
                for at in range(earlier + 1):
                    out_ref[pl.ds(base + at * rows, SUB), :] = values[at]


def mix_run(slab, sign_bits, block_mask, first, rows, earlier):
    width = slab.shape[1]
    chunks = 4
    flags = block_mask.shape[0]
    held = rows * (len(earlier) + 1)
    return pl.pallas_call(
        functools.partial(mix_kernel, first=first, earlier=len(earlier)),
        in_specs=[pl.BlockSpec(memory_space=pltpu.HBM)] * 3 + [pl.BlockSpec(memory_space=pltpu.VMEM)] * len(earlier),
        out_specs=pl.BlockSpec(memory_space=pltpu.VMEM),
        out_shape=jax.ShapeDtypeStruct((held, width), jnp.float32),
        scratch_shapes=[
            pltpu.VMEM((TILE, TILE), jnp.bfloat16),
            pltpu.VMEM((rows, width), jnp.float32),
            pltpu.VMEM((flags, LANES), jnp.int32),
            pltpu.SMEM((flags,), jnp.int32),
            pltpu.SemaphoreType.DMA((chunks + 2,)),
        ],
        compiler_params=pltpu.CompilerParams(vmem_limit_bytes=(36 if earlier else 50) << 20),
    )(slab, sign_bits, block_mask, *earlier)


def pick_kernel(pick_ref, mixed_ref, keep_ref, send_ref, *, start, count, order, pick_count, groups, norm_scale):
    device = lax.axis_index("rows")
    sub_row = lax.broadcasted_iota(jnp.int32, (SUB, mixed_ref.shape[1]), 0)
    octets = count // SUB
    for out_ref, low_bit in ((send_ref, 1), (keep_ref, 0)):
        @pl.loop(0, groups // 2)
        def _(pair):
            offset = low_bit
            for place, bit in enumerate(reversed(order)):
                offset = offset | ((pair >> place) & 1) << bit
            scale = parity_sign((device ^ offset) & device).astype(jnp.float32) * norm_scale
            for octet in range(octets):
                rows = None
                for sub in range(SUB):
                    index = pick_ref[offset * pick_count + start + octet * SUB + sub]
                    taken = jnp.broadcast_to(mixed_ref[pl.ds(index, 1), :], sub_row.shape)
                    rows = taken if rows is None else jnp.where(sub_row == sub, taken, rows)
                out_at = pl.multiple_of(pair * count + octet * SUB, SUB)
                out_ref[pl.ds(out_at, SUB), :] = rows * scale


def pick_rows(picks, mixed, start, count, order, groups):
    norm_scale = 1.0 / math.sqrt(mixed.shape[0] * groups)
    half = jax.ShapeDtypeStruct((groups // 2 * count, mixed.shape[1]), jnp.float32)
    return pl.pallas_call(
        functools.partial(pick_kernel, start=start, count=count, order=order, pick_count=picks.shape[0] // groups,
                          groups=groups, norm_scale=norm_scale),
        in_specs=[pl.BlockSpec(memory_space=pltpu.SMEM), pl.BlockSpec(memory_space=pltpu.VMEM)],
        out_specs=[pl.BlockSpec(memory_space=pltpu.VMEM)] * 2,
        out_shape=[half, half],
        compiler_params=pltpu.CompilerParams(vmem_limit_bytes=32 << 20),
    )(picks, mixed)


def gram_kernel(*refs, strips, scale, peers):
    pieces, (keep_ref, send_ref, full_ref, gram_ref) = refs[:-4], refs[-4:]
    total = full_ref.shape[1]
    width = total // peers
    column = lax.axis_index("cols")
    at = 0
    for run in range(len(pieces) // peers):
        count = pieces[run * peers].shape[0]
        for peer in range(peers):
            first = pl.multiple_of((column ^ peer) * width, width)
            full_ref[at:at + count, pl.ds(first, width)] = pieces[run * peers + peer][...]
        at += count
    height = LANES // strips
    mine = lax.axis_index("rows") & (strips - 1)
    block = 0
    for upper in range(total // LANES):
        left = full_ref[:, upper * LANES:(upper + 1) * LANES]
        rows = lax.dot_general(left, full_ref[:, upper * LANES:], (((0,), (0,)), ((), ())),
                               precision=lax.Precision.HIGHEST, preferred_element_type=jnp.float32)
        gram_ref[:, :total - upper * LANES] = rows * scale
        for right in range(upper, total // LANES):
            lane = (right - upper) * LANES
            for low_bit, out_ref in ((0, keep_ref), (1, send_ref)):
                for half in range(strips // 2):
                    strip = pl.multiple_of(((low_bit + 2 * half) ^ mine) * height, height)
                    out_ref[half, block * height:(block + 1) * height, :] = gram_ref[
                        pl.ds(strip, height), lane:lane + LANES]
            block += 1


def partial_gram(pieces, rows, peers, strips, scale):
    total = pieces[0].shape[1] * peers
    tiles = total // LANES
    half = jax.ShapeDtypeStruct(
        (strips // 2, tiles * (tiles + 1) // 2 * (LANES // strips), LANES), jnp.float32)
    return pl.pallas_call(
        functools.partial(gram_kernel, strips=strips, scale=scale, peers=peers),
        out_shape=[half, half],
        scratch_shapes=[pltpu.VMEM((rows, total), jnp.float32), pltpu.VMEM((LANES, total), jnp.float32)],
        compiler_params=pltpu.CompilerParams(vmem_limit_bytes=16 << 20),
    )(*pieces)


def lane_splat(value, lane):
    return jnp.broadcast_to(value[:, lane:lane + 1], (value.shape[0], LANES))


def row_splat(value, row):
    return jnp.broadcast_to(value[row:row + 1, :], value.shape)


def factor_tile(tile):
    done = []
    copies = tile[0].shape[1] // LANES
    sub_row = lax.broadcasted_iota(jnp.int32, tile[0].shape, 0)

    def widen(value):
        return jnp.concatenate([value] * copies, axis=1)

    for at in range(len(tile)):
        lead = tile[at]
        columns = [lane_splat(lead[:, :LANES], SUB * at + j) for j in range(SUB)]
        pivot = {(i, j): row_splat(columns[j], i) for j in range(SUB) for i in range(j + 1)}
        below = [[lane_splat(tile[u][:, :LANES], SUB * at + j) for j in range(SUB)]
                 for u in range(at + 1, len(tile))]
        rows = [row_splat(lead, m) for m in range(SUB)]
        panel = jnp.zeros_like(lead)
        for m in range(SUB):
            inverse = lax.rsqrt(pivot[m, m])
            for j in range(m + 1, SUB):
                pivot[m, j] = pivot[m, j] * inverse
            for i in range(m + 1, SUB):
                for j in range(i, SUB):
                    pivot[i, j] = pivot[i, j] - pivot[m, i] * pivot[m, j]
            rows[m] = rows[m] * widen(inverse)
            for j in range(m + 1, SUB):
                rows[j] = rows[j] - widen(pivot[m, j]) * rows[m]
            panel = jnp.where(sub_row == m, rows[m], panel)
            for u, column in enumerate(below):
                column[m] = column[m] * inverse
                for j in range(m + 1, SUB):
                    column[j] = column[j] - pivot[m, j] * column[m]
                tile[at + 1 + u] = tile[at + 1 + u] - widen(column[m]) * rows[m]
        done.append(panel)
    return done


def factor_kernel(even_ref, odd_ref, out_ref, gram_ref, factor_ref, *, strips):
    total = gram_ref.shape[0]
    tiles = total // LANES
    height = LANES // strips
    mine = lax.axis_index("rows") & (strips - 1)
    block = 0
    for upper in range(tiles):
        for right in range(upper, tiles):
            for low_bit, in_ref in ((0, even_ref), (1, odd_ref)):
                for half in range(strips // 2):
                    strip = pl.multiple_of(((low_bit + 2 * half) ^ mine) * height, height)
                    gram_ref[pl.ds(upper * LANES + strip, height), right * LANES:(right + 1) * LANES] = in_ref[
                        half, block * height:(block + 1) * height, :]
            block += 1
    factor_ref[...] = jnp.zeros_like(factor_ref)
    row = lax.broadcasted_iota(jnp.int32, (LANES, LANES), 0)
    col = lax.broadcasted_iota(jnp.int32, (LANES, LANES), 1)
    identity = (row == col).astype(jnp.float32)
    for at in range(tiles):
        here = slice(at * LANES, (at + 1) * LANES)
        diagonal = jnp.concatenate([gram_ref[here, here], identity], axis=1)
        slabs = [diagonal[SUB * t:SUB * t + SUB] for t in range(LANES // SUB)]
        factored = jnp.concatenate(factor_tile(slabs), axis=0)
        factor_ref[here, here] = jnp.where(col >= row, factored[:, :LANES], 0.0)
        if at < tiles - 1:
            rest = (at + 1) * LANES
            panel = jnp.dot(factored[:, LANES:], gram_ref[here, rest:], precision=lax.Precision.HIGHEST,
                            preferred_element_type=jnp.float32)
            factor_ref[here, rest:] = panel
            for below in range(at + 1, tiles):
                skip = (below - at - 1) * LANES
                gram_ref[below * LANES:(below + 1) * LANES, below * LANES:] -= lax.dot_general(
                    panel[:, skip:skip + LANES], panel[:, skip:], (((0,), (0,)), ((), ())),
                    precision=lax.Precision.HIGHEST, preferred_element_type=jnp.float32)
    width = out_ref.shape[1]
    first = pl.multiple_of(lax.axis_index("cols") * width, width)
    out_ref[...] = factor_ref[:, pl.ds(first, width)]


def factor_panel(even, odd, total, width):
    strips = 2 * even.shape[0]
    return pl.pallas_call(
        functools.partial(factor_kernel, strips=strips),
        out_shape=jax.ShapeDtypeStruct((total, width), jnp.float32),
        scratch_shapes=[pltpu.VMEM((total, total), jnp.float32)] * 2,
        compiler_params=pltpu.CompilerParams(vmem_limit_bytes=48 << 20),
    )(even, odd)


def reduce_run(keep, send, order):
    value = keep + swapped(send, "rows", 0)
    for bit in order:
        half = value.shape[0] // 2
        value = value[:half] + swapped(value[half:], "rows", bit)
    return value


def body(slab, sign_bits, block_mask, sample_rows):
    row_count, panel_width = slab.shape
    groups = lax.axis_size("rows")
    peers = lax.axis_size("cols")
    bits = groups.bit_length() - 1
    pick_count = sample_rows.shape[0]
    signs = sign_bits.reshape(row_count // LANES, LANES)
    picks = sample_rows
    runs = 4
    rows = row_count // runs
    mixed = []
    source = slab
    for bit in range(bits):
        other = swapped(picks, "rows", bit)
        run = bit - (bits - runs)
        if run >= 0:
            made = mix_run(source, signs, block_mask, run * rows, rows, mixed if run == runs - 1 else [])
            other, made, source = lax.optimization_barrier((other, made, source))
            mixed.append(made)
        picks = jnp.concatenate([picks, other])
    mixed = mixed[-1]
    first = pick_count // 2
    cross = list(range(1, bits))
    sketch = []
    pieces = []
    for start, count, order in ((0, first, cross), (first, pick_count - first, cross[1:] + cross[:1])):
        keep, send = pick_rows(picks, mixed, start, count, order, groups)
        part = reduce_run(keep, send, order)
        sketch.append(part)
        pieces.append(part)
        for peer in range(1, peers):
            pieces.append(lax.ppermute(part, "cols", [(i, i ^ peer) for i in range(peers)]))
    sketch = jnp.concatenate(sketch)
    keep, send = partial_gram(pieces, pick_count, peers, 4, 1.0 / (pick_count * groups))
    gram = keep + swapped(send, "rows", 0)
    gram = gram[:1] + swapped(gram[1:], "rows", 1)
    for bit in range(2, bits):
        gram = gram + swapped(gram, "rows", bit)
    gram = jnp.concatenate([gram, swapped(gram, "rows", 1)])
    r_panel = factor_panel(gram, swapped(gram, "rows", 0), panel_width * peers, panel_width)
    return (sketch, r_panel)


def solution(mesh):
    in_specs = (P("rows", "cols"), P("rows"), P("rows"), P("rows"))
    out_specs = (P("rows", "cols"), P(None, "cols"))
    return jax.shard_map(body, mesh=mesh, in_specs=in_specs, out_specs=out_specs, check_vma=False)
```

time: 121 us -> 110 us (0.909)
  blocking collectives: 5.64 us -> 0 us
  starting transfers between devices: 21.7 us -> 16.4 us
  waiting for transfers between devices: 54.1 us -> 49.7 us
  Pallas kernels: 36.2 us -> 39.2 us
    ppermute x14 -> x18, starting transfers between devices: 21.7 us -> 13.2 us  [swapped(): lax.ppermute(value, axis, [(i, i ^ 1 << bit) for i in range(lax.axis_size...]
    ppermute x14 -> x18, waiting for transfers between devices: 54.1 us -> 47 us  [swapped(): lax.ppermute(value, axis, [(i, i ^ 1 << bit) for i in range(lax.axis_size...]
    all_gather x1 -> x0, blocking collectives: 5.64 us -> none  [body(): full_rows = lax.all_gather(sketch, 'cols', axis=1, tiled=True)]
    ppermute x0 -> x2, starting transfers between devices: none -> 3.17 us  [body(): lax.ppermute(part, 'cols', [(i, i ^ peer) for i in range(peers)])]
    pallas_call x2 -> x7, Pallas kernels: 17.2 us -> 20.2 us  [the longest x4 13.4 us: mix_run(): pl.pallas_call(functools.partial(mix_kernel, first=first, earlier=len(ear...]
    ppermute x0 -> x2, waiting for transfers between devices: none -> 2.75 us  [body(): lax.ppermute(part, 'cols', [(i, i ^ peer) for i in range(peers)])]
  transfers between devices with their start and end apart: 14 -> 20, of which waited for: 14 -> 14; matrix products, arithmetic and copies ran while one was open for 0% -> 2% of each run, Pallas kernels for 0% -> 15%
where the time goes in v3:
time: 110 us; the launch traced here: 109 us
  waiting for transfers between devices  49.7 us (45%)
  Pallas kernels  39.2 us (36%)
  starting transfers between devices  16.4 us (15%)
  local copies, waits for them, and re-layouts  2.18 us (2%)
    ppermute x18, waiting for transfers between devices, swapped(): lax.ppermute(value, axis, [(i, i ^ 1 << bit) for i in range(lax.axis_size...  47 us
    pallas_call x1, Pallas kernels, factor_panel(): pl.pallas_call(functools.partial(factor_kernel, strips=strips), out_shape...  19 us
    pallas_call x4, Pallas kernels, mix_run(): pl.pallas_call(functools.partial(mix_kernel, first=first, earlier=len(ear...  13.4 us
    ppermute x18, starting transfers between devices, swapped(): lax.ppermute(value, axis, [(i, i ^ 1 << bit) for i in range(lax.axis_size...  13.2 us
    pallas_call x2, Pallas kernels, pick_rows(): pl.pallas_call(functools.partial(pick_kernel, start=start, count=count, o...  5.99 us
    ppermute x2, starting transfers between devices, body(): lax.ppermute(part, 'cols', [(i, i ^ peer) for i in range(peers)])  3.17 us
    ppermute x2, waiting for transfers between devices, body(): lax.ppermute(part, 'cols', [(i, i ^ peer) for i in range(peers)])  2.75 us
  transfers between devices with their start and end apart: 20, of which 14 were waited for; matrix products, arithmetic and copies ran while one was open for 2% of the time, Pallas kernels for 15%

profile of v3, /device:TPU:0, one launch (start us, length us, event | category | flops | bytes accessed | tf_op | source)
XLA Modules:
  0.0 109.5 jit_solution(5372783886238414986)
XLA Ops:
  3.2 2.9 %shard_map.59.refs_0_ = f32[2048,256]{1,0:T(8,128)S(1)} custom-call(f32[8192,256]{1,0:T(8,128)} %slab_ref.4, s32[64,128]{1,0:T(8,128)S(1)} %bitcast.1, s32[64]{0:T(128)S(1)} %copy-done.2), custom_call_target="tpu_custom_call" | custom-call | tf_op jit(solution)/shard_map/pallas_call | solution.py:110
  6.1 2.6 %collective-permute-start.1 = (s32[256]{0:T(256)S(1)}, s32[256]{0:T(256)S(1)}, u32[]{:S(2)}, u32[]{:S(2)}) collective-permute-start(s32[256]{0:T(256)S(1)} %pad_add_fusion.2), channel_id=1, source_target_pairs={{0,4},{2,6},{4,0},{6,2},{8,12},{10,14},{12,8},{14,10},{16,20},{18,... | collective-permute-start | bytes 3080 | tf_op jit(solution)/shard_map/ppermute | solution.py:17
  8.7 2.9 %shard_map.60.refs_1_ = f32[2048,256]{1,0:T(8,128)S(1)} custom-call(f32[8192,256]{1,0:T(8,128)} %slab_ref.4, s32[64,128]{1,0:T(8,128)S(1)} %bitcast.2, s32[64]{0:T(128)S(1)} %copy-done.2), custom_call_target="tpu_custom_call" | custom-call | tf_op jit(solution)/shard_map/pallas_call | solution.py:110
  11.6 1.6 %collective-permute-start.2 = (s32[512]{0:T(512)S(1)}, s32[512]{0:T(512)S(1)}, u32[]{:S(2)}, u32[]{:S(2)}) collective-permute-start(s32[512]{0:T(512)S(1)} %pad_add_fusion.1), channel_id=1, source_target_pairs={{0,8},{2,10},{4,12},{6,14},{8,0},{10,2},{12,4},{14,6},{16,24},{18,... | collective-permute-start | bytes 6152 | tf_op jit(solution)/shard_map/ppermute | solution.py:17
  13.3 2.9 %shard_map.61.refs_2_ = f32[2048,256]{1,0:T(8,128)S(1)} custom-call(f32[8192,256]{1,0:T(8,128)} %slab_ref.4, s32[64,128]{1,0:T(8,128)S(1)} %bitcast.3, s32[64]{0:T(128)S(1)} %copy-done.2), custom_call_target="tpu_custom_call" | custom-call | tf_op jit(solution)/shard_map/pallas_call | solution.py:110
  16.2 2.7 %collective-permute-start.3 = (s32[1024]{0:T(1024)S(1)}, s32[1024]{0:T(1024)S(1)}, u32[]{:S(2)}, u32[]{:S(2)}) collective-permute-start(s32[1024]{0:T(1024)S(1)} %pad_add_fusion), channel_id=1, source_target_pairs={{0,16},{2,18},{4,20},{6,22},{8,24},{10,26},{12,28},{14,30},{16,0},... | collective-permute-start | bytes 12296 | tf_op jit(solution)/shard_map/ppermute | solution.py:17
  18.9 4.7 %shard_map.62.mixed_ref = f32[8192,256]{1,0:T(8,128)S(1)} custom-call(f32[8192,256]{1,0:T(8,128)} %slab_ref.4, s32[64,128]{1,0:T(8,128)S(1)} %bitcast.4, s32[64]{0:T(128)S(1)} %copy-done.3, f32[2048,256]{1,0:T(8,128)S(1)} %shard_map.59.refs_0_, f32[2048,256]{1,0:T(8,128)S(1)} %shard_map.60.refs_1_, f32[2048,256]{1,0:T(8,128)S(1)} %shard_map.61.refs_2_), custom_call_target="tpu_custom_call" | custom-call | tf_op jit(solution)/shard_map/pallas_call | solution.py:110
  23.6 2.9 %shard_map.63 = (f32[512,256]{1,0:T(8,128)S(1)}, f32[512,256]{1,0:T(8,128)S(1)}) custom-call(s32[2048]{0:T(1024)S(1)} %constant_dynamic-update-slice_fusion.pick_ref, f32[8192,256]{1,0:T(8,128)S(1)} %shard_map.62.mixed_ref), custom_call_target="tpu_custom_call" | custom-call | tf_op jit(solution)/shard_map/pallas_call | solution.py:150
  26.6 3.1 %shard_map.64 = (f32[512,256]{1,0:T(8,128)S(1)}, f32[512,256]{1,0:T(8,128)S(1)}) custom-call(s32[2048]{0:T(1024)S(1)} %constant_dynamic-update-slice_fusion.pick_ref, f32[8192,256]{1,0:T(8,128)S(1)} %shard_map.62.mixed_ref), custom_call_target="tpu_custom_call" | custom-call | tf_op jit(solution)/shard_map/pallas_call | solution.py:150
  32.7 6.0 %collective-permute-done.5 = f32[256,256]{1,0:T(8,128)S(1)} collective-permute-done((f32[256,256]{1,0:T(8,128)S(1)}, f32[256,256]{1,0:T(8,128)S(1)}, u32[]{:S(2)}, u32[]{:S(2)}) %collective-permute-start.5) | collective-permute-done | bytes 262176 | tf_op jit(solution)/shard_map/ppermute | solution.py:17
  39.5 1.1 %collective-permute-done.9 = f32[256,256]{1,0:T(8,128)S(1)} collective-permute-done((f32[256,256]{1,0:T(8,128)S(1)}, f32[256,256]{1,0:T(8,128)S(1)}, u32[]{:S(2)}, u32[]{:S(2)}) %collective-permute-start.9) | collective-permute-done | bytes 262176 | tf_op jit(solution)/shard_map/ppermute | solution.py:17
  41.0 2.8 %collective-permute-done.6 = f32[128,256]{1,0:T(8,128)S(1)} collective-permute-done((f32[128,256]{1,0:T(8,128)S(1)}, f32[128,256]{1,0:T(8,128)S(1)}, u32[]{:S(2)}, u32[]{:S(2)}) %collective-permute-start.6) | collective-permute-done | bytes 131104 | tf_op jit(solution)/shard_map/ppermute | solution.py:17
  44.2 6.7 %collective-permute-done.10 = f32[128,256]{1,0:T(8,128)S(1)} collective-permute-done((f32[128,256]{1,0:T(8,128)S(1)}, f32[128,256]{1,0:T(8,128)S(1)}, u32[]{:S(2)}, u32[]{:S(2)}) %collective-permute-start.10) | collective-permute-done | bytes 131104 | tf_op jit(solution)/shard_map/ppermute | solution.py:17
  52.2 1.6 %collective-permute-start.12 = (f32[64,256]{1,0:T(8,128)S(1)}, f32[64,256]{1,0:T(8,128)S(1)}, u32[]{:S(2)}, u32[]{:S(2)}) collective-permute-start(f32[64,256]{1,0:T(8,128)S(1)} %slice_add_fusion.6.refs_0_), channel_id=1, source_target_pairs={{0,1},{1,0},{2,3},{3,2},{4,5},{5,4},{6,7},{7,6},{8,9},{9,8},{10,11... | collective-permute-start | bytes 196616 | tf_op jit(solution)/shard_map/ppermute | solution.py:335
  53.8 1.5 %collective-permute-done.11 = f32[64,256]{1,0:T(8,128)S(1)} collective-permute-done((f32[64,256]{1,0:T(8,128)S(1)}, f32[64,256]{1,0:T(8,128)S(1)}, u32[]{:S(2)}, u32[]{:S(2)}) %collective-permute-start.11) | collective-permute-done | bytes 65568 | tf_op jit(solution)/shard_map/ppermute | solution.py:17
  55.3 1.6 %collective-permute-start.13 = (f32[64,256]{1,0:T(8,128)S(1)}, f32[64,256]{1,0:T(8,128)S(1)}, u32[]{:S(2)}, u32[]{:S(2)}) collective-permute-start(f32[64,256]{1,0:T(8,128)S(1)} %slice_add_fusion.5.refs_2_), channel_id=1, source_target_pairs={{0,1},{1,0},{2,3},{3,2},{4,5},{5,4},{6,7},{7,6},{8,9},{9,8},{10,11... | collective-permute-start | bytes 196616 | tf_op jit(solution)/shard_map/ppermute | solution.py:335
  56.9 2.7 %collective-permute-done.13.refs_3_ = f32[64,256]{1,0:T(8,128)S(1)} collective-permute-done((f32[64,256]{1,0:T(8,128)S(1)}, f32[64,256]{1,0:T(8,128)S(1)}, u32[]{:S(2)}, u32[]{:S(2)}) %collective-permute-start.13) | collective-permute-done | bytes 65568 | tf_op jit(solution)/shard_map/ppermute | solution.py:335
  60.5 1.6 %collective-permute-done.14 = f32[2,320,128]{2,1,0:T(8,128)S(1)} collective-permute-done((f32[2,320,128]{2,1,0:T(8,128)S(1)}, f32[2,320,128]{2,1,0:T(8,128)S(1)}, u32[]{:S(2)}, u32[]{:S(2)}) %collective-permute-start.14) | collective-permute-done | bytes 327712 | tf_op jit(solution)/shard_map/ppermute | solution.py:17
  62.9 5.6 %collective-permute-done.15 = f32[1,320,128]{2,1,0:T(8,128)S(1)} collective-permute-done((f32[1,320,128]{2,1,0:T(8,128)S(1)}, f32[1,320,128]{2,1,0:T(8,128)S(1)}, u32[]{:S(2)}, u32[]{:S(2)}) %collective-permute-start.15) | collective-permute-done | bytes 163872 | tf_op jit(solution)/shard_map/ppermute | solution.py:17
  68.6 5.4 %collective-permute-done.16 = f32[1,320,128]{2,1,0:T(8,128)S(1)} collective-permute-done((f32[1,320,128]{2,1,0:T(8,128)S(1)}, f32[1,320,128]{2,1,0:T(8,128)S(1)}, u32[]{:S(2)}, u32[]{:S(2)}) %collective-permute-start.16) | collective-permute-done | bytes 163872 | tf_op jit(solution)/shard_map/ppermute | solution.py:17
  74.1 8.9 %collective-permute-done.17 = f32[1,320,128]{2,1,0:T(8,128)S(1)} collective-permute-done((f32[1,320,128]{2,1,0:T(8,128)S(1)}, f32[1,320,128]{2,1,0:T(8,128)S(1)}, u32[]{:S(2)}, u32[]{:S(2)}) %collective-permute-start.17) | collective-permute-done | bytes 163872 | tf_op jit(solution)/shard_map/ppermute | solution.py:17
  83.7 5.0 %collective-permute-done.18 = f32[1,320,128]{2,1,0:T(8,128)S(1)} collective-permute-done((f32[1,320,128]{2,1,0:T(8,128)S(1)}, f32[1,320,128]{2,1,0:T(8,128)S(1)}, u32[]{:S(2)}, u32[]{:S(2)}) %collective-permute-start.18) | collective-permute-done | bytes 163872 | tf_op jit(solution)/shard_map/ppermute | solution.py:17
  89.5 0.9 collective-permute-done.19.odd_ref
  90.4 19.0 %shard_map.66 = f32[512,256]{1,0:T(8,128)} custom-call(f32[2,320,128]{2,1,0:T(8,128)S(1)} %pad_maximum_fusion.even_ref, f32[2,320,128]{2,1,0:T(8,128)S(1)} %collective-permute-done.19.odd_ref), custom_call_target="tpu_custom_call" | custom-call | tf_op jit(solution)/shard_map/pallas_call | solution.py:288
  (64 shorter events, 11.7 us)
Async XLA Ops:
  0.6 5.5 %collective-permute-start = (s32[128]{0:T(128)}, s32[128]{0:T(128)S(1)}, u32[]{:S(2)}, u32[]{:S(2)}) collective-permute-start(s32[128]{0:T(128)} %param.7), channel_id=1, source_target_pairs={{0,2},{2,0},{4,6},{6,4},{8,10},{10,8},{12,14},{14,12},{16,18},{18,... | collective-permute-start | bytes 1544 | tf_op jit(solution)/shard_map/ppermute | solution.py:17
  1.8 0.8 copy-start
  3.2 2.9 %copy-start.4 = (s32[128]{0:T(128)S(1)}, s32[128]{0:T(128)}, u32[]{:S(2)}) copy-start(s32[128]{0:T(128)} %param.7) | copy-start | bytes 1540
  6.1 5.5 %collective-permute-start.1 = (s32[256]{0:T(256)S(1)}, s32[256]{0:T(256)S(1)}, u32[]{:S(2)}, u32[]{:S(2)}) collective-permute-start(s32[256]{0:T(256)S(1)} %pad_add_fusion.2), channel_id=1, source_target_pairs={{0,4},{2,6},{4,0},{6,2},{8,12},{10,14},{12,8},{14,10},{16,20},{18,... | collective-permute-start | bytes 3080 | tf_op jit(solution)/shard_map/ppermute | solution.py:17
  11.6 4.6 %collective-permute-start.2 = (s32[512]{0:T(512)S(1)}, s32[512]{0:T(512)S(1)}, u32[]{:S(2)}, u32[]{:S(2)}) collective-permute-start(s32[512]{0:T(512)S(1)} %pad_add_fusion.1), channel_id=1, source_target_pairs={{0,8},{2,10},{4,12},{6,14},{8,0},{10,2},{12,4},{14,6},{16,24},{18,... | collective-permute-start | bytes 6152 | tf_op jit(solution)/shard_map/ppermute | solution.py:17
  13.3 5.6 %copy-start.1 = (s32[8192]{0:T(1024)S(1)}, s32[8192]{0:T(1024)}, u32[]{:S(2)}) copy-start(s32[8192]{0:T(1024)} %param.5) | copy-start | bytes 98308
  13.3 5.6 %copy-start.3 = (s32[64]{0:T(128)S(1)}, s32[64]{0:T(128)}, u32[]{:S(2)}) copy-start(s32[64]{0:T(128)} %mask_ref.7) | copy-start | bytes 772
  16.2 7.4 %collective-permute-start.3 = (s32[1024]{0:T(1024)S(1)}, s32[1024]{0:T(1024)S(1)}, u32[]{:S(2)}, u32[]{:S(2)}) collective-permute-start(s32[1024]{0:T(1024)S(1)} %pad_add_fusion), channel_id=1, source_target_pairs={{0,16},{2,18},{4,20},{6,22},{8,24},{10,26},{12,28},{14,30},{16,0},... | collective-permute-start | bytes 12296 | tf_op jit(solution)/shard_map/ppermute | solution.py:17
  26.5 3.7 %collective-permute-start.4 = (f32[512,256]{1,0:T(8,128)S(1)}, f32[512,256]{1,0:T(8,128)S(1)}, u32[]{:S(2)}, u32[]{:S(2)}) collective-permute-start(f32[512,256]{1,0:T(8,128)S(1)} %get-tuple-element.31), channel_id=1, source_target_pairs={{0,2},{2,0},{4,6},{6,4},{8,10},{10,8},{12,14},{14,12},{16,18},{18,... | collective-permute-start | bytes 1572872 | tf_op jit(solution)/shard_map/ppermute | solution.py:17
  29.7 2.1 %collective-permute-start.8 = (f32[512,256]{1,0:T(8,128)S(1)}, f32[512,256]{1,0:T(8,128)S(1)}, u32[]{:S(2)}, u32[]{:S(2)}) collective-permute-start(f32[512,256]{1,0:T(8,128)S(1)} %get-tuple-element.33), channel_id=1, source_target_pairs={{0,2},{2,0},{4,6},{6,4},{8,10},{10,8},{12,14},{14,12},{16,18},{18,... | collective-permute-start | bytes 1572872 | tf_op jit(solution)/shard_map/ppermute | solution.py:17
  30.4 8.3 %collective-permute-start.5 = (f32[256,256]{1,0:T(8,128)S(1)}, f32[256,256]{1,0:T(8,128)S(1)}, u32[]{:S(2)}, u32[]{:S(2)}) collective-permute-start(f32[256,256]{1,0:T(8,128)S(1)} %slice.57), channel_id=1, source_target_pairs={{0,4},{2,6},{4,0},{6,2},{8,12},{10,14},{12,8},{14,10},{16,20},{18,... | collective-permute-start | bytes 786440 | tf_op jit(solution)/shard_map/ppermute | solution.py:17
  31.9 8.7 %collective-permute-start.9 = (f32[256,256]{1,0:T(8,128)S(1)}, f32[256,256]{1,0:T(8,128)S(1)}, u32[]{:S(2)}, u32[]{:S(2)}) collective-permute-start(f32[256,256]{1,0:T(8,128)S(1)} %slice.63), channel_id=1, source_target_pairs={{0,8},{2,10},{4,12},{6,14},{8,0},{10,2},{12,4},{14,6},{16,24},{18,... | collective-permute-start | bytes 786440 | tf_op jit(solution)/shard_map/ppermute | solution.py:17
  38.7 5.0 %collective-permute-start.6 = (f32[128,256]{1,0:T(8,128)S(1)}, f32[128,256]{1,0:T(8,128)S(1)}, u32[]{:S(2)}, u32[]{:S(2)}) collective-permute-start(f32[128,256]{1,0:T(8,128)S(1)} %slice.59), channel_id=1, source_target_pairs={{0,8},{2,10},{4,12},{6,14},{8,0},{10,2},{12,4},{14,6},{16,24},{18,... | collective-permute-start | bytes 393224 | tf_op jit(solution)/shard_map/ppermute | solution.py:17
  40.6 10.3 %collective-permute-start.10 = (f32[128,256]{1,0:T(8,128)S(1)}, f32[128,256]{1,0:T(8,128)S(1)}, u32[]{:S(2)}, u32[]{:S(2)}) collective-permute-start(f32[128,256]{1,0:T(8,128)S(1)} %slice.65), channel_id=1, source_target_pairs={{0,16},{2,18},{4,20},{6,22},{8,24},{10,26},{12,28},{14,30},{16,0},... | collective-permute-start | bytes 393224 | tf_op jit(solution)/shard_map/ppermute | solution.py:17
  43.8 8.3 %collective-permute-start.7 = (f32[64,256]{1,0:T(8,128)S(1)}, f32[64,256]{1,0:T(8,128)S(1)}, u32[]{:S(2)}, u32[]{:S(2)}) collective-permute-start(f32[64,256]{1,0:T(8,128)S(1)} %slice.61), channel_id=1, source_target_pairs={{0,16},{2,18},{4,20},{6,22},{8,24},{10,26},{12,28},{14,30},{16,0},... | collective-permute-start | bytes 196616 | tf_op jit(solution)/shard_map/ppermute | solution.py:17
  51.0 4.3 %collective-permute-start.11 = (f32[64,256]{1,0:T(8,128)S(1)}, f32[64,256]{1,0:T(8,128)S(1)}, u32[]{:S(2)}, u32[]{:S(2)}) collective-permute-start(f32[64,256]{1,0:T(8,128)S(1)} %slice.67), channel_id=1, source_target_pairs={{0,4},{2,6},{4,0},{6,2},{8,12},{10,14},{12,8},{14,10},{16,20},{18,... | collective-permute-start | bytes 196616 | tf_op jit(solution)/shard_map/ppermute | solution.py:17
  52.2 4.7 %collective-permute-start.12 = (f32[64,256]{1,0:T(8,128)S(1)}, f32[64,256]{1,0:T(8,128)S(1)}, u32[]{:S(2)}, u32[]{:S(2)}) collective-permute-start(f32[64,256]{1,0:T(8,128)S(1)} %slice_add_fusion.6.refs_0_), channel_id=1, source_target_pairs={{0,1},{1,0},{2,3},{3,2},{4,5},{5,4},{6,7},{7,6},{8,9},{9,8},{10,11... | collective-permute-start | bytes 196616 | tf_op jit(solution)/shard_map/ppermute | solution.py:335
  55.3 4.3 %collective-permute-start.13 = (f32[64,256]{1,0:T(8,128)S(1)}, f32[64,256]{1,0:T(8,128)S(1)}, u32[]{:S(2)}, u32[]{:S(2)}) collective-permute-start(f32[64,256]{1,0:T(8,128)S(1)} %slice_add_fusion.5.refs_2_), channel_id=1, source_target_pairs={{0,1},{1,0},{2,3},{3,2},{4,5},{5,4},{6,7},{7,6},{8,9},{9,8},{10,11... | collective-permute-start | bytes 196616 | tf_op jit(solution)/shard_map/ppermute | solution.py:335
  60.5 1.7 %collective-permute-start.14 = (f32[2,320,128]{2,1,0:T(8,128)S(1)}, f32[2,320,128]{2,1,0:T(8,128)S(1)}, u32[]{:S(2)}, u32[]{:S(2)}) collective-permute-start(f32[2,320,128]{2,1,0:T(8,128)S(1)} %get-tuple-element.35), channel_id=1, source_target_pairs={{0,2},{2,0},{4,6},{6,4},{8,10},{10,8},{12,14},{14,12},{16,18},{18,... | collective-permute-start | bytes 983048 | tf_op jit(solution)/shard_map/ppermute | solution.py:17
  62.2 6.3 %collective-permute-start.15 = (f32[1,320,128]{2,1,0:T(8,128)S(1)}, f32[1,320,128]{2,1,0:T(8,128)S(1)}, u32[]{:S(2)}, u32[]{:S(2)}) collective-permute-start(f32[1,320,128]{2,1,0:T(8,128)S(1)} %slice.69), channel_id=1, source_target_pairs={{0,4},{2,6},{4,0},{6,2},{8,12},{10,14},{12,8},{14,10},{16,20},{18,... | collective-permute-start | bytes 491528 | tf_op jit(solution)/shard_map/ppermute | solution.py:17
  68.6 5.5 %collective-permute-start.16 = (f32[1,320,128]{2,1,0:T(8,128)S(1)}, f32[1,320,128]{2,1,0:T(8,128)S(1)}, u32[]{:S(2)}, u32[]{:S(2)}) collective-permute-start(f32[1,320,128]{2,1,0:T(8,128)S(1)} %slice_add_fusion.2), channel_id=1, source_target_pairs={{0,8},{2,10},{4,12},{6,14},{8,0},{10,2},{12,4},{14,6},{16,24},{18,... | collective-permute-start | bytes 491528 | tf_op jit(solution)/shard_map/ppermute | solution.py:17
  74.1 9.0 %collective-permute-start.17 = (f32[1,320,128]{2,1,0:T(8,128)S(1)}, f32[1,320,128]{2,1,0:T(8,128)S(1)}, u32[]{:S(2)}, u32[]{:S(2)}) collective-permute-start(f32[1,320,128]{2,1,0:T(8,128)S(1)} %add.46), channel_id=1, source_target_pairs={{0,16},{2,18},{4,20},{6,22},{8,24},{10,26},{12,28},{14,30},{16,0},... | collective-permute-start | bytes 491528 | tf_op jit(solution)/shard_map/ppermute | solution.py:17
  83.0 5.7 %collective-permute-start.18 = (f32[1,320,128]{2,1,0:T(8,128)S(1)}, f32[1,320,128]{2,1,0:T(8,128)S(1)}, u32[]{:S(2)}, u32[]{:S(2)}) collective-permute-start(f32[1,320,128]{2,1,0:T(8,128)S(1)} %add.47), channel_id=1, source_target_pairs={{0,4},{2,6},{4,0},{6,2},{8,12},{10,14},{12,8},{14,10},{16,20},{18,... | collective-permute-start | bytes 491528 | tf_op jit(solution)/shard_map/ppermute | solution.py:17
  88.7 1.7 %collective-permute-start.19 = (f32[2,320,128]{2,1,0:T(8,128)S(1)}, f32[2,320,128]{2,1,0:T(8,128)S(1)}, u32[]{:S(2)}, u32[]{:S(2)}) collective-permute-start(f32[2,320,128]{2,1,0:T(8,128)S(1)} %pad_maximum_fusion.even_ref), channel_id=1, source_target_pairs={{0,2},{2,0},{4,6},{6,4},{8,10},{10,8},{12,14},{14,12},{16,18},{18,... | collective-permute-start | bytes 983048 | tf_op jit(solution)/shard_map/ppermute | solution.py:17
  (1 other events, 0.7 us)

commit v4 on v3

--- a/solution.py
+++ b/solution.py
@@ -11,6 +11,7 @@
 TILE = 256
 LANES = 128
 SUB = 8
+AHEAD = 3
 
 
 def swapped(value, axis, bit):
@@ -200,29 +201,61 @@
     )(*pieces)
 
 
+def split_three(value):
+    high = value.astype(jnp.bfloat16).astype(jnp.float32)
+    rest = value - high
+    middle = rest.astype(jnp.bfloat16).astype(jnp.float32)
+    return high, middle, rest - middle
+
+
+def left_terms(value, axis):
+    high, middle, low = split_three(value)
+    return jnp.concatenate([high, high, middle, high, middle, low], axis=axis).astype(jnp.bfloat16)
+
+
+def right_terms(value):
+    high, middle, low = split_three(value)
+    return jnp.concatenate([high, middle, high, low, middle, high], axis=0).astype(jnp.bfloat16)
+
+
+def times(left, right):
+    return jnp.dot(left_terms(left, 1), right_terms(right), preferred_element_type=jnp.float32)
+
+
+def inner_product(left, right):
+    return lax.dot_general(left_terms(left, 0), right_terms(right), (((0,), (0,)), ((), ())),
+                           preferred_element_type=jnp.float32)
+
+
 def lane_splat(value, lane):
     return jnp.broadcast_to(value[:, lane:lane + 1], (value.shape[0], LANES))
 
 
-def row_splat(value, row):
-    return jnp.broadcast_to(value[row:row + 1, :], value.shape)
-
-
-def factor_tile(tile):
+def factor_tile(diagonal, column_ref, lead_ref):
+    row = lax.broadcasted_iota(jnp.int32, (LANES, LANES), 0)
+    col = lax.broadcasted_iota(jnp.int32, (LANES, LANES), 1)
+    identity = (row == col).astype(jnp.float32)
+    whole = jnp.concatenate([diagonal, identity], axis=1)
+    slabs = LANES // SUB
+    tile = [whole[SUB * t:SUB * t + SUB] for t in range(slabs)]
+    sub_row = lax.broadcasted_iota(jnp.int32, tile[0].shape, 0)
     done = []
-    copies = tile[0].shape[1] // LANES
-    sub_row = lax.broadcasted_iota(jnp.int32, tile[0].shape, 0)
 
     def widen(value):
-        return jnp.concatenate([value] * copies, axis=1)
-
-    for at in range(len(tile)):
+        return jnp.concatenate([value, value], axis=1)
+
+    for at in range(slabs):
         lead = tile[at]
-        columns = [lane_splat(lead[:, :LANES], SUB * at + j) for j in range(SUB)]
-        pivot = {(i, j): row_splat(columns[j], i) for j in range(SUB) for i in range(j + 1)}
-        below = [[lane_splat(tile[u][:, :LANES], SUB * at + j) for j in range(SUB)]
-                 for u in range(at + 1, len(tile))]
-        rows = [row_splat(lead, m) for m in range(SUB)]
+        direct = range(at + 1, min(slabs, at + 1 + AHEAD))
+        for j in range(SUB):
+            column_ref[(at * SUB + j) * SUB:(at * SUB + j + 1) * SUB, :] = lane_splat(lead[:, :LANES], SUB * at + j)
+        for half in range(2):
+            lead_ref[half * LANES + at * SUB:half * LANES + (at + 1) * SUB, :] = lead[:, half * LANES:(half + 1) * LANES]
+        pivot = {(i, j): column_ref[pl.ds((at * SUB + j) * SUB + i, SUB, stride=0), :]
+                 for j in range(SUB) for i in range(j + 1)}
+        below = [[lane_splat(tile[u][:, :LANES], SUB * at + j) for j in range(SUB)] for u in direct]
+        rows = [jnp.concatenate([lead_ref[pl.ds(half * LANES + at * SUB + m, SUB, stride=0), :] for half in range(2)],
+                                axis=1) for m in range(SUB)]
         panel = jnp.zeros_like(lead)
         for m in range(SUB):
             inverse = lax.rsqrt(pivot[m, m])
@@ -235,16 +268,22 @@
             for j in range(m + 1, SUB):
                 rows[j] = rows[j] - widen(pivot[m, j]) * rows[m]
             panel = jnp.where(sub_row == m, rows[m], panel)
-            for u, column in enumerate(below):
+            for column, u in zip(below, direct):
                 column[m] = column[m] * inverse
                 for j in range(m + 1, SUB):
                     column[j] = column[j] - pivot[m, j] * column[m]
-                tile[at + 1 + u] = tile[at + 1 + u] - widen(column[m]) * rows[m]
+                tile[u] = tile[u] - widen(column[m]) * rows[m]
         done.append(panel)
-    return done
-
-
-def factor_kernel(even_ref, odd_ref, out_ref, gram_ref, factor_ref, *, strips):
+        if at + 1 + AHEAD < slabs:
+            update = lax.dot_general(left_terms(panel[:, :LANES], 0), right_terms(panel), (((0,), (0,)), ((), ())),
+                                     preferred_element_type=jnp.float32)
+            for u in range(at + 1 + AHEAD, slabs):
+                tile[u] = tile[u] - update[SUB * u:SUB * u + SUB]
+    factored = jnp.concatenate(done, axis=0)
+    return jnp.where(col >= row, factored[:, :LANES], 0.0), factored[:, LANES:]
+
+
+def factor_kernel(even_ref, odd_ref, out_ref, gram_ref, factor_ref, column_ref, lead_ref, *, strips):
     total = gram_ref.shape[0]
     tiles = total // LANES
     height = LANES // strips
@@ -259,25 +298,15 @@
                         half, block * height:(block + 1) * height, :]
             block += 1
     factor_ref[...] = jnp.zeros_like(factor_ref)
-    row = lax.broadcasted_iota(jnp.int32, (LANES, LANES), 0)
-    col = lax.broadcasted_iota(jnp.int32, (LANES, LANES), 1)
-    identity = (row == col).astype(jnp.float32)
     for at in range(tiles):
         here = slice(at * LANES, (at + 1) * LANES)
-        diagonal = jnp.concatenate([gram_ref[here, here], identity], axis=1)
-        slabs = [diagonal[SUB * t:SUB * t + SUB] for t in range(LANES // SUB)]
-        factored = jnp.concatenate(factor_tile(slabs), axis=0)
-        factor_ref[here, here] = jnp.where(col >= row, factored[:, :LANES], 0.0)
+        factor, inverse = factor_tile(gram_ref[here, here], column_ref, lead_ref)
+        factor_ref[here, here] = factor
         if at < tiles - 1:
             rest = (at + 1) * LANES
-            panel = jnp.dot(factored[:, LANES:], gram_ref[here, rest:], precision=lax.Precision.HIGHEST,
-                            preferred_element_type=jnp.float32)
+            panel = times(inverse, gram_ref[here, rest:])
             factor_ref[here, rest:] = panel
-            for below in range(at + 1, tiles):
-                skip = (below - at - 1) * LANES
-                gram_ref[below * LANES:(below + 1) * LANES, below * LANES:] -= lax.dot_general(
-                    panel[:, skip:skip + LANES], panel[:, skip:], (((0,), (0,)), ((), ())),
-                    precision=lax.Precision.HIGHEST, preferred_element_type=jnp.float32)
+            gram_ref[rest:, rest:] -= inner_product(panel, panel)
     width = out_ref.shape[1]
     first = pl.multiple_of(lax.axis_index("cols") * width, width)
     out_ref[...] = factor_ref[:, pl.ds(first, width)]
@@ -288,7 +317,8 @@
     return pl.pallas_call(
         functools.partial(factor_kernel, strips=strips),
         out_shape=jax.ShapeDtypeStruct((total, width), jnp.float32),
-        scratch_shapes=[pltpu.VMEM((total, total), jnp.float32)] * 2,
+        scratch_shapes=[pltpu.VMEM((total, total), jnp.float32)] * 2 + [
+            pltpu.VMEM((LANES * SUB, LANES), jnp.float32), pltpu.VMEM((2 * LANES, LANES), jnp.float32)],
         compiler_params=pltpu.CompilerParams(vmem_limit_bytes=48 << 20),
     )(even, odd)
 
@@ -326,7 +356,7 @@
     cross = list(range(1, bits))
     sketch = []
     pieces = []
-    for start, count, order in ((0, first, cross), (first, pick_count - first, cross[1:] + cross[:1])):
+    for start, count, order in ((0, first, cross), (first, pick_count - first, cross[1:2] + cross[:1] + cross[2:])):
         keep, send = pick_rows(picks, mixed, start, count, order, groups)
         part = reduce_run(keep, send, order)
         sketch.append(part)

time: 110 us -> 103 us (0.936)
  Pallas kernels: 39.2 us -> 34.5 us
  waiting for transfers between devices: 49.7 us -> 47.2 us
    pallas_call x1, Pallas kernels: 19 us -> 14.4 us  [factor_panel(): pl.pallas_call(functools.partial(factor_kernel, strips=strips), out_shape...]
    ppermute x18, waiting for transfers between devices: 47 us -> 43.6 us  [swapped(): lax.ppermute(value, axis, [(i, i ^ 1 << bit) for i in range(lax.axis_size...]
  transfers between devices with their start and end apart: 20 -> 20, of which waited for: 14 -> 14; matrix products, arithmetic and copies ran while one was open for 2% -> 2% of each run, Pallas kernels for 15% -> 16%
where the time goes in v4:
time: 103 us; the launch traced here: 102 us
  waiting for transfers between devices  47.2 us (46%)
  Pallas kernels  34.5 us (33%)
  starting transfers between devices  16.4 us (16%)
  local copies, waits for them, and re-layouts  2.18 us (2%)
  other arithmetic  1.08 us (1%)
    ppermute x18, waiting for transfers between devices, swapped(): lax.ppermute(value, axis, [(i, i ^ 1 << bit) for i in range(lax.axis_size...  43.6 us
    pallas_call x1, Pallas kernels, factor_panel(): pl.pallas_call(functools.partial(factor_kernel, strips=strips), out_shape...  14.4 us
    ppermute x18, starting transfers between devices, swapped(): lax.ppermute(value, axis, [(i, i ^ 1 << bit) for i in range(lax.axis_size...  14.1 us
    pallas_call x4, Pallas kernels, mix_run(): pl.pallas_call(functools.partial(mix_kernel, first=first, earlier=len(ear...  13.4 us
    pallas_call x2, Pallas kernels, pick_rows(): pl.pallas_call(functools.partial(pick_kernel, start=start, count=count, o...  5.99 us
    ppermute x2, waiting for transfers between devices, body(): lax.ppermute(part, 'cols', [(i, i ^ peer) for i in range(peers)])  3.64 us
    ppermute x2, starting transfers between devices, body(): lax.ppermute(part, 'cols', [(i, i ^ peer) for i in range(peers)])  2.27 us
    unnamed x14, local copies, waits for them, and re-layouts  2.1 us
  transfers between devices with their start and end apart: 20, of which 14 were waited for; matrix products, arithmetic and copies ran while one was open for 2% of the time, Pallas kernels for 16%

profile of v4, /device:TPU:0, one launch (start us, length us, event | category | flops | bytes accessed | tf_op | source)
XLA Modules:
  0.0 102.3 jit_solution(2405006173634677539)
XLA Ops:
  3.2 2.9 %shard_map.59.refs_0_ = f32[2048,256]{1,0:T(8,128)S(1)} custom-call(f32[8192,256]{1,0:T(8,128)} %slab_ref.4, s32[64,128]{1,0:T(8,128)S(1)} %bitcast.1, s32[64]{0:T(128)S(1)} %copy-done.2), custom_call_target="tpu_custom_call" | custom-call | tf_op jit(solution)/shard_map/pallas_call | solution.py:111
  6.1 2.6 %collective-permute-start.1 = (s32[256]{0:T(256)S(1)}, s32[256]{0:T(256)S(1)}, u32[]{:S(2)}, u32[]{:S(2)}) collective-permute-start(s32[256]{0:T(256)S(1)} %pad_add_fusion.2), channel_id=1, source_target_pairs={{0,4},{2,6},{4,0},{6,2},{8,12},{10,14},{12,8},{14,10},{16,20},{18,... | collective-permute-start | bytes 3080 | tf_op jit(solution)/shard_map/ppermute | solution.py:18
  8.7 2.9 %shard_map.60.refs_1_ = f32[2048,256]{1,0:T(8,128)S(1)} custom-call(f32[8192,256]{1,0:T(8,128)} %slab_ref.4, s32[64,128]{1,0:T(8,128)S(1)} %bitcast.2, s32[64]{0:T(128)S(1)} %copy-done.2), custom_call_target="tpu_custom_call" | custom-call | tf_op jit(solution)/shard_map/pallas_call | solution.py:111
  11.6 1.6 %collective-permute-start.2 = (s32[512]{0:T(512)S(1)}, s32[512]{0:T(512)S(1)}, u32[]{:S(2)}, u32[]{:S(2)}) collective-permute-start(s32[512]{0:T(512)S(1)} %pad_add_fusion.1), channel_id=1, source_target_pairs={{0,8},{2,10},{4,12},{6,14},{8,0},{10,2},{12,4},{14,6},{16,24},{18,... | collective-permute-start | bytes 6152 | tf_op jit(solution)/shard_map/ppermute | solution.py:18
  13.3 2.9 %shard_map.61.refs_2_ = f32[2048,256]{1,0:T(8,128)S(1)} custom-call(f32[8192,256]{1,0:T(8,128)} %slab_ref.4, s32[64,128]{1,0:T(8,128)S(1)} %bitcast.3, s32[64]{0:T(128)S(1)} %copy-done.2), custom_call_target="tpu_custom_call" | custom-call | tf_op jit(solution)/shard_map/pallas_call | solution.py:111
  16.2 2.7 %collective-permute-start.3 = (s32[1024]{0:T(1024)S(1)}, s32[1024]{0:T(1024)S(1)}, u32[]{:S(2)}, u32[]{:S(2)}) collective-permute-start(s32[1024]{0:T(1024)S(1)} %pad_add_fusion), channel_id=1, source_target_pairs={{0,16},{2,18},{4,20},{6,22},{8,24},{10,26},{12,28},{14,30},{16,0},... | collective-permute-start | bytes 12296 | tf_op jit(solution)/shard_map/ppermute | solution.py:18
  18.9 4.7 %shard_map.62.mixed_ref = f32[8192,256]{1,0:T(8,128)S(1)} custom-call(f32[8192,256]{1,0:T(8,128)} %slab_ref.4, s32[64,128]{1,0:T(8,128)S(1)} %bitcast.4, s32[64]{0:T(128)S(1)} %copy-done.3, f32[2048,256]{1,0:T(8,128)S(1)} %shard_map.59.refs_0_, f32[2048,256]{1,0:T(8,128)S(1)} %shard_map.60.refs_1_, f32[2048,256]{1,0:T(8,128)S(1)} %shard_map.61.refs_2_), custom_call_target="tpu_custom_call" | custom-call | tf_op jit(solution)/shard_map/pallas_call | solution.py:111
  23.6 2.9 %shard_map.63 = (f32[512,256]{1,0:T(8,128)S(1)}, f32[512,256]{1,0:T(8,128)S(1)}) custom-call(s32[2048]{0:T(1024)S(1)} %constant_dynamic-update-slice_fusion.pick_ref, f32[8192,256]{1,0:T(8,128)S(1)} %shard_map.62.mixed_ref), custom_call_target="tpu_custom_call" | custom-call | tf_op jit(solution)/shard_map/pallas_call | solution.py:151
  26.6 3.1 %shard_map.64 = (f32[512,256]{1,0:T(8,128)S(1)}, f32[512,256]{1,0:T(8,128)S(1)}) custom-call(s32[2048]{0:T(1024)S(1)} %constant_dynamic-update-slice_fusion.pick_ref, f32[8192,256]{1,0:T(8,128)S(1)} %shard_map.62.mixed_ref), custom_call_target="tpu_custom_call" | custom-call | tf_op jit(solution)/shard_map/pallas_call | solution.py:151
  32.7 6.0 %collective-permute-done.5 = f32[256,256]{1,0:T(8,128)S(1)} collective-permute-done((f32[256,256]{1,0:T(8,128)S(1)}, f32[256,256]{1,0:T(8,128)S(1)}, u32[]{:S(2)}, u32[]{:S(2)}) %collective-permute-start.5) | collective-permute-done | bytes 262176 | tf_op jit(solution)/shard_map/ppermute | solution.py:18
  39.5 1.1 %collective-permute-done.9 = f32[256,256]{1,0:T(8,128)S(1)} collective-permute-done((f32[256,256]{1,0:T(8,128)S(1)}, f32[256,256]{1,0:T(8,128)S(1)}, u32[]{:S(2)}, u32[]{:S(2)}) %collective-permute-start.9) | collective-permute-done | bytes 262176 | tf_op jit(solution)/shard_map/ppermute | solution.py:18
  41.3 2.5 %collective-permute-done.6 = f32[128,256]{1,0:T(8,128)S(1)} collective-permute-done((f32[128,256]{1,0:T(8,128)S(1)}, f32[128,256]{1,0:T(8,128)S(1)}, u32[]{:S(2)}, u32[]{:S(2)}) %collective-permute-start.6) | collective-permute-done | bytes 131104 | tf_op jit(solution)/shard_map/ppermute | solution.py:18
  44.2 1.4 %collective-permute-done.10 = f32[128,256]{1,0:T(8,128)S(1)} collective-permute-done((f32[128,256]{1,0:T(8,128)S(1)}, f32[128,256]{1,0:T(8,128)S(1)}, u32[]{:S(2)}, u32[]{:S(2)}) %collective-permute-start.10) | collective-permute-done | bytes 131104 | tf_op jit(solution)/shard_map/ppermute | solution.py:18
  45.7 1.2 %collective-permute-start.11 = (f32[64,256]{1,0:T(8,128)S(1)}, f32[64,256]{1,0:T(8,128)S(1)}, u32[]{:S(2)}, u32[]{:S(2)}) collective-permute-start(f32[64,256]{1,0:T(8,128)S(1)} %slice.67), channel_id=1, source_target_pairs={{0,16},{2,18},{4,20},{6,22},{8,24},{10,26},{12,28},{14,30},{16,0},... | collective-permute-start | bytes 196616 | tf_op jit(solution)/shard_map/ppermute | solution.py:18
  46.9 4.3 %collective-permute-done.7 = f32[64,256]{1,0:T(8,128)S(1)} collective-permute-done((f32[64,256]{1,0:T(8,128)S(1)}, f32[64,256]{1,0:T(8,128)S(1)}, u32[]{:S(2)}, u32[]{:S(2)}) %collective-permute-start.7) | collective-permute-done | bytes 65568 | tf_op jit(solution)/shard_map/ppermute | solution.py:18
  51.2 1.6 %collective-permute-start.12 = (f32[64,256]{1,0:T(8,128)S(1)}, f32[64,256]{1,0:T(8,128)S(1)}, u32[]{:S(2)}, u32[]{:S(2)}) collective-permute-start(f32[64,256]{1,0:T(8,128)S(1)} %slice_add_fusion.6.refs_0_), channel_id=1, source_target_pairs={{0,1},{1,0},{2,3},{3,2},{4,5},{5,4},{6,7},{7,6},{8,9},{9,8},{10,11... | collective-permute-start | bytes 196616 | tf_op jit(solution)/shard_map/ppermute | solution.py:365
  53.5 2.0 %collective-permute-done.12.refs_1_ = f32[64,256]{1,0:T(8,128)S(1)} collective-permute-done((f32[64,256]{1,0:T(8,128)S(1)}, f32[64,256]{1,0:T(8,128)S(1)}, u32[]{:S(2)}, u32[]{:S(2)}) %collective-permute-start.12) | collective-permute-done | bytes 65568 | tf_op jit(solution)/shard_map/ppermute | solution.py:365
  55.5 1.6 %collective-permute-done.13.refs_3_ = f32[64,256]{1,0:T(8,128)S(1)} collective-permute-done((f32[64,256]{1,0:T(8,128)S(1)}, f32[64,256]{1,0:T(8,128)S(1)}, u32[]{:S(2)}, u32[]{:S(2)}) %collective-permute-start.13) | collective-permute-done | bytes 65568 | tf_op jit(solution)/shard_map/ppermute | solution.py:365
  58.0 1.6 %collective-permute-done.14 = f32[2,320,128]{2,1,0:T(8,128)S(1)} collective-permute-done((f32[2,320,128]{2,1,0:T(8,128)S(1)}, f32[2,320,128]{2,1,0:T(8,128)S(1)}, u32[]{:S(2)}, u32[]{:S(2)}) %collective-permute-start.14) | collective-permute-done | bytes 327712 | tf_op jit(solution)/shard_map/ppermute | solution.py:18
  60.4 5.6 %collective-permute-done.15 = f32[1,320,128]{2,1,0:T(8,128)S(1)} collective-permute-done((f32[1,320,128]{2,1,0:T(8,128)S(1)}, f32[1,320,128]{2,1,0:T(8,128)S(1)}, u32[]{:S(2)}, u32[]{:S(2)}) %collective-permute-start.15) | collective-permute-done | bytes 163872 | tf_op jit(solution)/shard_map/ppermute | solution.py:18
  66.1 5.4 %collective-permute-done.16 = f32[1,320,128]{2,1,0:T(8,128)S(1)} collective-permute-done((f32[1,320,128]{2,1,0:T(8,128)S(1)}, f32[1,320,128]{2,1,0:T(8,128)S(1)}, u32[]{:S(2)}, u32[]{:S(2)}) %collective-permute-start.16) | collective-permute-done | bytes 163872 | tf_op jit(solution)/shard_map/ppermute | solution.py:18
  71.6 8.9 %collective-permute-done.17 = f32[1,320,128]{2,1,0:T(8,128)S(1)} collective-permute-done((f32[1,320,128]{2,1,0:T(8,128)S(1)}, f32[1,320,128]{2,1,0:T(8,128)S(1)}, u32[]{:S(2)}, u32[]{:S(2)}) %collective-permute-start.17) | collective-permute-done | bytes 163872 | tf_op jit(solution)/shard_map/ppermute | solution.py:18
  81.2 5.0 %collective-permute-done.18 = f32[1,320,128]{2,1,0:T(8,128)S(1)} collective-permute-done((f32[1,320,128]{2,1,0:T(8,128)S(1)}, f32[1,320,128]{2,1,0:T(8,128)S(1)}, u32[]{:S(2)}, u32[]{:S(2)}) %collective-permute-start.18) | collective-permute-done | bytes 163872 | tf_op jit(solution)/shard_map/ppermute | solution.py:18
  87.9 14.4 %shard_map.66 = f32[512,256]{1,0:T(8,128)} custom-call(f32[2,320,128]{2,1,0:T(8,128)S(1)} %pad_maximum_fusion.even_ref, f32[2,320,128]{2,1,0:T(8,128)S(1)} %collective-permute-done.19.odd_ref), custom_call_target="tpu_custom_call" | custom-call | tf_op jit(solution)/shard_map/pallas_call | solution.py:317
  (64 shorter events, 12.5 us)
Async XLA Ops:
  0.6 5.5 %collective-permute-start = (s32[128]{0:T(128)}, s32[128]{0:T(128)S(1)}, u32[]{:S(2)}, u32[]{:S(2)}) collective-permute-start(s32[128]{0:T(128)} %param.7), channel_id=1, source_target_pairs={{0,2},{2,0},{4,6},{6,4},{8,10},{10,8},{12,14},{14,12},{16,18},{18,... | collective-permute-start | bytes 1544 | tf_op jit(solution)/shard_map/ppermute | solution.py:18
  1.8 0.8 copy-start
  3.2 2.9 %copy-start.4 = (s32[128]{0:T(128)S(1)}, s32[128]{0:T(128)}, u32[]{:S(2)}) copy-start(s32[128]{0:T(128)} %param.7) | copy-start | bytes 1540
  6.1 5.5 %collective-permute-start.1 = (s32[256]{0:T(256)S(1)}, s32[256]{0:T(256)S(1)}, u32[]{:S(2)}, u32[]{:S(2)}) collective-permute-start(s32[256]{0:T(256)S(1)} %pad_add_fusion.2), channel_id=1, source_target_pairs={{0,4},{2,6},{4,0},{6,2},{8,12},{10,14},{12,8},{14,10},{16,20},{18,... | collective-permute-start | bytes 3080 | tf_op jit(solution)/shard_map/ppermute | solution.py:18
  11.6 4.6 %collective-permute-start.2 = (s32[512]{0:T(512)S(1)}, s32[512]{0:T(512)S(1)}, u32[]{:S(2)}, u32[]{:S(2)}) collective-permute-start(s32[512]{0:T(512)S(1)} %pad_add_fusion.1), channel_id=1, source_target_pairs={{0,8},{2,10},{4,12},{6,14},{8,0},{10,2},{12,4},{14,6},{16,24},{18,... | collective-permute-start | bytes 6152 | tf_op jit(solution)/shard_map/ppermute | solution.py:18
  13.3 5.6 %copy-start.1 = (s32[8192]{0:T(1024)S(1)}, s32[8192]{0:T(1024)}, u32[]{:S(2)}) copy-start(s32[8192]{0:T(1024)} %param.5) | copy-start | bytes 98308
  13.3 5.6 %copy-start.3 = (s32[64]{0:T(128)S(1)}, s32[64]{0:T(128)}, u32[]{:S(2)}) copy-start(s32[64]{0:T(128)} %mask_ref.7) | copy-start | bytes 772
  16.2 7.4 %collective-permute-start.3 = (s32[1024]{0:T(1024)S(1)}, s32[1024]{0:T(1024)S(1)}, u32[]{:S(2)}, u32[]{:S(2)}) collective-permute-start(s32[1024]{0:T(1024)S(1)} %pad_add_fusion), channel_id=1, source_target_pairs={{0,16},{2,18},{4,20},{6,22},{8,24},{10,26},{12,28},{14,30},{16,0},... | collective-permute-start | bytes 12296 | tf_op jit(solution)/shard_map/ppermute | solution.py:18
  26.5 3.7 %collective-permute-start.4 = (f32[512,256]{1,0:T(8,128)S(1)}, f32[512,256]{1,0:T(8,128)S(1)}, u32[]{:S(2)}, u32[]{:S(2)}) collective-permute-start(f32[512,256]{1,0:T(8,128)S(1)} %get-tuple-element.31), channel_id=1, source_target_pairs={{0,2},{2,0},{4,6},{6,4},{8,10},{10,8},{12,14},{14,12},{16,18},{18,... | collective-permute-start | bytes 1572872 | tf_op jit(solution)/shard_map/ppermute | solution.py:18
  29.7 2.1 %collective-permute-start.8 = (f32[512,256]{1,0:T(8,128)S(1)}, f32[512,256]{1,0:T(8,128)S(1)}, u32[]{:S(2)}, u32[]{:S(2)}) collective-permute-start(f32[512,256]{1,0:T(8,128)S(1)} %get-tuple-element.33), channel_id=1, source_target_pairs={{0,2},{2,0},{4,6},{6,4},{8,10},{10,8},{12,14},{14,12},{16,18},{18,... | collective-permute-start | bytes 1572872 | tf_op jit(solution)/shard_map/ppermute | solution.py:18
  30.4 8.3 %collective-permute-start.5 = (f32[256,256]{1,0:T(8,128)S(1)}, f32[256,256]{1,0:T(8,128)S(1)}, u32[]{:S(2)}, u32[]{:S(2)}) collective-permute-start(f32[256,256]{1,0:T(8,128)S(1)} %slice.57), channel_id=1, source_target_pairs={{0,4},{2,6},{4,0},{6,2},{8,12},{10,14},{12,8},{14,10},{16,20},{18,... | collective-permute-start | bytes 786440 | tf_op jit(solution)/shard_map/ppermute | solution.py:18
  31.9 8.7 %collective-permute-start.9 = (f32[256,256]{1,0:T(8,128)S(1)}, f32[256,256]{1,0:T(8,128)S(1)}, u32[]{:S(2)}, u32[]{:S(2)}) collective-permute-start(f32[256,256]{1,0:T(8,128)S(1)} %slice.63), channel_id=1, source_target_pairs={{0,8},{2,10},{4,12},{6,14},{8,0},{10,2},{12,4},{14,6},{16,24},{18,... | collective-permute-start | bytes 786440 | tf_op jit(solution)/shard_map/ppermute | solution.py:18
  38.7 5.0 %collective-permute-start.6 = (f32[128,256]{1,0:T(8,128)S(1)}, f32[128,256]{1,0:T(8,128)S(1)}, u32[]{:S(2)}, u32[]{:S(2)}) collective-permute-start(f32[128,256]{1,0:T(8,128)S(1)} %slice.59), channel_id=1, source_target_pairs={{0,8},{2,10},{4,12},{6,14},{8,0},{10,2},{12,4},{14,6},{16,24},{18,... | collective-permute-start | bytes 393224 | tf_op jit(solution)/shard_map/ppermute | solution.py:18
  40.6 5.0 %collective-permute-start.10 = (f32[128,256]{1,0:T(8,128)S(1)}, f32[128,256]{1,0:T(8,128)S(1)}, u32[]{:S(2)}, u32[]{:S(2)}) collective-permute-start(f32[128,256]{1,0:T(8,128)S(1)} %slice.65), channel_id=1, source_target_pairs={{0,4},{2,6},{4,0},{6,2},{8,12},{10,14},{12,8},{14,10},{16,20},{18,... | collective-permute-start | bytes 393224 | tf_op jit(solution)/shard_map/ppermute | solution.py:18
  43.8 7.4 %collective-permute-start.7 = (f32[64,256]{1,0:T(8,128)S(1)}, f32[64,256]{1,0:T(8,128)S(1)}, u32[]{:S(2)}, u32[]{:S(2)}) collective-permute-start(f32[64,256]{1,0:T(8,128)S(1)} %slice.61), channel_id=1, source_target_pairs={{0,16},{2,18},{4,20},{6,22},{8,24},{10,26},{12,28},{14,30},{16,0},... | collective-permute-start | bytes 196616 | tf_op jit(solution)/shard_map/ppermute | solution.py:18
  45.7 7.1 %collective-permute-start.11 = (f32[64,256]{1,0:T(8,128)S(1)}, f32[64,256]{1,0:T(8,128)S(1)}, u32[]{:S(2)}, u32[]{:S(2)}) collective-permute-start(f32[64,256]{1,0:T(8,128)S(1)} %slice.67), channel_id=1, source_target_pairs={{0,16},{2,18},{4,20},{6,22},{8,24},{10,26},{12,28},{14,30},{16,0},... | collective-permute-start | bytes 196616 | tf_op jit(solution)/shard_map/ppermute | solution.py:18
  51.2 4.3 %collective-permute-start.12 = (f32[64,256]{1,0:T(8,128)S(1)}, f32[64,256]{1,0:T(8,128)S(1)}, u32[]{:S(2)}, u32[]{:S(2)}) collective-permute-start(f32[64,256]{1,0:T(8,128)S(1)} %slice_add_fusion.6.refs_0_), channel_id=1, source_target_pairs={{0,1},{1,0},{2,3},{3,2},{4,5},{5,4},{6,7},{7,6},{8,9},{9,8},{10,11... | collective-permute-start | bytes 196616 | tf_op jit(solution)/shard_map/ppermute | solution.py:365
  52.8 4.3 %collective-permute-start.13 = (f32[64,256]{1,0:T(8,128)S(1)}, f32[64,256]{1,0:T(8,128)S(1)}, u32[]{:S(2)}, u32[]{:S(2)}) collective-permute-start(f32[64,256]{1,0:T(8,128)S(1)} %slice_add_fusion.5.refs_2_), channel_id=1, source_target_pairs={{0,1},{1,0},{2,3},{3,2},{4,5},{5,4},{6,7},{7,6},{8,9},{9,8},{10,11... | collective-permute-start | bytes 196616 | tf_op jit(solution)/shard_map/ppermute | solution.py:365
  57.9 1.7 %collective-permute-start.14 = (f32[2,320,128]{2,1,0:T(8,128)S(1)}, f32[2,320,128]{2,1,0:T(8,128)S(1)}, u32[]{:S(2)}, u32[]{:S(2)}) collective-permute-start(f32[2,320,128]{2,1,0:T(8,128)S(1)} %get-tuple-element.35), channel_id=1, source_target_pairs={{0,2},{2,0},{4,6},{6,4},{8,10},{10,8},{12,14},{14,12},{16,18},{18,... | collective-permute-start | bytes 983048 | tf_op jit(solution)/shard_map/ppermute | solution.py:18
  59.7 6.3 %collective-permute-start.15 = (f32[1,320,128]{2,1,0:T(8,128)S(1)}, f32[1,320,128]{2,1,0:T(8,128)S(1)}, u32[]{:S(2)}, u32[]{:S(2)}) collective-permute-start(f32[1,320,128]{2,1,0:T(8,128)S(1)} %slice.69), channel_id=1, source_target_pairs={{0,4},{2,6},{4,0},{6,2},{8,12},{10,14},{12,8},{14,10},{16,20},{18,... | collective-permute-start | bytes 491528 | tf_op jit(solution)/shard_map/ppermute | solution.py:18
  66.0 5.5 %collective-permute-start.16 = (f32[1,320,128]{2,1,0:T(8,128)S(1)}, f32[1,320,128]{2,1,0:T(8,128)S(1)}, u32[]{:S(2)}, u32[]{:S(2)}) collective-permute-start(f32[1,320,128]{2,1,0:T(8,128)S(1)} %slice_add_fusion.2), channel_id=1, source_target_pairs={{0,8},{2,10},{4,12},{6,14},{8,0},{10,2},{12,4},{14,6},{16,24},{18,... | collective-permute-start | bytes 491528 | tf_op jit(solution)/shard_map/ppermute | solution.py:18
  71.5 9.0 %collective-permute-start.17 = (f32[1,320,128]{2,1,0:T(8,128)S(1)}, f32[1,320,128]{2,1,0:T(8,128)S(1)}, u32[]{:S(2)}, u32[]{:S(2)}) collective-permute-start(f32[1,320,128]{2,1,0:T(8,128)S(1)} %add.46), channel_id=1, source_target_pairs={{0,16},{2,18},{4,20},{6,22},{8,24},{10,26},{12,28},{14,30},{16,0},... | collective-permute-start | bytes 491528 | tf_op jit(solution)/shard_map/ppermute | solution.py:18
  80.5 5.7 %collective-permute-start.18 = (f32[1,320,128]{2,1,0:T(8,128)S(1)}, f32[1,320,128]{2,1,0:T(8,128)S(1)}, u32[]{:S(2)}, u32[]{:S(2)}) collective-permute-start(f32[1,320,128]{2,1,0:T(8,128)S(1)} %add.47), channel_id=1, source_target_pairs={{0,4},{2,6},{4,0},{6,2},{8,12},{10,14},{12,8},{14,10},{16,20},{18,... | collective-permute-start | bytes 491528 | tf_op jit(solution)/shard_map/ppermute | solution.py:18
  86.2 1.7 %collective-permute-start.19 = (f32[2,320,128]{2,1,0:T(8,128)S(1)}, f32[2,320,128]{2,1,0:T(8,128)S(1)}, u32[]{:S(2)}, u32[]{:S(2)}) collective-permute-start(f32[2,320,128]{2,1,0:T(8,128)S(1)} %pad_maximum_fusion.even_ref), channel_id=1, source_target_pairs={{0,2},{2,0},{4,6},{6,4},{8,10},{10,8},{12,14},{14,12},{16,18},{18,... | collective-permute-start | bytes 983048 | tf_op jit(solution)/shard_map/ppermute | solution.py:18
  (1 other events, 0.7 us)

commit v5 on v4

--- a/solution.py
+++ b/solution.py
@@ -11,7 +11,9 @@
 TILE = 256
 LANES = 128
 SUB = 8
+STRIPS = 8
 AHEAD = 3
+MIX_LIMIT = 32
 
 
 def swapped(value, axis, bit):
@@ -41,87 +43,68 @@
     return high, low
 
 
-def mix_kernel(slab_ref, sign_ref, mask_ref, *refs, first, earlier):
+def mix_kernel(mask_ref, slab_ref, sign_ref, *refs, first, earlier):
     joined = refs[:earlier]
-    out_ref, had_ref, buf_ref, bits_ref, flags_ref, sems = refs[earlier:]
-    rows = buf_ref.shape[0]
-    chunks = sems.shape[0] - 2
-    span = rows // chunks
-    per_tile = TILE // LANES
-
-    def fetch(part):
-        return pltpu.make_async_copy(slab_ref.at[pl.ds(first + part * span, span), :],
-                                     buf_ref.at[pl.ds(part * span, span), :], sems.at[part])
-
-    bits_copy = pltpu.make_async_copy(sign_ref, bits_ref, sems.at[chunks])
-    flags_copy = pltpu.make_async_copy(mask_ref, flags_ref, sems.at[chunks + 1])
-    bits_copy.start()
-    flags_copy.start()
-    for part in range(chunks):
-        fetch(part).start()
+    out_ref, had_ref = refs[earlier:]
+    step = joined[0].shape[0] if earlier else out_ref.shape[0]
+    base_out = earlier * step
+    rows = out_ref.shape[0] - base_out
     row = lax.broadcasted_iota(jnp.int32, (TILE, TILE), 0)
     col = lax.broadcasted_iota(jnp.int32, (TILE, TILE), 1)
     had_ref[...] = parity_sign(row & col).astype(jnp.float32).astype(jnp.bfloat16)
-    bits_copy.wait()
-    flags_copy.wait()
-    base_out = out_ref.shape[0] - rows
-    tiles = span // TILE
-    for part in range(chunks):
-        fetch(part).wait()
+    per_tile = TILE // LANES
+    pair = 2
+    for start in range(0, rows // TILE, pair):
         mixed = []
-        for block in range(part * tiles, (part + 1) * tiles):
+        for block in range(start, start + pair):
             signed = []
             for half in range(per_tile):
                 at = first // LANES + block * per_tile + half
-                sign = (2 * bits_ref[at:at + 1, :] - 1) * flags_ref[at]
+                sign = (2 * sign_ref[at:at + 1, :] - 1) * mask_ref[at]
                 sign = sign.astype(jnp.float32).astype(jnp.bfloat16)
                 signed.append(had_ref[:, half * LANES:(half + 1) * LANES] * sign)
             left = jnp.concatenate(signed * 2, axis=1)
-            right = jnp.concatenate(split_two(buf_ref[block * TILE:(block + 1) * TILE, :]), axis=0)
+            part = slab_ref[first + block * TILE:first + (block + 1) * TILE, :]
+            right = jnp.concatenate(split_two(part), axis=0)
             mixed.append(jnp.dot(left, right, preferred_element_type=jnp.float32))
         mixed = butterfly(mixed)
-        for block in range(tiles):
-            at = base_out + (part * tiles + block) * TILE
+        for block in range(pair):
+            at = base_out + (start + block) * TILE
             out_ref[at:at + TILE, :] = mixed[block]
 
-    @pl.loop(0, span // SUB // 4)
-    def _(part):
-        for eighth in range(4):
-            base = pl.multiple_of(part * 4 * SUB, 4 * SUB) + eighth * SUB
-            values = butterfly([out_ref[pl.ds(base_out + base + at * span, SUB), :] for at in range(chunks)])
-            for at in range(chunks):
-                out_ref[pl.ds(base_out + base + at * span, SUB), :] = values[at]
+    span = pair * TILE
+    for part in range(rows // step):
+        @pl.loop(0, span // SUB // 4)
+        def _(batch):
+            for eighth in range(4):
+                base = base_out + part * step + pl.multiple_of(batch * 4 * SUB, 4 * SUB) + eighth * SUB
+                values = butterfly([out_ref[pl.ds(base + at * span, SUB), :] for at in range(step // span)])
+                for at in range(step // span):
+                    out_ref[pl.ds(base + at * span, SUB), :] = values[at]
 
     if earlier:
-        @pl.loop(0, rows // SUB // 8)
-        def _(part):
+        @pl.loop(0, step // SUB // 8)
+        def _(batch):
             for eighth in range(8):
-                base = pl.multiple_of(part * 8 * SUB, 8 * SUB) + eighth * SUB
+                base = pl.multiple_of(batch * 8 * SUB, 8 * SUB) + eighth * SUB
                 values = [ref[pl.ds(base, SUB), :] for ref in joined]
-                values = butterfly(values + [out_ref[pl.ds(base_out + base, SUB), :]])
-                for at in range(earlier + 1):
-                    out_ref[pl.ds(base + at * rows, SUB), :] = values[at]
+                for part in range(rows // step):
+                    values.append(out_ref[pl.ds(base_out + part * step + base, SUB), :])
+                values = butterfly(values)
+                for at, value in enumerate(values):
+                    out_ref[pl.ds(base + at * step, SUB), :] = value
 
 
 def mix_run(slab, sign_bits, block_mask, first, rows, earlier):
-    width = slab.shape[1]
-    chunks = 4
-    flags = block_mask.shape[0]
-    held = rows * (len(earlier) + 1)
+    held = rows + sum(value.shape[0] for value in earlier)
     return pl.pallas_call(
         functools.partial(mix_kernel, first=first, earlier=len(earlier)),
-        in_specs=[pl.BlockSpec(memory_space=pltpu.HBM)] * 3 + [pl.BlockSpec(memory_space=pltpu.VMEM)] * len(earlier),
+        in_specs=[pl.BlockSpec(memory_space=pltpu.SMEM)] + [pl.BlockSpec(memory_space=pltpu.VMEM)] * (2 + len(earlier)),
         out_specs=pl.BlockSpec(memory_space=pltpu.VMEM),
-        out_shape=jax.ShapeDtypeStruct((held, width), jnp.float32),
-        scratch_shapes=[
-            pltpu.VMEM((TILE, TILE), jnp.bfloat16),
-            pltpu.VMEM((rows, width), jnp.float32),
-            pltpu.VMEM((flags, LANES), jnp.int32),
-            pltpu.SMEM((flags,), jnp.int32),
-            pltpu.SemaphoreType.DMA((chunks + 2,)),
-        ],
-        compiler_params=pltpu.CompilerParams(vmem_limit_bytes=(36 if earlier else 50) << 20),
-    )(slab, sign_bits, block_mask, *earlier)
+        out_shape=jax.ShapeDtypeStruct((held, slab.shape[1]), jnp.float32),
+        scratch_shapes=[pltpu.VMEM((TILE, TILE), jnp.bfloat16)],
+        compiler_params=pltpu.CompilerParams(vmem_limit_bytes=MIX_LIMIT << 20),
+    )(block_mask, slab, sign_bits, *earlier)
 
 
 def pick_kernel(pick_ref, mixed_ref, keep_ref, send_ref, *, start, count, order, pick_count, groups, norm_scale):
@@ -158,8 +141,29 @@
     )(picks, mixed)
 
 
-def gram_kernel(*refs, strips, scale, peers):
-    pieces, (keep_ref, send_ref, full_ref, gram_ref) = refs[:-4], refs[-4:]
+def strip_bits(group):
+    return (0, 1, 2) if group == 0 else (0, 2, 1)
+
+
+def block_groups(tiles):
+    pairs = [(i, j) for i in range(tiles) for j in range(i, tiles)]
+    return [pairs[:len(pairs) // 2], pairs[len(pairs) // 2:]]
+
+
+def strip_starts(group, low_bit):
+    height = LANES // STRIPS
+    mine = lax.axis_index("rows") & (STRIPS - 1)
+    order = strip_bits(group)
+    starts = []
+    for slot in range(STRIPS // 2):
+        offset = low_bit | (slot >> 1) << order[1] | (slot & 1) << order[2]
+        starts.append(pl.multiple_of((mine ^ offset) * height, height))
+    return starts
+
+
+def gram_kernel(*refs, scale, peers, groups):
+    outs = 2 * len(groups)
+    pieces, out_refs, (full_ref, gram_ref) = refs[:-outs - 2], refs[-outs - 2:-2], refs[-2:]
     total = full_ref.shape[1]
     width = total // peers
     column = lax.axis_index("cols")
@@ -170,33 +174,30 @@
             first = pl.multiple_of((column ^ peer) * width, width)
             full_ref[at:at + count, pl.ds(first, width)] = pieces[run * peers + peer][...]
         at += count
-    height = LANES // strips
-    mine = lax.axis_index("rows") & (strips - 1)
-    block = 0
     for upper in range(total // LANES):
-        left = full_ref[:, upper * LANES:(upper + 1) * LANES]
-        rows = lax.dot_general(left, full_ref[:, upper * LANES:], (((0,), (0,)), ((), ())),
+        here = slice(upper * LANES, (upper + 1) * LANES)
+        rows = lax.dot_general(full_ref[:, here], full_ref[:, upper * LANES:], (((0,), (0,)), ((), ())),
                                precision=lax.Precision.HIGHEST, preferred_element_type=jnp.float32)
-        gram_ref[:, :total - upper * LANES] = rows * scale
-        for right in range(upper, total // LANES):
-            lane = (right - upper) * LANES
-            for low_bit, out_ref in ((0, keep_ref), (1, send_ref)):
-                for half in range(strips // 2):
-                    strip = pl.multiple_of(((low_bit + 2 * half) ^ mine) * height, height)
-                    out_ref[half, block * height:(block + 1) * height, :] = gram_ref[
-                        pl.ds(strip, height), lane:lane + LANES]
-            block += 1
-
-
-def partial_gram(pieces, rows, peers, strips, scale):
+        gram_ref[here, upper * LANES:] = rows * scale
+    height = LANES // STRIPS
+    for group, pairs in enumerate(groups):
+        for low_bit in range(2):
+            for slot, strip in enumerate(strip_starts(group, low_bit)):
+                for block, (upper, right) in enumerate(pairs):
+                    out_refs[2 * group + low_bit][slot, block * height:(block + 1) * height, :] = gram_ref[
+                        pl.ds(upper * LANES + strip, height), right * LANES:(right + 1) * LANES]
+
+
+def partial_gram(pieces, rows, peers, scale):
     total = pieces[0].shape[1] * peers
-    tiles = total // LANES
-    half = jax.ShapeDtypeStruct(
-        (strips // 2, tiles * (tiles + 1) // 2 * (LANES // strips), LANES), jnp.float32)
+    groups = block_groups(total // LANES)
+    shapes = []
+    for pairs in groups:
+        shapes += [jax.ShapeDtypeStruct((STRIPS // 2, len(pairs) * (LANES // STRIPS), LANES), jnp.float32)] * 2
     return pl.pallas_call(
-        functools.partial(gram_kernel, strips=strips, scale=scale, peers=peers),
-        out_shape=[half, half],
-        scratch_shapes=[pltpu.VMEM((rows, total), jnp.float32), pltpu.VMEM((LANES, total), jnp.float32)],
+        functools.partial(gram_kernel, scale=scale, peers=peers, groups=groups),
+        out_shape=shapes,
+        scratch_shapes=[pltpu.VMEM((rows, total), jnp.float32), pltpu.VMEM((total, total), jnp.float32)],
         compiler_params=pltpu.CompilerParams(vmem_limit_bytes=16 << 20),
     )(*pieces)
 
@@ -283,20 +284,16 @@
     return jnp.where(col >= row, factored[:, :LANES], 0.0), factored[:, LANES:]
 
 
-def factor_kernel(even_ref, odd_ref, out_ref, gram_ref, factor_ref, column_ref, lead_ref, *, strips):
-    total = gram_ref.shape[0]
-    tiles = total // LANES
-    height = LANES // strips
-    mine = lax.axis_index("rows") & (strips - 1)
-    block = 0
-    for upper in range(tiles):
-        for right in range(upper, tiles):
-            for low_bit, in_ref in ((0, even_ref), (1, odd_ref)):
-                for half in range(strips // 2):
-                    strip = pl.multiple_of(((low_bit + 2 * half) ^ mine) * height, height)
-                    gram_ref[pl.ds(upper * LANES + strip, height), right * LANES:(right + 1) * LANES] = in_ref[
-                        half, block * height:(block + 1) * height, :]
-            block += 1
+def factor_kernel(*refs, groups):
+    strip_refs, (out_ref, gram_ref, factor_ref, column_ref, lead_ref) = refs[:-5], refs[-5:]
+    tiles = gram_ref.shape[0] // LANES
+    height = LANES // STRIPS
+    for group, pairs in enumerate(groups):
+        for low_bit in range(2):
+            for slot, strip in enumerate(strip_starts(group, low_bit)):
+                for block, (upper, right) in enumerate(pairs):
+                    gram_ref[pl.ds(upper * LANES + strip, height), right * LANES:(right + 1) * LANES] = strip_refs[
+                        2 * group + low_bit][slot, block * height:(block + 1) * height, :]
     factor_ref[...] = jnp.zeros_like(factor_ref)
     for at in range(tiles):
         here = slice(at * LANES, (at + 1) * LANES)
@@ -312,15 +309,27 @@
     out_ref[...] = factor_ref[:, pl.ds(first, width)]
 
 
-def factor_panel(even, odd, total, width):
-    strips = 2 * even.shape[0]
+def factor_panel(strips, total, width):
     return pl.pallas_call(
-        functools.partial(factor_kernel, strips=strips),
+        functools.partial(factor_kernel, groups=block_groups(total // LANES)),
         out_shape=jax.ShapeDtypeStruct((total, width), jnp.float32),
         scratch_shapes=[pltpu.VMEM((total, total), jnp.float32)] * 2 + [
             pltpu.VMEM((LANES * SUB, LANES), jnp.float32), pltpu.VMEM((2 * LANES, LANES), jnp.float32)],
-        compiler_params=pltpu.CompilerParams(vmem_limit_bytes=48 << 20),
-    )(even, odd)
+        compiler_params=pltpu.CompilerParams(vmem_limit_bytes=16 << 20),
+    )(*strips)
+
+
+def summed_strips(keep, send, group, bits):
+    core, *order = strip_bits(group)
+    gram = keep + swapped(send, "rows", core)
+    for bit in order:
+        half = gram.shape[0] // 2
+        gram = gram[:half] + swapped(gram[half:], "rows", bit)
+    for bit in range(len(order) + 1, bits):
+        gram = gram + swapped(gram, "rows", bit)
+    for bit in reversed(order):
+        gram = jnp.concatenate([gram, swapped(gram, "rows", bit)])
+    return [gram, swapped(gram, "rows", core)]
 
 
 def reduce_run(keep, send, order):
@@ -339,15 +348,17 @@
     pick_count = sample_rows.shape[0]
     signs = sign_bits.reshape(row_count // LANES, LANES)
     picks = sample_rows
-    runs = 4
-    rows = row_count // runs
+    step = row_count // 4
     mixed = []
     source = slab
     for bit in range(bits):
+        run = bit - (bits - 3)
+        if run == 0:
+            picks, signs = lax.optimization_barrier((picks, signs))
         other = swapped(picks, "rows", bit)
-        run = bit - (bits - runs)
         if run >= 0:
-            made = mix_run(source, signs, block_mask, run * rows, rows, mixed if run == runs - 1 else [])
+            last = run == 2
+            made = mix_run(source, signs, block_mask, run * step, 2 * step if last else step, mixed if last else [])
             other, made, source = lax.optimization_barrier((other, made, source))
             mixed.append(made)
         picks = jnp.concatenate([picks, other])
@@ -364,13 +375,11 @@
         for peer in range(1, peers):
             pieces.append(lax.ppermute(part, "cols", [(i, i ^ peer) for i in range(peers)]))
     sketch = jnp.concatenate(sketch)
-    keep, send = partial_gram(pieces, pick_count, peers, 4, 1.0 / (pick_count * groups))
-    gram = keep + swapped(send, "rows", 0)
-    gram = gram[:1] + swapped(gram[1:], "rows", 1)
-    for bit in range(2, bits):
-        gram = gram + swapped(gram, "rows", bit)
-    gram = jnp.concatenate([gram, swapped(gram, "rows", 1)])
-    r_panel = factor_panel(gram, swapped(gram, "rows", 0), panel_width * peers, panel_width)
+    parts = partial_gram(pieces, pick_count, peers, 1.0 / (pick_count * groups))
+    strips = []
+    for group in range(len(parts) // 2):
+        strips += summed_strips(parts[2 * group], parts[2 * group + 1], group, bits)
+    r_panel = factor_panel(strips, panel_width * peers, panel_width)
     return (sketch, r_panel)
 
 

time: 103 us -> 98 us (0.951)
  waiting for transfers between devices: 47.2 us -> 32.6 us
  starting transfers between devices: 16.4 us -> 27.5 us
  Pallas kernels: 34.5 us -> 30.2 us
  local copies, waits for them, and re-layouts: 2.18 us -> 4.91 us
    ppermute x18 -> x26, waiting for transfers between devices: 43.6 us -> 28.9 us  [swapped(): lax.ppermute(value, axis, [(i, i ^ 1 << bit) for i in range(lax.axis_size...]
    ppermute x18 -> x26, starting transfers between devices: 14.1 us -> 25.2 us  [swapped(): lax.ppermute(value, axis, [(i, i ^ 1 << bit) for i in range(lax.axis_size...]
    pallas_call x4 -> x3, Pallas kernels: 13.4 us -> 9.05 us  [mix_run(): pl.pallas_call(functools.partial(mix_kernel, first=first, earlier=len(ear...]
    unnamed x14 -> x9, local copies, waits for them, and re-layouts: 2.1 us -> 4.81 us
  transfers between devices with their start and end apart: 20 -> 28, of which waited for: 14 -> 20; matrix products, arithmetic and copies ran while one was open for 2% -> 1% of each run, Pallas kernels for 16% -> 12%
where the time goes in v5:
time: 98 us; the launch traced here: 97.8 us
  waiting for transfers between devices  32.6 us (33%)
  Pallas kernels  30.2 us (31%)
  starting transfers between devices  27.5 us (28%)
  local copies, waits for them, and re-layouts  4.91 us (5%)
  other arithmetic  1.73 us (2%)
    ppermute x26, waiting for transfers between devices, swapped(): lax.ppermute(value, axis, [(i, i ^ 1 << bit) for i in range(lax.axis_size...  28.9 us
    ppermute x26, starting transfers between devices, swapped(): lax.ppermute(value, axis, [(i, i ^ 1 << bit) for i in range(lax.axis_size...  25.2 us
    pallas_call x1, Pallas kernels, factor_panel(): pl.pallas_call(functools.partial(factor_kernel, groups=block_groups(total...  14.4 us
    pallas_call x3, Pallas kernels, mix_run(): pl.pallas_call(functools.partial(mix_kernel, first=first, earlier=len(ear...  9.05 us
    pallas_call x2, Pallas kernels, pick_rows(): pl.pallas_call(functools.partial(pick_kernel, start=start, count=count, o...  5.99 us
    unnamed x9, local copies, waits for them, and re-layouts  4.81 us
    ppermute x2, waiting for transfers between devices, body(): lax.ppermute(part, 'cols', [(i, i ^ peer) for i in range(peers)])  3.63 us
    ppermute x2, starting transfers between devices, body(): lax.ppermute(part, 'cols', [(i, i ^ peer) for i in range(peers)])  2.28 us
  transfers between devices with their start and end apart: 28, of which 20 were waited for; matrix products, arithmetic and copies ran while one was open for 1% of the time, Pallas kernels for 12%

profile of v5, /device:TPU:0, one launch (start us, length us, event | category | flops | bytes accessed | tf_op | source)
XLA Modules:
  0.0 97.8 jit_solution(10434115919834459521)
XLA Ops:
  2.8 2.8 %collective-permute-start.1 = (s32[256]{0:T(256)S(1)}, s32[256]{0:T(256)S(1)}, u32[]{:S(2)}, u32[]{:S(2)}) collective-permute-start(s32[256]{0:T(256)S(1)} %pad_add_fusion.2), channel_id=1, source_target_pairs={{0,4},{2,6},{4,0},{6,2},{8,12},{10,14},{12,8},{14,10},{16,20},{18,... | collective-permute-start | bytes 3080 | tf_op jit(solution)/shard_map/ppermute | solution.py:20
  5.6 3.4 %copy-done = f32[8192,256]{1,0:T(8,128)S(1)} copy-done((f32[8192,256]{1,0:T(8,128)S(1)}, f32[8192,256]{1,0:T(8,128)}, u32[]{:S(2)}) %copy-start) | copy-done | bytes 8388632
  10.4 2.0 %shard_map.59.refs_0_ = f32[2048,256]{1,0:T(8,128)S(1)} custom-call(s32[64]{0:T(128)S(1)} %copy-done.2, f32[8192,256]{1,0:T(8,128)S(1)} %copy-done, s32[64,128]{1,0:T(8,128)S(1)} %bitcast.1), custom_call_target="tpu_custom_call" | custom-call | tf_op jit(solution)/shard_map/pallas_call | solution.py:100
  12.4 1.6 %collective-permute-start.2 = (s32[512]{0:T(512)S(1)}, s32[512]{0:T(512)S(1)}, u32[]{:S(2)}, u32[]{:S(2)}) collective-permute-start(s32[512]{0:T(512)S(1)} %pad_add_fusion.1), channel_id=1, source_target_pairs={{0,8},{2,10},{4,12},{6,14},{8,0},{10,2},{12,4},{14,6},{16,24},{18,... | collective-permute-start | bytes 6152 | tf_op jit(solution)/shard_map/ppermute | solution.py:20
  14.0 2.0 %shard_map.60.refs_1_ = f32[2048,256]{1,0:T(8,128)S(1)} custom-call(s32[64]{0:T(128)S(1)} %copy-done.2, f32[8192,256]{1,0:T(8,128)S(1)} %copy-done, s32[64,128]{1,0:T(8,128)S(1)} %bitcast.2), custom_call_target="tpu_custom_call" | custom-call | tf_op jit(solution)/shard_map/pallas_call | solution.py:100
  16.1 2.7 %collective-permute-start.3 = (s32[1024]{0:T(1024)S(1)}, s32[1024]{0:T(1024)S(1)}, u32[]{:S(2)}, u32[]{:S(2)}) collective-permute-start(s32[1024]{0:T(1024)S(1)} %pad_add_fusion), channel_id=1, source_target_pairs={{0,16},{2,18},{4,20},{6,22},{8,24},{10,26},{12,28},{14,30},{16,0},... | collective-permute-start | bytes 12296 | tf_op jit(solution)/shard_map/ppermute | solution.py:20
  18.7 5.1 %shard_map.61.mixed_ref = f32[8192,256]{1,0:T(8,128)S(1)} custom-call(s32[64]{0:T(128)S(1)} %copy-done.2, f32[8192,256]{1,0:T(8,128)S(1)} %copy-done, s32[64,128]{1,0:T(8,128)S(1)} %bitcast.3, f32[2048,256]{1,0:T(8,128)S(1)} %shard_map.59.refs_0_, f32[2048,256]{1,0:T(8,128)S(1)} %shard_map.60.refs_1_), custom_call_target="tpu_custom_call" | custom-call | tf_op jit(solution)/shard_map/pallas_call | solution.py:100
  23.8 2.9 %shard_map.62 = (f32[512,256]{1,0:T(8,128)S(1)}, f32[512,256]{1,0:T(8,128)S(1)}) custom-call(s32[2048]{0:T(1024)S(1)} %constant_dynamic-update-slice_fusion.pick_ref, f32[8192,256]{1,0:T(8,128)S(1)} %shard_map.61.mixed_ref), custom_call_target="tpu_custom_call" | custom-call | tf_op jit(solution)/shard_map/pallas_call | solution.py:134
  26.8 3.1 %shard_map.63 = (f32[512,256]{1,0:T(8,128)S(1)}, f32[512,256]{1,0:T(8,128)S(1)}) custom-call(s32[2048]{0:T(1024)S(1)} %constant_dynamic-update-slice_fusion.pick_ref, f32[8192,256]{1,0:T(8,128)S(1)} %shard_map.61.mixed_ref), custom_call_target="tpu_custom_call" | custom-call | tf_op jit(solution)/shard_map/pallas_call | solution.py:134
  33.7 5.2 %collective-permute-done.5 = f32[256,256]{1,0:T(8,128)S(1)} collective-permute-done((f32[256,256]{1,0:T(8,128)S(1)}, f32[256,256]{1,0:T(8,128)S(1)}, u32[]{:S(2)}, u32[]{:S(2)}) %collective-permute-start.5) | collective-permute-done | bytes 262176 | tf_op jit(solution)/shard_map/ppermute | solution.py:20
  41.4 2.5 %collective-permute-done.6 = f32[128,256]{1,0:T(8,128)S(1)} collective-permute-done((f32[128,256]{1,0:T(8,128)S(1)}, f32[128,256]{1,0:T(8,128)S(1)}, u32[]{:S(2)}, u32[]{:S(2)}) %collective-permute-start.6) | collective-permute-done | bytes 131104 | tf_op jit(solution)/shard_map/ppermute | solution.py:20
  47.1 3.6 %collective-permute-done.7 = f32[64,256]{1,0:T(8,128)S(1)} collective-permute-done((f32[64,256]{1,0:T(8,128)S(1)}, f32[64,256]{1,0:T(8,128)S(1)}, u32[]{:S(2)}, u32[]{:S(2)}) %collective-permute-start.7) | collective-permute-done | bytes 65568 | tf_op jit(solution)/shard_map/ppermute | solution.py:20
  50.6 1.6 %collective-permute-start.12 = (f32[64,256]{1,0:T(8,128)S(1)}, f32[64,256]{1,0:T(8,128)S(1)}, u32[]{:S(2)}, u32[]{:S(2)}) collective-permute-start(f32[64,256]{1,0:T(8,128)S(1)} %slice_add_fusion.7.refs_0_), channel_id=1, source_target_pairs={{0,1},{1,0},{2,3},{3,2},{4,5},{5,4},{6,7},{7,6},{8,9},{9,8},{10,11... | collective-permute-start | bytes 196616 | tf_op jit(solution)/shard_map/ppermute | solution.py:376
  52.9 2.0 %collective-permute-done.12.refs_1_ = f32[64,256]{1,0:T(8,128)S(1)} collective-permute-done((f32[64,256]{1,0:T(8,128)S(1)}, f32[64,256]{1,0:T(8,128)S(1)}, u32[]{:S(2)}, u32[]{:S(2)}) %collective-permute-start.12) | collective-permute-done | bytes 65568 | tf_op jit(solution)/shard_map/ppermute | solution.py:376
  55.0 1.6 %collective-permute-done.13.refs_3_ = f32[64,256]{1,0:T(8,128)S(1)} collective-permute-done((f32[64,256]{1,0:T(8,128)S(1)}, f32[64,256]{1,0:T(8,128)S(1)}, u32[]{:S(2)}, u32[]{:S(2)}) %collective-permute-start.13) | collective-permute-done | bytes 65568 | tf_op jit(solution)/shard_map/ppermute | solution.py:376
  60.1 3.3 %collective-permute-done.22 = f32[2,80,128]{2,1,0:T(8,128)S(1)} collective-permute-done((f32[2,80,128]{2,1,0:T(8,128)S(1)}, f32[2,80,128]{2,1,0:T(8,128)S(1)}, u32[]{:S(2)}, u32[]{:S(2)}) %collective-permute-start.22) | collective-permute-done | bytes 81952 | tf_op jit(solution)/shard_map/ppermute | solution.py:20
  65.6 1.9 %collective-permute-done.23 = f32[1,80,128]{2,1,0:T(8,128)S(1)} collective-permute-done((f32[1,80,128]{2,1,0:T(8,128)S(1)}, f32[1,80,128]{2,1,0:T(8,128)S(1)}, u32[]{:S(2)}, u32[]{:S(2)}) %collective-permute-start.23) | collective-permute-done | bytes 40992 | tf_op jit(solution)/shard_map/ppermute | solution.py:20
  68.1 2.4 %collective-permute-start.17 = (f32[1,80,128]{2,1,0:T(8,128)S(1)}, f32[1,80,128]{2,1,0:T(8,128)S(1)}, u32[]{:S(2)}, u32[]{:S(2)}) collective-permute-start(f32[1,80,128]{2,1,0:T(8,128)S(1)} %slice_add_fusion.9), channel_id=1, source_target_pairs={{0,16},{2,18},{4,20},{6,22},{8,24},{10,26},{12,28},{14,30},{16,0},... | collective-permute-start | bytes 122888 | tf_op jit(solution)/shard_map/ppermute | solution.py:20
  70.5 2.3 %collective-permute-done.24 = f32[1,80,128]{2,1,0:T(8,128)S(1)} collective-permute-done((f32[1,80,128]{2,1,0:T(8,128)S(1)}, f32[1,80,128]{2,1,0:T(8,128)S(1)}, u32[]{:S(2)}, u32[]{:S(2)}) %collective-permute-start.24) | collective-permute-done | bytes 40992 | tf_op jit(solution)/shard_map/ppermute | solution.py:20
  73.4 1.6 %collective-permute-start.18 = (f32[1,80,128]{2,1,0:T(8,128)S(1)}, f32[1,80,128]{2,1,0:T(8,128)S(1)}, u32[]{:S(2)}, u32[]{:S(2)}) collective-permute-start(f32[1,80,128]{2,1,0:T(8,128)S(1)} %add.59), channel_id=1, source_target_pairs={{0,8},{2,10},{4,12},{6,14},{8,0},{10,2},{12,4},{14,6},{16,24},{18,... | collective-permute-start | bytes 122888 | tf_op jit(solution)/shard_map/ppermute | solution.py:20
  75.0 2.3 %collective-permute-done.25 = f32[1,80,128]{2,1,0:T(8,128)S(1)} collective-permute-done((f32[1,80,128]{2,1,0:T(8,128)S(1)}, f32[1,80,128]{2,1,0:T(8,128)S(1)}, u32[]{:S(2)}, u32[]{:S(2)}) %collective-permute-start.25) | collective-permute-done | bytes 40992 | tf_op jit(solution)/shard_map/ppermute | solution.py:20
  77.5 1.7 %collective-permute-start.19 = (f32[2,80,128]{2,1,0:T(8,128)S(1)}, f32[2,80,128]{2,1,0:T(8,128)S(1)}, u32[]{:S(2)}, u32[]{:S(2)}) collective-permute-start(f32[2,80,128]{2,1,0:T(8,128)S(1)} %pad_maximum_fusion.3), channel_id=1, source_target_pairs={{0,4},{2,6},{4,0},{6,2},{8,12},{10,14},{12,8},{14,10},{16,20},{18,... | collective-permute-start | bytes 245768 | tf_op jit(solution)/shard_map/ppermute | solution.py:20
  79.1 2.6 %collective-permute-done.26 = f32[2,80,128]{2,1,0:T(8,128)S(1)} collective-permute-done((f32[2,80,128]{2,1,0:T(8,128)S(1)}, f32[2,80,128]{2,1,0:T(8,128)S(1)}, u32[]{:S(2)}, u32[]{:S(2)}) %collective-permute-start.26) | collective-permute-done | bytes 81952 | tf_op jit(solution)/shard_map/ppermute | solution.py:20
  83.4 14.4 %shard_map.65 = f32[512,256]{1,0:T(8,128)} custom-call(f32[4,80,128]{2,1,0:T(8,128)S(1)} %pad_maximum_fusion.refs_0_, f32[4,80,128]{2,1,0:T(8,128)S(1)} %collective-permute-done.20.refs_1_, f32[4,80,128]{2,1,0:T(8,128)S(1)} %pad_maximum_fusion.1.refs_2_, f32[4,80,128]{2,1,0:T(8,128)S(1)} %collective-permute-done.27.refs_3_), custom_call_target="tpu_custom_call" | custom-call | tf_op jit(solution)/shard_map/pallas_call | solution.py:313
  (84 shorter events, 22.4 us)
Async XLA Ops:
  2.8 9.6 %collective-permute-start.1 = (s32[256]{0:T(256)S(1)}, s32[256]{0:T(256)S(1)}, u32[]{:S(2)}, u32[]{:S(2)}) collective-permute-start(s32[256]{0:T(256)S(1)} %pad_add_fusion.2), channel_id=1, source_target_pairs={{0,4},{2,6},{4,0},{6,2},{8,12},{10,14},{12,8},{14,10},{16,20},{18,... | collective-permute-start | bytes 3080 | tf_op jit(solution)/shard_map/ppermute | solution.py:20
  12.4 3.7 %collective-permute-start.2 = (s32[512]{0:T(512)S(1)}, s32[512]{0:T(512)S(1)}, u32[]{:S(2)}, u32[]{:S(2)}) collective-permute-start(s32[512]{0:T(512)S(1)} %pad_add_fusion.1), channel_id=1, source_target_pairs={{0,8},{2,10},{4,12},{6,14},{8,0},{10,2},{12,4},{14,6},{16,24},{18,... | collective-permute-start | bytes 6152 | tf_op jit(solution)/shard_map/ppermute | solution.py:20
  16.1 7.7 %collective-permute-start.3 = (s32[1024]{0:T(1024)S(1)}, s32[1024]{0:T(1024)S(1)}, u32[]{:S(2)}, u32[]{:S(2)}) collective-permute-start(s32[1024]{0:T(1024)S(1)} %pad_add_fusion), channel_id=1, source_target_pairs={{0,16},{2,18},{4,20},{6,22},{8,24},{10,26},{12,28},{14,30},{16,0},... | collective-permute-start | bytes 12296 | tf_op jit(solution)/shard_map/ppermute | solution.py:20
  26.7 3.7 %collective-permute-start.4 = (f32[512,256]{1,0:T(8,128)S(1)}, f32[512,256]{1,0:T(8,128)S(1)}, u32[]{:S(2)}, u32[]{:S(2)}) collective-permute-start(f32[512,256]{1,0:T(8,128)S(1)} %get-tuple-element.31), channel_id=1, source_target_pairs={{0,2},{2,0},{4,6},{6,4},{8,10},{10,8},{12,14},{14,12},{16,18},{18,... | collective-permute-start | bytes 1572872 | tf_op jit(solution)/shard_map/ppermute | solution.py:20
  29.9 2.1 %collective-permute-start.8 = (f32[512,256]{1,0:T(8,128)S(1)}, f32[512,256]{1,0:T(8,128)S(1)}, u32[]{:S(2)}, u32[]{:S(2)}) collective-permute-start(f32[512,256]{1,0:T(8,128)S(1)} %get-tuple-element.33), channel_id=1, source_target_pairs={{0,2},{2,0},{4,6},{6,4},{8,10},{10,8},{12,14},{14,12},{16,18},{18,... | collective-permute-start | bytes 1572872 | tf_op jit(solution)/shard_map/ppermute | solution.py:20
  30.5 8.3 %collective-permute-start.5 = (f32[256,256]{1,0:T(8,128)S(1)}, f32[256,256]{1,0:T(8,128)S(1)}, u32[]{:S(2)}, u32[]{:S(2)}) collective-permute-start(f32[256,256]{1,0:T(8,128)S(1)} %slice.81), channel_id=1, source_target_pairs={{0,4},{2,6},{4,0},{6,2},{8,12},{10,14},{12,8},{14,10},{16,20},{18,... | collective-permute-start | bytes 786440 | tf_op jit(solution)/shard_map/ppermute | solution.py:20
  32.1 8.7 %collective-permute-start.9 = (f32[256,256]{1,0:T(8,128)S(1)}, f32[256,256]{1,0:T(8,128)S(1)}, u32[]{:S(2)}, u32[]{:S(2)}) collective-permute-start(f32[256,256]{1,0:T(8,128)S(1)} %slice.87), channel_id=1, source_target_pairs={{0,8},{2,10},{4,12},{6,14},{8,0},{10,2},{12,4},{14,6},{16,24},{18,... | collective-permute-start | bytes 786440 | tf_op jit(solution)/shard_map/ppermute | solution.py:20
  38.9 5.0 %collective-permute-start.6 = (f32[128,256]{1,0:T(8,128)S(1)}, f32[128,256]{1,0:T(8,128)S(1)}, u32[]{:S(2)}, u32[]{:S(2)}) collective-permute-start(f32[128,256]{1,0:T(8,128)S(1)} %slice.83), channel_id=1, source_target_pairs={{0,8},{2,10},{4,12},{6,14},{8,0},{10,2},{12,4},{14,6},{16,24},{18,... | collective-permute-start | bytes 393224 | tf_op jit(solution)/shard_map/ppermute | solution.py:20
  40.8 5.0 %collective-permute-start.10 = (f32[128,256]{1,0:T(8,128)S(1)}, f32[128,256]{1,0:T(8,128)S(1)}, u32[]{:S(2)}, u32[]{:S(2)}) collective-permute-start(f32[128,256]{1,0:T(8,128)S(1)} %slice.89), channel_id=1, source_target_pairs={{0,4},{2,6},{4,0},{6,2},{8,12},{10,14},{12,8},{14,10},{16,20},{18,... | collective-permute-start | bytes 393224 | tf_op jit(solution)/shard_map/ppermute | solution.py:20
  44.0 6.7 %collective-permute-start.7 = (f32[64,256]{1,0:T(8,128)S(1)}, f32[64,256]{1,0:T(8,128)S(1)}, u32[]{:S(2)}, u32[]{:S(2)}) collective-permute-start(f32[64,256]{1,0:T(8,128)S(1)} %slice.85), channel_id=1, source_target_pairs={{0,16},{2,18},{4,20},{6,22},{8,24},{10,26},{12,28},{14,30},{16,0},... | collective-permute-start | bytes 196616 | tf_op jit(solution)/shard_map/ppermute | solution.py:20
  45.9 6.4 %collective-permute-start.11 = (f32[64,256]{1,0:T(8,128)S(1)}, f32[64,256]{1,0:T(8,128)S(1)}, u32[]{:S(2)}, u32[]{:S(2)}) collective-permute-start(f32[64,256]{1,0:T(8,128)S(1)} %slice.91), channel_id=1, source_target_pairs={{0,16},{2,18},{4,20},{6,22},{8,24},{10,26},{12,28},{14,30},{16,0},... | collective-permute-start | bytes 196616 | tf_op jit(solution)/shard_map/ppermute | solution.py:20
  50.6 4.3 %collective-permute-start.12 = (f32[64,256]{1,0:T(8,128)S(1)}, f32[64,256]{1,0:T(8,128)S(1)}, u32[]{:S(2)}, u32[]{:S(2)}) collective-permute-start(f32[64,256]{1,0:T(8,128)S(1)} %slice_add_fusion.7.refs_0_), channel_id=1, source_target_pairs={{0,1},{1,0},{2,3},{3,2},{4,5},{5,4},{6,7},{7,6},{8,9},{9,8},{10,11... | collective-permute-start | bytes 196616 | tf_op jit(solution)/shard_map/ppermute | solution.py:376
  52.2 4.3 %collective-permute-start.13 = (f32[64,256]{1,0:T(8,128)S(1)}, f32[64,256]{1,0:T(8,128)S(1)}, u32[]{:S(2)}, u32[]{:S(2)}) collective-permute-start(f32[64,256]{1,0:T(8,128)S(1)} %slice_add_fusion.6.refs_2_), channel_id=1, source_target_pairs={{0,1},{1,0},{2,3},{3,2},{4,5},{5,4},{6,7},{7,6},{8,9},{9,8},{10,11... | collective-permute-start | bytes 196616 | tf_op jit(solution)/shard_map/ppermute | solution.py:376
  57.5 2.0 %collective-permute-start.14 = (f32[4,80,128]{2,1,0:T(8,128)S(1)}, f32[4,80,128]{2,1,0:T(8,128)S(1)}, u32[]{:S(2)}, u32[]{:S(2)}) collective-permute-start(f32[4,80,128]{2,1,0:T(8,128)S(1)} %get-tuple-element.35), channel_id=1, source_target_pairs={{0,2},{2,0},{4,6},{6,4},{8,10},{10,8},{12,14},{14,12},{16,18},{18,... | collective-permute-start | bytes 491528 | tf_op jit(solution)/shard_map/ppermute | solution.py:20
  58.9 4.6 %collective-permute-start.22 = (f32[2,80,128]{2,1,0:T(8,128)S(1)}, f32[2,80,128]{2,1,0:T(8,128)S(1)}, u32[]{:S(2)}, u32[]{:S(2)}) collective-permute-start(f32[2,80,128]{2,1,0:T(8,128)S(1)} %slice.97), channel_id=1, source_target_pairs={{0,8},{2,10},{4,12},{6,14},{8,0},{10,2},{12,4},{14,6},{16,24},{18,... | collective-permute-start | bytes 245768 | tf_op jit(solution)/shard_map/ppermute | solution.py:20
  59.5 4.5 %collective-permute-start.15 = (f32[2,80,128]{2,1,0:T(8,128)S(1)}, f32[2,80,128]{2,1,0:T(8,128)S(1)}, u32[]{:S(2)}, u32[]{:S(2)}) collective-permute-start(f32[2,80,128]{2,1,0:T(8,128)S(1)} %slice.93), channel_id=1, source_target_pairs={{0,4},{2,6},{4,0},{6,2},{8,12},{10,14},{12,8},{14,10},{16,20},{18,... | collective-permute-start | bytes 245768 | tf_op jit(solution)/shard_map/ppermute | solution.py:20
  63.5 4.1 %collective-permute-start.23 = (f32[1,80,128]{2,1,0:T(8,128)S(1)}, f32[1,80,128]{2,1,0:T(8,128)S(1)}, u32[]{:S(2)}, u32[]{:S(2)}) collective-permute-start(f32[1,80,128]{2,1,0:T(8,128)S(1)} %slice.99), channel_id=1, source_target_pairs={{0,4},{2,6},{4,0},{6,2},{8,12},{10,14},{12,8},{14,10},{16,20},{18,... | collective-permute-start | bytes 122888 | tf_op jit(solution)/shard_map/ppermute | solution.py:20
  64.1 4.1 %collective-permute-start.16 = (f32[1,80,128]{2,1,0:T(8,128)S(1)}, f32[1,80,128]{2,1,0:T(8,128)S(1)}, u32[]{:S(2)}, u32[]{:S(2)}) collective-permute-start(f32[1,80,128]{2,1,0:T(8,128)S(1)} %slice.95), channel_id=1, source_target_pairs={{0,8},{2,10},{4,12},{6,14},{8,0},{10,2},{12,4},{14,6},{16,24},{18,... | collective-permute-start | bytes 122888 | tf_op jit(solution)/shard_map/ppermute | solution.py:20
  67.5 5.3 %collective-permute-start.24 = (f32[1,80,128]{2,1,0:T(8,128)S(1)}, f32[1,80,128]{2,1,0:T(8,128)S(1)}, u32[]{:S(2)}, u32[]{:S(2)}) collective-permute-start(f32[1,80,128]{2,1,0:T(8,128)S(1)} %slice_add_fusion.8), channel_id=1, source_target_pairs={{0,16},{2,18},{4,20},{6,22},{8,24},{10,26},{12,28},{14,30},{16,0},... | collective-permute-start | bytes 122888 | tf_op jit(solution)/shard_map/ppermute | solution.py:20
  68.1 5.2 %collective-permute-start.17 = (f32[1,80,128]{2,1,0:T(8,128)S(1)}, f32[1,80,128]{2,1,0:T(8,128)S(1)}, u32[]{:S(2)}, u32[]{:S(2)}) collective-permute-start(f32[1,80,128]{2,1,0:T(8,128)S(1)} %slice_add_fusion.9), channel_id=1, source_target_pairs={{0,16},{2,18},{4,20},{6,22},{8,24},{10,26},{12,28},{14,30},{16,0},... | collective-permute-start | bytes 122888 | tf_op jit(solution)/shard_map/ppermute | solution.py:20
  72.8 4.4 %collective-permute-start.25 = (f32[1,80,128]{2,1,0:T(8,128)S(1)}, f32[1,80,128]{2,1,0:T(8,128)S(1)}, u32[]{:S(2)}, u32[]{:S(2)}) collective-permute-start(f32[1,80,128]{2,1,0:T(8,128)S(1)} %add.63), channel_id=1, source_target_pairs={{0,4},{2,6},{4,0},{6,2},{8,12},{10,14},{12,8},{14,10},{16,20},{18,... | collective-permute-start | bytes 122888 | tf_op jit(solution)/shard_map/ppermute | solution.py:20
  73.4 4.1 %collective-permute-start.18 = (f32[1,80,128]{2,1,0:T(8,128)S(1)}, f32[1,80,128]{2,1,0:T(8,128)S(1)}, u32[]{:S(2)}, u32[]{:S(2)}) collective-permute-start(f32[1,80,128]{2,1,0:T(8,128)S(1)} %add.59), channel_id=1, source_target_pairs={{0,8},{2,10},{4,12},{6,14},{8,0},{10,2},{12,4},{14,6},{16,24},{18,... | collective-permute-start | bytes 122888 | tf_op jit(solution)/shard_map/ppermute | solution.py:20
  77.3 4.4 %collective-permute-start.26 = (f32[2,80,128]{2,1,0:T(8,128)S(1)}, f32[2,80,128]{2,1,0:T(8,128)S(1)}, u32[]{:S(2)}, u32[]{:S(2)}) collective-permute-start(f32[2,80,128]{2,1,0:T(8,128)S(1)} %pad_maximum_fusion.4), channel_id=1, source_target_pairs={{0,8},{2,10},{4,12},{6,14},{8,0},{10,2},{12,4},{14,6},{16,24},{18,... | collective-permute-start | bytes 245768 | tf_op jit(solution)/shard_map/ppermute | solution.py:20
  77.5 4.5 %collective-permute-start.19 = (f32[2,80,128]{2,1,0:T(8,128)S(1)}, f32[2,80,128]{2,1,0:T(8,128)S(1)}, u32[]{:S(2)}, u32[]{:S(2)}) collective-permute-start(f32[2,80,128]{2,1,0:T(8,128)S(1)} %pad_maximum_fusion.3), channel_id=1, source_target_pairs={{0,4},{2,6},{4,0},{6,2},{8,12},{10,14},{12,8},{14,10},{16,20},{18,... | collective-permute-start | bytes 245768 | tf_op jit(solution)/shard_map/ppermute | solution.py:20
  (7 other events, 10.7 us)

commit v6 on v5

--- a/solution.py
+++ b/solution.py
@@ -13,7 +13,7 @@
 SUB = 8
 STRIPS = 8
 AHEAD = 3
-MIX_LIMIT = 32
+FIRST_LIMIT = 40
 
 
 def swapped(value, axis, bit):
@@ -43,68 +43,117 @@
     return high, low
 
 
-def mix_kernel(mask_ref, slab_ref, sign_ref, *refs, first, earlier):
-    joined = refs[:earlier]
-    out_ref, had_ref = refs[earlier:]
-    step = joined[0].shape[0] if earlier else out_ref.shape[0]
-    base_out = earlier * step
-    rows = out_ref.shape[0] - base_out
+def fill_hadamard(had_ref):
     row = lax.broadcasted_iota(jnp.int32, (TILE, TILE), 0)
     col = lax.broadcasted_iota(jnp.int32, (TILE, TILE), 1)
     had_ref[...] = parity_sign(row & col).astype(jnp.float32).astype(jnp.bfloat16)
+
+
+def mix_tiles(source_ref, sign_ref, had_ref, out_ref, source_at, sign_at, out_at, count):
     per_tile = TILE // LANES
+    mixed = []
+    for block in range(count):
+        signed = []
+        for half in range(per_tile):
+            at = sign_at // LANES + block * per_tile + half
+            sign = sign_ref[at:at + 1, :].astype(jnp.bfloat16)
+            signed.append(had_ref[:, half * LANES:(half + 1) * LANES] * sign)
+        left = jnp.concatenate(signed * 2, axis=1)
+        part = source_ref[source_at + block * TILE:source_at + (block + 1) * TILE, :]
+        right = jnp.concatenate(split_two(part), axis=0)
+        mixed.append(jnp.dot(left, right, preferred_element_type=jnp.float32))
+    mixed = butterfly(mixed)
+    for block in range(count):
+        at = out_at + block * TILE
+        out_ref[at:at + TILE, :] = mixed[block]
+
+
+def join_runs(refs, starts, out_ref, out_starts, rows, unroll):
+    @pl.loop(0, rows // (SUB * unroll))
+    def _(batch):
+        for sub in range(unroll):
+            base = pl.multiple_of(batch * SUB * unroll, SUB * unroll) + sub * SUB
+            values = butterfly([ref[pl.ds(start + base, SUB), :] for ref, start in zip(refs, starts)])
+            for start, value in zip(out_starts, values):
+                out_ref[pl.ds(start + base, SUB), :] = value
+
+
+def mix_first_kernel(slab_ref, sign_ref, out_ref, rest_ref, had_ref, buf_ref, sems, *, quarter):
     pair = 2
-    for start in range(0, rows // TILE, pair):
-        mixed = []
-        for block in range(start, start + pair):
-            signed = []
-            for half in range(per_tile):
-                at = first // LANES + block * per_tile + half
-                sign = (2 * sign_ref[at:at + 1, :] - 1) * mask_ref[at]
-                sign = sign.astype(jnp.float32).astype(jnp.bfloat16)
-                signed.append(had_ref[:, half * LANES:(half + 1) * LANES] * sign)
-            left = jnp.concatenate(signed * 2, axis=1)
-            part = slab_ref[first + block * TILE:first + (block + 1) * TILE, :]
-            right = jnp.concatenate(split_two(part), axis=0)
-            mixed.append(jnp.dot(left, right, preferred_element_type=jnp.float32))
-        mixed = butterfly(mixed)
-        for block in range(pair):
-            at = base_out + (start + block) * TILE
-            out_ref[at:at + TILE, :] = mixed[block]
-
     span = pair * TILE
-    for part in range(rows // step):
-        @pl.loop(0, span // SUB // 4)
-        def _(batch):
-            for eighth in range(4):
-                base = base_out + part * step + pl.multiple_of(batch * 4 * SUB, 4 * SUB) + eighth * SUB
-                values = butterfly([out_ref[pl.ds(base + at * span, SUB), :] for at in range(step // span)])
-                for at in range(step // span):
-                    out_ref[pl.ds(base + at * span, SUB), :] = values[at]
-
+    chunks = quarter // span
+
+    def fetch(part):
+        rows = pl.ds(part * span, span)
+        if part < 2 * chunks:
+            target = buf_ref.at[rows, :]
+        else:
+            target = rest_ref.at[pl.ds((part - 2 * chunks) * span, span), :]
+        return pltpu.make_async_copy(slab_ref.at[rows, :], target, sems.at[part])
+
+    for part in range(4 * chunks):
+        fetch(part).start()
+    fill_hadamard(had_ref)
+    for half in range(2):
+        for part in range(half * chunks, (half + 1) * chunks):
+            fetch(part).wait()
+            mix_tiles(buf_ref, sign_ref, had_ref, out_ref, part * span, part * span, part * span, pair)
+        starts = [half * quarter + at * span for at in range(chunks)]
+        join_runs([out_ref] * chunks, starts, out_ref, starts, span, 4)
+    for part in range(2 * chunks, 4 * chunks):
+        fetch(part).wait()
+
+
+def mix_next_kernel(rest_ref, sign_ref, *refs, at, earlier, quarter):
+    joined = refs[:earlier]
+    out_ref, had_ref = refs[earlier:]
+    pair = 2
+    span = pair * TILE
+    chunks = quarter // span
+    base = out_ref.shape[0] - quarter
+    fill_hadamard(had_ref)
+    for part in range(chunks):
+        mix_tiles(rest_ref, sign_ref, had_ref, out_ref, (at - 2) * quarter + part * span,
+                  at * quarter + part * span, base + part * span, pair)
+    starts = [base + part * span for part in range(chunks)]
+    join_runs([out_ref] * chunks, starts, out_ref, starts, span, 4)
     if earlier:
-        @pl.loop(0, step // SUB // 8)
-        def _(batch):
-            for eighth in range(8):
-                base = pl.multiple_of(batch * 8 * SUB, 8 * SUB) + eighth * SUB
-                values = [ref[pl.ds(base, SUB), :] for ref in joined]
-                for part in range(rows // step):
-                    values.append(out_ref[pl.ds(base_out + part * step + base, SUB), :])
-                values = butterfly(values)
-                for at, value in enumerate(values):
-                    out_ref[pl.ds(base + at * step, SUB), :] = value
-
-
-def mix_run(slab, sign_bits, block_mask, first, rows, earlier):
-    held = rows + sum(value.shape[0] for value in earlier)
+        sources, starts = [], []
+        for ref in joined:
+            for start in range(0, ref.shape[0], quarter):
+                sources.append(ref)
+                starts.append(start)
+        join_runs(sources + [out_ref], starts + [base], out_ref, range(0, 4 * quarter, quarter), quarter, 8)
+
+
+def mix_first(slab, signs):
+    rows, width = slab.shape
+    half = jax.ShapeDtypeStruct((rows // 2, width), jnp.float32)
     return pl.pallas_call(
-        functools.partial(mix_kernel, first=first, earlier=len(earlier)),
-        in_specs=[pl.BlockSpec(memory_space=pltpu.SMEM)] + [pl.BlockSpec(memory_space=pltpu.VMEM)] * (2 + len(earlier)),
+        functools.partial(mix_first_kernel, quarter=rows // 4),
+        in_specs=[pl.BlockSpec(memory_space=pltpu.HBM), pl.BlockSpec(memory_space=pltpu.VMEM)],
+        out_specs=[pl.BlockSpec(memory_space=pltpu.VMEM)] * 2,
+        out_shape=[half, half],
+        scratch_shapes=[
+            pltpu.VMEM((TILE, TILE), jnp.bfloat16),
+            pltpu.VMEM(half.shape, jnp.float32),
+            pltpu.SemaphoreType.DMA((rows // (2 * TILE),)),
+        ],
+        compiler_params=pltpu.CompilerParams(vmem_limit_bytes=FIRST_LIMIT << 20),
+    )(slab, signs)
+
+
+def mix_next(rest, signs, at, earlier):
+    quarter = rest.shape[0] // 2
+    held = quarter + sum(value.shape[0] for value in earlier)
+    return pl.pallas_call(
+        functools.partial(mix_next_kernel, at=at, earlier=len(earlier), quarter=quarter),
+        in_specs=[pl.BlockSpec(memory_space=pltpu.VMEM)] * (2 + len(earlier)),
         out_specs=pl.BlockSpec(memory_space=pltpu.VMEM),
-        out_shape=jax.ShapeDtypeStruct((held, slab.shape[1]), jnp.float32),
+        out_shape=jax.ShapeDtypeStruct((held, rest.shape[1]), jnp.float32),
         scratch_shapes=[pltpu.VMEM((TILE, TILE), jnp.bfloat16)],
-        compiler_params=pltpu.CompilerParams(vmem_limit_bytes=MIX_LIMIT << 20),
-    )(block_mask, slab, sign_bits, *earlier)
+        compiler_params=pltpu.CompilerParams(vmem_limit_bytes=32 << 20),
+    )(rest, signs, *earlier)
 
 
 def pick_kernel(pick_ref, mixed_ref, keep_ref, send_ref, *, start, count, order, pick_count, groups, norm_scale):
@@ -346,20 +395,22 @@
     peers = lax.axis_size("cols")
     bits = groups.bit_length() - 1
     pick_count = sample_rows.shape[0]
-    signs = sign_bits.reshape(row_count // LANES, LANES)
+    blocks = block_mask.shape[0]
+    signs = (2 * sign_bits - 1).reshape(blocks, row_count // blocks) * block_mask.reshape(blocks, 1)
+    signs = signs.reshape(row_count // LANES, LANES).astype(jnp.float32)
     picks = sample_rows
-    step = row_count // 4
     mixed = []
-    source = slab
     for bit in range(bits):
         run = bit - (bits - 3)
         if run == 0:
             picks, signs = lax.optimization_barrier((picks, signs))
         other = swapped(picks, "rows", bit)
+        if run == 0:
+            made, rest = mix_first(slab, signs)
+        elif run > 0:
+            made = mix_next(rest, signs, run + 1, mixed if run == 2 else [])
         if run >= 0:
-            last = run == 2
-            made = mix_run(source, signs, block_mask, run * step, 2 * step if last else step, mixed if last else [])
-            other, made, source = lax.optimization_barrier((other, made, source))
+            other, made, rest = lax.optimization_barrier((other, made, rest))
             mixed.append(made)
         picks = jnp.concatenate([picks, other])
     mixed = mixed[-1]

time: 98 us -> 94.7 us (0.966)
  local copies, waits for them, and re-layouts: 4.91 us -> 0.11 us
    unnamed x9 -> x3, local copies, waits for them, and re-layouts: 4.81 us -> 0.01 us
  transfers between devices with their start and end apart: 28 -> 28, of which waited for: 20 -> 20; matrix products, arithmetic and copies ran while one was open for 1% -> 2% of each run, Pallas kernels for 12% -> 13%
where the time goes in v6:
time: 94.7 us; the launch traced here: 94.5 us
  waiting for transfers between devices  32.1 us (34%)
  Pallas kernels  30.5 us (32%)
  starting transfers between devices  28.3 us (30%)
  other arithmetic  2.57 us (3%)
    ppermute x26, waiting for transfers between devices, swapped(): lax.ppermute(value, axis, [(i, i ^ 1 << bit) for i in range(lax.axis_size...  28.5 us
    ppermute x26, starting transfers between devices, swapped(): lax.ppermute(value, axis, [(i, i ^ 1 << bit) for i in range(lax.axis_size...  26 us
    pallas_call x1, Pallas kernels, factor_panel(): pl.pallas_call(functools.partial(factor_kernel, groups=block_groups(total...  14.4 us
    pallas_call x2, Pallas kernels, pick_rows(): pl.pallas_call(functools.partial(pick_kernel, start=start, count=count, o...  5.99 us
    pallas_call x1, Pallas kernels, mix_first(): pl.pallas_call(functools.partial(mix_first_kernel, quarter=rows // 4), in...  4.72 us
    pallas_call x2, Pallas kernels, mix_next(): pl.pallas_call(functools.partial(mix_next_kernel, at=at, earlier=len(earl...  4.61 us
    ppermute x2, waiting for transfers between devices, body(): lax.ppermute(part, 'cols', [(i, i ^ peer) for i in range(peers)])  3.64 us
    ppermute x2, starting transfers between devices, body(): lax.ppermute(part, 'cols', [(i, i ^ peer) for i in range(peers)])  2.28 us
  transfers between devices with their start and end apart: 28, of which 20 were waited for; matrix products, arithmetic and copies ran while one was open for 2% of the time, Pallas kernels for 13%

profile of v6, /device:TPU:0, one launch (start us, length us, event | category | flops | bytes accessed | tf_op | source)
XLA Modules:
  0.0 94.5 jit_solution(12830502434068301976)
XLA Ops:
  2.8 2.8 %collective-permute-start.1 = (s32[256]{0:T(256)S(1)}, s32[256]{0:T(256)S(1)}, u32[]{:S(2)}, u32[]{:S(2)}) collective-permute-start(s32[256]{0:T(256)S(1)} %pad_add_fusion.2), channel_id=1, source_target_pairs={{0,4},{2,6},{4,0},{6,2},{8,12},{10,14},{12,8},{14,10},{16,20},{18,... | collective-permute-start | bytes 3080 | tf_op jit(solution)/shard_map/ppermute | solution.py:20
  5.6 4.7 %shard_map.59 = (f32[4096,256]{1,0:T(8,128)S(1)}, f32[4096,256]{1,0:T(8,128)S(1)}) custom-call(f32[8192,256]{1,0:T(8,128)} %slab_ref.1, f32[64,128]{1,0:T(8,128)S(1)} %fusion.sign_ref), custom_call_target="tpu_custom_call" | custom-call | tf_op jit(solution)/shard_map/pallas_call | solution.py:132
  10.3 1.6 %collective-permute-start.2 = (s32[512]{0:T(512)S(1)}, s32[512]{0:T(512)S(1)}, u32[]{:S(2)}, u32[]{:S(2)}) collective-permute-start(s32[512]{0:T(512)S(1)} %pad_add_fusion.1), channel_id=1, source_target_pairs={{0,8},{2,10},{4,12},{6,14},{8,0},{10,2},{12,4},{14,6},{16,24},{18,... | collective-permute-start | bytes 6152 | tf_op jit(solution)/shard_map/ppermute | solution.py:20
  14.0 2.6 %collective-permute-start.3 = (s32[1024]{0:T(1024)S(1)}, s32[1024]{0:T(1024)S(1)}, u32[]{:S(2)}, u32[]{:S(2)}) collective-permute-start(s32[1024]{0:T(1024)S(1)} %pad_add_fusion), channel_id=1, source_target_pairs={{0,16},{2,18},{4,20},{6,22},{8,24},{10,26},{12,28},{14,30},{16,0},... | collective-permute-start | bytes 12296 | tf_op jit(solution)/shard_map/ppermute | solution.py:20
  16.5 3.2 %shard_map.61.mixed_ref = f32[8192,256]{1,0:T(8,128)S(1)} custom-call(f32[4096,256]{1,0:T(8,128)S(1)} %get-tuple-element.29.rest_ref, f32[64,128]{1,0:T(8,128)S(1)} %fusion.sign_ref, f32[4096,256]{1,0:T(8,128)S(1)} %get-tuple-element.30.refs_0_, f32[2048,256]{1,0:T(8,128)S(1)} %shard_map.60.refs_1_), custom_call_target="tpu_custom_call" | custom-call | tf_op jit(solution)/shard_map/pallas_call | solution.py:149
  19.8 2.9 %shard_map.62 = (f32[512,256]{1,0:T(8,128)S(1)}, f32[512,256]{1,0:T(8,128)S(1)}) custom-call(s32[2048]{0:T(1024)S(1)} %constant_dynamic-update-slice_fusion.pick_ref, f32[8192,256]{1,0:T(8,128)S(1)} %shard_map.61.mixed_ref), custom_call_target="tpu_custom_call" | custom-call | tf_op jit(solution)/shard_map/pallas_call | solution.py:183
  22.8 3.1 %shard_map.63 = (f32[512,256]{1,0:T(8,128)S(1)}, f32[512,256]{1,0:T(8,128)S(1)}) custom-call(s32[2048]{0:T(1024)S(1)} %constant_dynamic-update-slice_fusion.pick_ref, f32[8192,256]{1,0:T(8,128)S(1)} %shard_map.61.mixed_ref), custom_call_target="tpu_custom_call" | custom-call | tf_op jit(solution)/shard_map/pallas_call | solution.py:183
  28.1 1.7 %collective-permute-start.9 = (f32[256,256]{1,0:T(8,128)S(1)}, f32[256,256]{1,0:T(8,128)S(1)}, u32[]{:S(2)}, u32[]{:S(2)}) collective-permute-start(f32[256,256]{1,0:T(8,128)S(1)} %slice.87), channel_id=1, source_target_pairs={{0,8},{2,10},{4,12},{6,14},{8,0},{10,2},{12,4},{14,6},{16,24},{18,... | collective-permute-start | bytes 786440 | tf_op jit(solution)/shard_map/ppermute | solution.py:20
  29.7 5.1 %collective-permute-done.5 = f32[256,256]{1,0:T(8,128)S(1)} collective-permute-done((f32[256,256]{1,0:T(8,128)S(1)}, f32[256,256]{1,0:T(8,128)S(1)}, u32[]{:S(2)}, u32[]{:S(2)}) %collective-permute-start.5) | collective-permute-done | bytes 262176 | tf_op jit(solution)/shard_map/ppermute | solution.py:20
  34.9 1.7 %collective-permute-start.6 = (f32[128,256]{1,0:T(8,128)S(1)}, f32[128,256]{1,0:T(8,128)S(1)}, u32[]{:S(2)}, u32[]{:S(2)}) collective-permute-start(f32[128,256]{1,0:T(8,128)S(1)} %slice.83), channel_id=1, source_target_pairs={{0,8},{2,10},{4,12},{6,14},{8,0},{10,2},{12,4},{14,6},{16,24},{18,... | collective-permute-start | bytes 393224 | tf_op jit(solution)/shard_map/ppermute | solution.py:20
  37.4 2.5 %collective-permute-done.6 = f32[128,256]{1,0:T(8,128)S(1)} collective-permute-done((f32[128,256]{1,0:T(8,128)S(1)}, f32[128,256]{1,0:T(8,128)S(1)}, u32[]{:S(2)}, u32[]{:S(2)}) %collective-permute-start.6) | collective-permute-done | bytes 131104 | tf_op jit(solution)/shard_map/ppermute | solution.py:20
  43.2 3.5 %collective-permute-done.7 = f32[64,256]{1,0:T(8,128)S(1)} collective-permute-done((f32[64,256]{1,0:T(8,128)S(1)}, f32[64,256]{1,0:T(8,128)S(1)}, u32[]{:S(2)}, u32[]{:S(2)}) %collective-permute-start.7) | collective-permute-done | bytes 65568 | tf_op jit(solution)/shard_map/ppermute | solution.py:20
  46.6 1.6 %collective-permute-start.12 = (f32[64,256]{1,0:T(8,128)S(1)}, f32[64,256]{1,0:T(8,128)S(1)}, u32[]{:S(2)}, u32[]{:S(2)}) collective-permute-start(f32[64,256]{1,0:T(8,128)S(1)} %slice_add_fusion.7.refs_0_), channel_id=1, source_target_pairs={{0,1},{1,0},{2,3},{3,2},{4,5},{5,4},{6,7},{7,6},{8,9},{9,8},{10,11... | collective-permute-start | bytes 196616 | tf_op jit(solution)/shard_map/ppermute | solution.py:427
  48.9 2.0 %collective-permute-done.12.refs_1_ = f32[64,256]{1,0:T(8,128)S(1)} collective-permute-done((f32[64,256]{1,0:T(8,128)S(1)}, f32[64,256]{1,0:T(8,128)S(1)}, u32[]{:S(2)}, u32[]{:S(2)}) %collective-permute-start.12) | collective-permute-done | bytes 65568 | tf_op jit(solution)/shard_map/ppermute | solution.py:427
  51.0 1.6 %collective-permute-done.13.refs_3_ = f32[64,256]{1,0:T(8,128)S(1)} collective-permute-done((f32[64,256]{1,0:T(8,128)S(1)}, f32[64,256]{1,0:T(8,128)S(1)}, u32[]{:S(2)}, u32[]{:S(2)}) %collective-permute-start.13) | collective-permute-done | bytes 65568 | tf_op jit(solution)/shard_map/ppermute | solution.py:427
  56.0 3.4 %collective-permute-done.22 = f32[2,80,128]{2,1,0:T(8,128)S(1)} collective-permute-done((f32[2,80,128]{2,1,0:T(8,128)S(1)}, f32[2,80,128]{2,1,0:T(8,128)S(1)}, u32[]{:S(2)}, u32[]{:S(2)}) %collective-permute-start.22) | collective-permute-done | bytes 81952 | tf_op jit(solution)/shard_map/ppermute | solution.py:20
  60.1 1.5 %collective-permute-start.16 = (f32[1,80,128]{2,1,0:T(8,128)S(1)}, f32[1,80,128]{2,1,0:T(8,128)S(1)}, u32[]{:S(2)}, u32[]{:S(2)}) collective-permute-start(f32[1,80,128]{2,1,0:T(8,128)S(1)} %slice.95), channel_id=1, source_target_pairs={{0,8},{2,10},{4,12},{6,14},{8,0},{10,2},{12,4},{14,6},{16,24},{18,... | collective-permute-start | bytes 122888 | tf_op jit(solution)/shard_map/ppermute | solution.py:20
  61.6 1.9 %collective-permute-done.23 = f32[1,80,128]{2,1,0:T(8,128)S(1)} collective-permute-done((f32[1,80,128]{2,1,0:T(8,128)S(1)}, f32[1,80,128]{2,1,0:T(8,128)S(1)}, u32[]{:S(2)}, u32[]{:S(2)}) %collective-permute-start.23) | collective-permute-done | bytes 40992 | tf_op jit(solution)/shard_map/ppermute | solution.py:20
  63.5 1.7 %collective-permute-start.24 = (f32[1,80,128]{2,1,0:T(8,128)S(1)}, f32[1,80,128]{2,1,0:T(8,128)S(1)}, u32[]{:S(2)}, u32[]{:S(2)}) collective-permute-start(f32[1,80,128]{2,1,0:T(8,128)S(1)} %slice_add_fusion.8), channel_id=1, source_target_pairs={{0,16},{2,18},{4,20},{6,22},{8,24},{10,26},{12,28},{14,30},{16,0},... | collective-permute-start | bytes 122888 | tf_op jit(solution)/shard_map/ppermute | solution.py:20
  65.2 1.8 %collective-permute-start.17 = (f32[1,80,128]{2,1,0:T(8,128)S(1)}, f32[1,80,128]{2,1,0:T(8,128)S(1)}, u32[]{:S(2)}, u32[]{:S(2)}) collective-permute-start(f32[1,80,128]{2,1,0:T(8,128)S(1)} %slice_add_fusion.9), channel_id=1, source_target_pairs={{0,16},{2,18},{4,20},{6,22},{8,24},{10,26},{12,28},{14,30},{16,0},... | collective-permute-start | bytes 122888 | tf_op jit(solution)/shard_map/ppermute | solution.py:20
  67.0 2.1 %collective-permute-done.24 = f32[1,80,128]{2,1,0:T(8,128)S(1)} collective-permute-done((f32[1,80,128]{2,1,0:T(8,128)S(1)}, f32[1,80,128]{2,1,0:T(8,128)S(1)}, u32[]{:S(2)}, u32[]{:S(2)}) %collective-permute-start.24) | collective-permute-done | bytes 40992 | tf_op jit(solution)/shard_map/ppermute | solution.py:20
  70.2 1.7 %collective-permute-start.18 = (f32[1,80,128]{2,1,0:T(8,128)S(1)}, f32[1,80,128]{2,1,0:T(8,128)S(1)}, u32[]{:S(2)}, u32[]{:S(2)}) collective-permute-start(f32[1,80,128]{2,1,0:T(8,128)S(1)} %add.60), channel_id=1, source_target_pairs={{0,8},{2,10},{4,12},{6,14},{8,0},{10,2},{12,4},{14,6},{16,24},{18,... | collective-permute-start | bytes 122888 | tf_op jit(solution)/shard_map/ppermute | solution.py:20
  75.3 2.5 %collective-permute-done.26 = f32[2,80,128]{2,1,0:T(8,128)S(1)} collective-permute-done((f32[2,80,128]{2,1,0:T(8,128)S(1)}, f32[2,80,128]{2,1,0:T(8,128)S(1)}, u32[]{:S(2)}, u32[]{:S(2)}) %collective-permute-start.26) | collective-permute-done | bytes 81952 | tf_op jit(solution)/shard_map/ppermute | solution.py:20
  80.1 14.4 %shard_map.65 = f32[512,256]{1,0:T(8,128)} custom-call(f32[4,80,128]{2,1,0:T(8,128)S(1)} %pad_maximum_fusion.refs_0_, f32[4,80,128]{2,1,0:T(8,128)S(1)} %collective-permute-done.20.refs_1_, f32[4,80,128]{2,1,0:T(8,128)S(1)} %pad_maximum_fusion.1.refs_2_, f32[4,80,128]{2,1,0:T(8,128)S(1)} %collective-permute-done.27.refs_3_), custom_call_target="tpu_custom_call" | custom-call | tf_op jit(solution)/shard_map/pallas_call | solution.py:362
  (79 shorter events, 22.0 us)
Async XLA Ops:
  2.8 7.5 %collective-permute-start.1 = (s32[256]{0:T(256)S(1)}, s32[256]{0:T(256)S(1)}, u32[]{:S(2)}, u32[]{:S(2)}) collective-permute-start(s32[256]{0:T(256)S(1)} %pad_add_fusion.2), channel_id=1, source_target_pairs={{0,4},{2,6},{4,0},{6,2},{8,12},{10,14},{12,8},{14,10},{16,20},{18,... | collective-permute-start | bytes 3080 | tf_op jit(solution)/shard_map/ppermute | solution.py:20
  10.3 3.7 %collective-permute-start.2 = (s32[512]{0:T(512)S(1)}, s32[512]{0:T(512)S(1)}, u32[]{:S(2)}, u32[]{:S(2)}) collective-permute-start(s32[512]{0:T(512)S(1)} %pad_add_fusion.1), channel_id=1, source_target_pairs={{0,8},{2,10},{4,12},{6,14},{8,0},{10,2},{12,4},{14,6},{16,24},{18,... | collective-permute-start | bytes 6152 | tf_op jit(solution)/shard_map/ppermute | solution.py:20
  14.0 5.8 %collective-permute-start.3 = (s32[1024]{0:T(1024)S(1)}, s32[1024]{0:T(1024)S(1)}, u32[]{:S(2)}, u32[]{:S(2)}) collective-permute-start(s32[1024]{0:T(1024)S(1)} %pad_add_fusion), channel_id=1, source_target_pairs={{0,16},{2,18},{4,20},{6,22},{8,24},{10,26},{12,28},{14,30},{16,0},... | collective-permute-start | bytes 12296 | tf_op jit(solution)/shard_map/ppermute | solution.py:20
  22.7 3.7 %collective-permute-start.4 = (f32[512,256]{1,0:T(8,128)S(1)}, f32[512,256]{1,0:T(8,128)S(1)}, u32[]{:S(2)}, u32[]{:S(2)}) collective-permute-start(f32[512,256]{1,0:T(8,128)S(1)} %get-tuple-element.35), channel_id=1, source_target_pairs={{0,2},{2,0},{4,6},{6,4},{8,10},{10,8},{12,14},{14,12},{16,18},{18,... | collective-permute-start | bytes 1572872 | tf_op jit(solution)/shard_map/ppermute | solution.py:20
  25.9 2.1 %collective-permute-start.8 = (f32[512,256]{1,0:T(8,128)S(1)}, f32[512,256]{1,0:T(8,128)S(1)}, u32[]{:S(2)}, u32[]{:S(2)}) collective-permute-start(f32[512,256]{1,0:T(8,128)S(1)} %get-tuple-element.37), channel_id=1, source_target_pairs={{0,2},{2,0},{4,6},{6,4},{8,10},{10,8},{12,14},{14,12},{16,18},{18,... | collective-permute-start | bytes 1572872 | tf_op jit(solution)/shard_map/ppermute | solution.py:20
  26.5 8.3 %collective-permute-start.5 = (f32[256,256]{1,0:T(8,128)S(1)}, f32[256,256]{1,0:T(8,128)S(1)}, u32[]{:S(2)}, u32[]{:S(2)}) collective-permute-start(f32[256,256]{1,0:T(8,128)S(1)} %slice.81), channel_id=1, source_target_pairs={{0,4},{2,6},{4,0},{6,2},{8,12},{10,14},{12,8},{14,10},{16,20},{18,... | collective-permute-start | bytes 786440 | tf_op jit(solution)/shard_map/ppermute | solution.py:20
  28.1 8.7 %collective-permute-start.9 = (f32[256,256]{1,0:T(8,128)S(1)}, f32[256,256]{1,0:T(8,128)S(1)}, u32[]{:S(2)}, u32[]{:S(2)}) collective-permute-start(f32[256,256]{1,0:T(8,128)S(1)} %slice.87), channel_id=1, source_target_pairs={{0,8},{2,10},{4,12},{6,14},{8,0},{10,2},{12,4},{14,6},{16,24},{18,... | collective-permute-start | bytes 786440 | tf_op jit(solution)/shard_map/ppermute | solution.py:20
  34.9 5.0 %collective-permute-start.6 = (f32[128,256]{1,0:T(8,128)S(1)}, f32[128,256]{1,0:T(8,128)S(1)}, u32[]{:S(2)}, u32[]{:S(2)}) collective-permute-start(f32[128,256]{1,0:T(8,128)S(1)} %slice.83), channel_id=1, source_target_pairs={{0,8},{2,10},{4,12},{6,14},{8,0},{10,2},{12,4},{14,6},{16,24},{18,... | collective-permute-start | bytes 393224 | tf_op jit(solution)/shard_map/ppermute | solution.py:20
  36.8 5.0 %collective-permute-start.10 = (f32[128,256]{1,0:T(8,128)S(1)}, f32[128,256]{1,0:T(8,128)S(1)}, u32[]{:S(2)}, u32[]{:S(2)}) collective-permute-start(f32[128,256]{1,0:T(8,128)S(1)} %slice.89), channel_id=1, source_target_pairs={{0,4},{2,6},{4,0},{6,2},{8,12},{10,14},{12,8},{14,10},{16,20},{18,... | collective-permute-start | bytes 393224 | tf_op jit(solution)/shard_map/ppermute | solution.py:20
  40.0 6.7 %collective-permute-start.7 = (f32[64,256]{1,0:T(8,128)S(1)}, f32[64,256]{1,0:T(8,128)S(1)}, u32[]{:S(2)}, u32[]{:S(2)}) collective-permute-start(f32[64,256]{1,0:T(8,128)S(1)} %slice.85), channel_id=1, source_target_pairs={{0,16},{2,18},{4,20},{6,22},{8,24},{10,26},{12,28},{14,30},{16,0},... | collective-permute-start | bytes 196616 | tf_op jit(solution)/shard_map/ppermute | solution.py:20
  41.8 6.4 %collective-permute-start.11 = (f32[64,256]{1,0:T(8,128)S(1)}, f32[64,256]{1,0:T(8,128)S(1)}, u32[]{:S(2)}, u32[]{:S(2)}) collective-permute-start(f32[64,256]{1,0:T(8,128)S(1)} %slice.91), channel_id=1, source_target_pairs={{0,16},{2,18},{4,20},{6,22},{8,24},{10,26},{12,28},{14,30},{16,0},... | collective-permute-start | bytes 196616 | tf_op jit(solution)/shard_map/ppermute | solution.py:20
  46.6 4.3 %collective-permute-start.12 = (f32[64,256]{1,0:T(8,128)S(1)}, f32[64,256]{1,0:T(8,128)S(1)}, u32[]{:S(2)}, u32[]{:S(2)}) collective-permute-start(f32[64,256]{1,0:T(8,128)S(1)} %slice_add_fusion.7.refs_0_), channel_id=1, source_target_pairs={{0,1},{1,0},{2,3},{3,2},{4,5},{5,4},{6,7},{7,6},{8,9},{9,8},{10,11... | collective-permute-start | bytes 196616 | tf_op jit(solution)/shard_map/ppermute | solution.py:427
  48.2 4.3 %collective-permute-start.13 = (f32[64,256]{1,0:T(8,128)S(1)}, f32[64,256]{1,0:T(8,128)S(1)}, u32[]{:S(2)}, u32[]{:S(2)}) collective-permute-start(f32[64,256]{1,0:T(8,128)S(1)} %slice_add_fusion.6.refs_2_), channel_id=1, source_target_pairs={{0,1},{1,0},{2,3},{3,2},{4,5},{5,4},{6,7},{7,6},{8,9},{9,8},{10,11... | collective-permute-start | bytes 196616 | tf_op jit(solution)/shard_map/ppermute | solution.py:427
  53.5 1.9 %collective-permute-start.14 = (f32[4,80,128]{2,1,0:T(8,128)S(1)}, f32[4,80,128]{2,1,0:T(8,128)S(1)}, u32[]{:S(2)}, u32[]{:S(2)}) collective-permute-start(f32[4,80,128]{2,1,0:T(8,128)S(1)} %get-tuple-element.39), channel_id=1, source_target_pairs={{0,2},{2,0},{4,6},{6,4},{8,10},{10,8},{12,14},{14,12},{16,18},{18,... | collective-permute-start | bytes 491528 | tf_op jit(solution)/shard_map/ppermute | solution.py:20
  54.9 4.6 %collective-permute-start.22 = (f32[2,80,128]{2,1,0:T(8,128)S(1)}, f32[2,80,128]{2,1,0:T(8,128)S(1)}, u32[]{:S(2)}, u32[]{:S(2)}) collective-permute-start(f32[2,80,128]{2,1,0:T(8,128)S(1)} %slice.97), channel_id=1, source_target_pairs={{0,8},{2,10},{4,12},{6,14},{8,0},{10,2},{12,4},{14,6},{16,24},{18,... | collective-permute-start | bytes 245768 | tf_op jit(solution)/shard_map/ppermute | solution.py:20
  55.4 4.6 %collective-permute-start.15 = (f32[2,80,128]{2,1,0:T(8,128)S(1)}, f32[2,80,128]{2,1,0:T(8,128)S(1)}, u32[]{:S(2)}, u32[]{:S(2)}) collective-permute-start(f32[2,80,128]{2,1,0:T(8,128)S(1)} %slice.93), channel_id=1, source_target_pairs={{0,4},{2,6},{4,0},{6,2},{8,12},{10,14},{12,8},{14,10},{16,20},{18,... | collective-permute-start | bytes 245768 | tf_op jit(solution)/shard_map/ppermute | solution.py:20
  59.5 4.1 %collective-permute-start.23 = (f32[1,80,128]{2,1,0:T(8,128)S(1)}, f32[1,80,128]{2,1,0:T(8,128)S(1)}, u32[]{:S(2)}, u32[]{:S(2)}) collective-permute-start(f32[1,80,128]{2,1,0:T(8,128)S(1)} %slice.99), channel_id=1, source_target_pairs={{0,4},{2,6},{4,0},{6,2},{8,12},{10,14},{12,8},{14,10},{16,20},{18,... | collective-permute-start | bytes 122888 | tf_op jit(solution)/shard_map/ppermute | solution.py:20
  60.1 5.1 %collective-permute-start.16 = (f32[1,80,128]{2,1,0:T(8,128)S(1)}, f32[1,80,128]{2,1,0:T(8,128)S(1)}, u32[]{:S(2)}, u32[]{:S(2)}) collective-permute-start(f32[1,80,128]{2,1,0:T(8,128)S(1)} %slice.95), channel_id=1, source_target_pairs={{0,8},{2,10},{4,12},{6,14},{8,0},{10,2},{12,4},{14,6},{16,24},{18,... | collective-permute-start | bytes 122888 | tf_op jit(solution)/shard_map/ppermute | solution.py:20
  63.5 5.6 %collective-permute-start.24 = (f32[1,80,128]{2,1,0:T(8,128)S(1)}, f32[1,80,128]{2,1,0:T(8,128)S(1)}, u32[]{:S(2)}, u32[]{:S(2)}) collective-permute-start(f32[1,80,128]{2,1,0:T(8,128)S(1)} %slice_add_fusion.8), channel_id=1, source_target_pairs={{0,16},{2,18},{4,20},{6,22},{8,24},{10,26},{12,28},{14,30},{16,0},... | collective-permute-start | bytes 122888 | tf_op jit(solution)/shard_map/ppermute | solution.py:20
  65.2 5.0 %collective-permute-start.17 = (f32[1,80,128]{2,1,0:T(8,128)S(1)}, f32[1,80,128]{2,1,0:T(8,128)S(1)}, u32[]{:S(2)}, u32[]{:S(2)}) collective-permute-start(f32[1,80,128]{2,1,0:T(8,128)S(1)} %slice_add_fusion.9), channel_id=1, source_target_pairs={{0,16},{2,18},{4,20},{6,22},{8,24},{10,26},{12,28},{14,30},{16,0},... | collective-permute-start | bytes 122888 | tf_op jit(solution)/shard_map/ppermute | solution.py:20
  69.2 4.1 %collective-permute-start.25 = (f32[1,80,128]{2,1,0:T(8,128)S(1)}, f32[1,80,128]{2,1,0:T(8,128)S(1)}, u32[]{:S(2)}, u32[]{:S(2)}) collective-permute-start(f32[1,80,128]{2,1,0:T(8,128)S(1)} %add.64), channel_id=1, source_target_pairs={{0,4},{2,6},{4,0},{6,2},{8,12},{10,14},{12,8},{14,10},{16,20},{18,... | collective-permute-start | bytes 122888 | tf_op jit(solution)/shard_map/ppermute | solution.py:20
  70.2 4.0 %collective-permute-start.18 = (f32[1,80,128]{2,1,0:T(8,128)S(1)}, f32[1,80,128]{2,1,0:T(8,128)S(1)}, u32[]{:S(2)}, u32[]{:S(2)}) collective-permute-start(f32[1,80,128]{2,1,0:T(8,128)S(1)} %add.60), channel_id=1, source_target_pairs={{0,8},{2,10},{4,12},{6,14},{8,0},{10,2},{12,4},{14,6},{16,24},{18,... | collective-permute-start | bytes 122888 | tf_op jit(solution)/shard_map/ppermute | solution.py:20
  73.3 4.4 %collective-permute-start.26 = (f32[2,80,128]{2,1,0:T(8,128)S(1)}, f32[2,80,128]{2,1,0:T(8,128)S(1)}, u32[]{:S(2)}, u32[]{:S(2)}) collective-permute-start(f32[2,80,128]{2,1,0:T(8,128)S(1)} %pad_maximum_fusion.4), channel_id=1, source_target_pairs={{0,8},{2,10},{4,12},{6,14},{8,0},{10,2},{12,4},{14,6},{16,24},{18,... | collective-permute-start | bytes 245768 | tf_op jit(solution)/shard_map/ppermute | solution.py:20
  74.2 4.4 %collective-permute-start.19 = (f32[2,80,128]{2,1,0:T(8,128)S(1)}, f32[2,80,128]{2,1,0:T(8,128)S(1)}, u32[]{:S(2)}, u32[]{:S(2)}) collective-permute-start(f32[2,80,128]{2,1,0:T(8,128)S(1)} %pad_maximum_fusion.3), channel_id=1, source_target_pairs={{0,4},{2,6},{4,0},{6,2},{8,12},{10,14},{12,8},{14,10},{16,20},{18,... | collective-permute-start | bytes 245768 | tf_op jit(solution)/shard_map/ppermute | solution.py:20
  (4 other events, 6.1 us)

commit v7 on v6

--- a/solution.py
+++ b/solution.py
@@ -104,26 +104,21 @@
         fetch(part).wait()
 
 
-def mix_next_kernel(rest_ref, sign_ref, *refs, at, earlier, quarter):
-    joined = refs[:earlier]
-    out_ref, had_ref = refs[earlier:]
+def mix_next_kernel(rest_ref, sign_ref, out_ref, had_ref, *, quarter):
     pair = 2
     span = pair * TILE
     chunks = quarter // span
-    base = out_ref.shape[0] - quarter
     fill_hadamard(had_ref)
-    for part in range(chunks):
-        mix_tiles(rest_ref, sign_ref, had_ref, out_ref, (at - 2) * quarter + part * span,
-                  at * quarter + part * span, base + part * span, pair)
-    starts = [base + part * span for part in range(chunks)]
-    join_runs([out_ref] * chunks, starts, out_ref, starts, span, 4)
-    if earlier:
-        sources, starts = [], []
-        for ref in joined:
-            for start in range(0, ref.shape[0], quarter):
-                sources.append(ref)
-                starts.append(start)
-        join_runs(sources + [out_ref], starts + [base], out_ref, range(0, 4 * quarter, quarter), quarter, 8)
+    for half in range(2):
+        for part in range(half * chunks, (half + 1) * chunks):
+            mix_tiles(rest_ref, sign_ref, had_ref, out_ref, part * span, 2 * quarter + part * span, part * span, pair)
+        starts = [half * quarter + part * span for part in range(chunks)]
+        join_runs([out_ref] * chunks, starts, out_ref, starts, span, 4)
+
+
+def join_kernel(low_ref, high_ref, out_ref, *, quarter):
+    join_runs([low_ref, low_ref, high_ref, high_ref], [0, quarter] * 2, out_ref, range(0, 4 * quarter, quarter),
+              quarter, 8)
 
 
 def mix_first(slab, signs):
@@ -143,17 +138,26 @@
     )(slab, signs)
 
 
-def mix_next(rest, signs, at, earlier):
-    quarter = rest.shape[0] // 2
-    held = quarter + sum(value.shape[0] for value in earlier)
-    return pl.pallas_call(
-        functools.partial(mix_next_kernel, at=at, earlier=len(earlier), quarter=quarter),
-        in_specs=[pl.BlockSpec(memory_space=pltpu.VMEM)] * (2 + len(earlier)),
+def mix_next(rest, signs):
+    return pl.pallas_call(
+        functools.partial(mix_next_kernel, quarter=rest.shape[0] // 2),
+        in_specs=[pl.BlockSpec(memory_space=pltpu.VMEM)] * 2,
         out_specs=pl.BlockSpec(memory_space=pltpu.VMEM),
-        out_shape=jax.ShapeDtypeStruct((held, rest.shape[1]), jnp.float32),
+        out_shape=jax.ShapeDtypeStruct(rest.shape, jnp.float32),
         scratch_shapes=[pltpu.VMEM((TILE, TILE), jnp.bfloat16)],
         compiler_params=pltpu.CompilerParams(vmem_limit_bytes=32 << 20),
-    )(rest, signs, *earlier)
+    )(rest, signs)
+
+
+def mix_join(low, high):
+    rows, width = low.shape
+    return pl.pallas_call(
+        functools.partial(join_kernel, quarter=rows // 2),
+        in_specs=[pl.BlockSpec(memory_space=pltpu.VMEM)] * 2,
+        out_specs=pl.BlockSpec(memory_space=pltpu.VMEM),
+        out_shape=jax.ShapeDtypeStruct((2 * rows, width), jnp.float32),
+        compiler_params=pltpu.CompilerParams(vmem_limit_bytes=32 << 20),
+    )(low, high)
 
 
 def pick_kernel(pick_ref, mixed_ref, keep_ref, send_ref, *, start, count, order, pick_count, groups, norm_scale):
@@ -281,7 +285,7 @@
     return jnp.broadcast_to(value[:, lane:lane + 1], (value.shape[0], LANES))
 
 
-def factor_tile(diagonal, column_ref, lead_ref):
+def factor_tile(diagonal, column_ref, lead_ref, below_ref):
     row = lax.broadcasted_iota(jnp.int32, (LANES, LANES), 0)
     col = lax.broadcasted_iota(jnp.int32, (LANES, LANES), 1)
     identity = (row == col).astype(jnp.float32)
@@ -294,16 +298,24 @@
     def widen(value):
         return jnp.concatenate([value, value], axis=1)
 
+    def splats(slab, at):
+        return [lane_splat(tile[slab][:, :LANES], SUB * at + j) for j in range(SUB)]
+
+    own, near = splats(0, 0), splats(1, 0)
     for at in range(slabs):
         lead = tile[at]
         direct = range(at + 1, min(slabs, at + 1 + AHEAD))
         for j in range(SUB):
-            column_ref[(at * SUB + j) * SUB:(at * SUB + j + 1) * SUB, :] = lane_splat(lead[:, :LANES], SUB * at + j)
+            column_ref[(at * SUB + j) * SUB:(at * SUB + j + 1) * SUB, :] = own[j]
         for half in range(2):
             lead_ref[half * LANES + at * SUB:half * LANES + (at + 1) * SUB, :] = lead[:, half * LANES:(half + 1) * LANES]
         pivot = {(i, j): column_ref[pl.ds((at * SUB + j) * SUB + i, SUB, stride=0), :]
                  for j in range(SUB) for i in range(j + 1)}
-        below = [[lane_splat(tile[u][:, :LANES], SUB * at + j) for j in range(SUB)] for u in direct]
+        below = [near if u == at + 1 else splats(u, at) for u in direct]
+        if at + 1 < slabs:
+            own = splats(at + 1, at + 1)
+        if at + 2 < slabs:
+            near = splats(at + 2, at + 1)
         rows = [jnp.concatenate([lead_ref[pl.ds(half * LANES + at * SUB + m, SUB, stride=0), :] for half in range(2)],
                                 axis=1) for m in range(SUB)]
         panel = jnp.zeros_like(lead)
@@ -323,6 +335,14 @@
                 for j in range(m + 1, SUB):
                     column[j] = column[j] - pivot[m, j] * column[m]
                 tile[u] = tile[u] - widen(column[m]) * rows[m]
+            if below:
+                slot = (at * SUB + m) * SUB
+                below_ref[slot:slot + SUB, :] = below[0][m]
+                for j in range(SUB):
+                    spread = below_ref[pl.ds(slot + j, SUB, stride=0), :]
+                    own[j] = own[j] - below[0][m] * spread
+                    if len(below) > 1:
+                        near[j] = near[j] - below[1][m] * spread
         done.append(panel)
         if at + 1 + AHEAD < slabs:
             update = lax.dot_general(left_terms(panel[:, :LANES], 0), right_terms(panel), (((0,), (0,)), ((), ())),
@@ -334,7 +354,7 @@
 
 
 def factor_kernel(*refs, groups):
-    strip_refs, (out_ref, gram_ref, factor_ref, column_ref, lead_ref) = refs[:-5], refs[-5:]
+    strip_refs, (out_ref, gram_ref, factor_ref, column_ref, lead_ref, below_ref) = refs[:-6], refs[-6:]
     tiles = gram_ref.shape[0] // LANES
     height = LANES // STRIPS
     for group, pairs in enumerate(groups):
@@ -346,7 +366,7 @@
     factor_ref[...] = jnp.zeros_like(factor_ref)
     for at in range(tiles):
         here = slice(at * LANES, (at + 1) * LANES)
-        factor, inverse = factor_tile(gram_ref[here, here], column_ref, lead_ref)
+        factor, inverse = factor_tile(gram_ref[here, here], column_ref, lead_ref, below_ref)
         factor_ref[here, here] = factor
         if at < tiles - 1:
             rest = (at + 1) * LANES
@@ -363,7 +383,8 @@
         functools.partial(factor_kernel, groups=block_groups(total // LANES)),
         out_shape=jax.ShapeDtypeStruct((total, width), jnp.float32),
         scratch_shapes=[pltpu.VMEM((total, total), jnp.float32)] * 2 + [
-            pltpu.VMEM((LANES * SUB, LANES), jnp.float32), pltpu.VMEM((2 * LANES, LANES), jnp.float32)],
+            pltpu.VMEM((LANES * SUB, LANES), jnp.float32), pltpu.VMEM((2 * LANES, LANES), jnp.float32),
+            pltpu.VMEM((LANES * SUB, LANES), jnp.float32)],
         compiler_params=pltpu.CompilerParams(vmem_limit_bytes=16 << 20),
     )(*strips)
 
@@ -399,21 +420,21 @@
     signs = (2 * sign_bits - 1).reshape(blocks, row_count // blocks) * block_mask.reshape(blocks, 1)
     signs = signs.reshape(row_count // LANES, LANES).astype(jnp.float32)
     picks = sample_rows
-    mixed = []
     for bit in range(bits):
         run = bit - (bits - 3)
         if run == 0:
             picks, signs = lax.optimization_barrier((picks, signs))
         other = swapped(picks, "rows", bit)
         if run == 0:
-            made, rest = mix_first(slab, signs)
-        elif run > 0:
-            made = mix_next(rest, signs, run + 1, mixed if run == 2 else [])
-        if run >= 0:
-            other, made, rest = lax.optimization_barrier((other, made, rest))
-            mixed.append(made)
+            low, rest = mix_first(slab, signs)
+            other, low, rest = lax.optimization_barrier((other, low, rest))
+        elif run == 1:
+            high = mix_next(rest, signs)
+            other, low, high = lax.optimization_barrier((other, low, high))
+        elif run == 2:
+            mixed = mix_join(low, high)
+            other, mixed = lax.optimization_barrier((other, mixed))
         picks = jnp.concatenate([picks, other])
-    mixed = mixed[-1]
     first = pick_count // 2
     cross = list(range(1, bits))
     sketch = []

time: 94.7 us -> 92.9 us (0.981)
  Pallas kernels: 30.5 us -> 28.8 us
    pallas_call x1, Pallas kernels: 14.4 us -> 13.1 us  [factor_panel(): pl.pallas_call(functools.partial(factor_kernel, groups=block_groups(total...]
  transfers between devices with their start and end apart: 28 -> 28, of which waited for: 20 -> 21; matrix products, arithmetic and copies ran while one was open for 2% -> 2% of each run, Pallas kernels for 13% -> 13%
where the time goes in v7:
time: 92.9 us; the launch traced here: 92.7 us
  waiting for transfers between devices  31.3 us (34%)
  starting transfers between devices  29 us (31%)
  Pallas kernels  28.8 us (31%)
  other arithmetic  2.57 us (3%)
    ppermute x26, waiting for transfers between devices, swapped(): lax.ppermute(value, axis, [(i, i ^ 1 << bit) for i in range(lax.axis_size...  28.5 us
    ppermute x26, starting transfers between devices, swapped(): lax.ppermute(value, axis, [(i, i ^ 1 << bit) for i in range(lax.axis_size...  25.9 us
    pallas_call x1, Pallas kernels, factor_panel(): pl.pallas_call(functools.partial(factor_kernel, groups=block_groups(total...  13.1 us
    pallas_call x2, Pallas kernels, pick_rows(): pl.pallas_call(functools.partial(pick_kernel, start=start, count=count, o...  5.99 us
    pallas_call x1, Pallas kernels, mix_first(): pl.pallas_call(functools.partial(mix_first_kernel, quarter=rows // 4), in...  4.72 us
    ppermute x2, starting transfers between devices, body(): lax.ppermute(part, 'cols', [(i, i ^ peer) for i in range(peers)])  3.15 us
    ppermute x2, waiting for transfers between devices, body(): lax.ppermute(part, 'cols', [(i, i ^ peer) for i in range(peers)])  2.77 us
    pallas_call x1, Pallas kernels, mix_next(): pl.pallas_call(functools.partial(mix_next_kernel, quarter=rest.shape[0] /...  2.69 us
  transfers between devices with their start and end apart: 28, of which 21 were waited for; matrix products, arithmetic and copies ran while one was open for 2% of the time, Pallas kernels for 13%

profile of v7, /device:TPU:0, one launch (start us, length us, event | category | flops | bytes accessed | tf_op | source)
XLA Modules:
  0.0 92.7 jit_solution(9363676874491108119)
XLA Ops:
  2.8 2.8 %collective-permute-start.1 = (s32[256]{0:T(256)S(1)}, s32[256]{0:T(256)S(1)}, u32[]{:S(2)}, u32[]{:S(2)}) collective-permute-start(s32[256]{0:T(256)S(1)} %pad_add_fusion.2), channel_id=1, source_target_pairs={{0,4},{2,6},{4,0},{6,2},{8,12},{10,14},{12,8},{14,10},{16,20},{18,... | collective-permute-start | bytes 3080 | tf_op jit(solution)/shard_map/ppermute | solution.py:20
  5.6 4.7 %shard_map.59 = (f32[4096,256]{1,0:T(8,128)S(1)}, f32[4096,256]{1,0:T(8,128)S(1)}) custom-call(f32[8192,256]{1,0:T(8,128)} %slab_ref.1, f32[64,128]{1,0:T(8,128)S(1)} %fusion.sign_ref), custom_call_target="tpu_custom_call" | custom-call | tf_op jit(solution)/shard_map/pallas_call | solution.py:127
  10.3 1.6 %collective-permute-start.2 = (s32[512]{0:T(512)S(1)}, s32[512]{0:T(512)S(1)}, u32[]{:S(2)}, u32[]{:S(2)}) collective-permute-start(s32[512]{0:T(512)S(1)} %pad_add_fusion.1), channel_id=1, source_target_pairs={{0,8},{2,10},{4,12},{6,14},{8,0},{10,2},{12,4},{14,6},{16,24},{18,... | collective-permute-start | bytes 6152 | tf_op jit(solution)/shard_map/ppermute | solution.py:20
  12.0 2.7 %shard_map.60.high_ref = f32[4096,256]{1,0:T(8,128)S(1)} custom-call(f32[4096,256]{1,0:T(8,128)S(1)} %get-tuple-element.28.rest_ref, f32[64,128]{1,0:T(8,128)S(1)} %fusion.sign_ref), custom_call_target="tpu_custom_call" | custom-call | tf_op jit(solution)/shard_map/pallas_call | solution.py:142
  14.7 2.7 %collective-permute-start.3 = (s32[1024]{0:T(1024)S(1)}, s32[1024]{0:T(1024)S(1)}, u32[]{:S(2)}, u32[]{:S(2)}) collective-permute-start(s32[1024]{0:T(1024)S(1)} %pad_add_fusion), channel_id=1, source_target_pairs={{0,16},{2,18},{4,20},{6,22},{8,24},{10,26},{12,28},{14,30},{16,0},... | collective-permute-start | bytes 12296 | tf_op jit(solution)/shard_map/ppermute | solution.py:20
  17.3 1.5 %shard_map.61.mixed_ref = f32[8192,256]{1,0:T(8,128)S(1)} custom-call(f32[4096,256]{1,0:T(8,128)S(1)} %get-tuple-element.30.low_ref, f32[4096,256]{1,0:T(8,128)S(1)} %shard_map.60.high_ref), custom_call_target="tpu_custom_call" | custom-call | tf_op jit(solution)/shard_map/pallas_call | solution.py:154
  19.2 2.9 %shard_map.62 = (f32[512,256]{1,0:T(8,128)S(1)}, f32[512,256]{1,0:T(8,128)S(1)}) custom-call(s32[2048]{0:T(1024)S(1)} %constant_dynamic-update-slice_fusion.pick_ref, f32[8192,256]{1,0:T(8,128)S(1)} %shard_map.61.mixed_ref), custom_call_target="tpu_custom_call" | custom-call | tf_op jit(solution)/shard_map/pallas_call | solution.py:187
  22.2 3.1 %shard_map.63 = (f32[512,256]{1,0:T(8,128)S(1)}, f32[512,256]{1,0:T(8,128)S(1)}) custom-call(s32[2048]{0:T(1024)S(1)} %constant_dynamic-update-slice_fusion.pick_ref, f32[8192,256]{1,0:T(8,128)S(1)} %shard_map.61.mixed_ref), custom_call_target="tpu_custom_call" | custom-call | tf_op jit(solution)/shard_map/pallas_call | solution.py:187
  28.4 5.9 %collective-permute-done.5 = f32[256,256]{1,0:T(8,128)S(1)} collective-permute-done((f32[256,256]{1,0:T(8,128)S(1)}, f32[256,256]{1,0:T(8,128)S(1)}, u32[]{:S(2)}, u32[]{:S(2)}) %collective-permute-start.5) | collective-permute-done | bytes 262176 | tf_op jit(solution)/shard_map/ppermute | solution.py:20
  36.8 2.5 %collective-permute-done.6 = f32[128,256]{1,0:T(8,128)S(1)} collective-permute-done((f32[128,256]{1,0:T(8,128)S(1)}, f32[128,256]{1,0:T(8,128)S(1)}, u32[]{:S(2)}, u32[]{:S(2)}) %collective-permute-start.6) | collective-permute-done | bytes 131104 | tf_op jit(solution)/shard_map/ppermute | solution.py:20
  39.4 2.8 %collective-permute-start.7 = (f32[64,256]{1,0:T(8,128)S(1)}, f32[64,256]{1,0:T(8,128)S(1)}, u32[]{:S(2)}, u32[]{:S(2)}) collective-permute-start(f32[64,256]{1,0:T(8,128)S(1)} %slice.85), channel_id=1, source_target_pairs={{0,16},{2,18},{4,20},{6,22},{8,24},{10,26},{12,28},{14,30},{16,0},... | collective-permute-start | bytes 196616 | tf_op jit(solution)/shard_map/ppermute | solution.py:20
  42.2 1.7 %collective-permute-start.11 = (f32[64,256]{1,0:T(8,128)S(1)}, f32[64,256]{1,0:T(8,128)S(1)}, u32[]{:S(2)}, u32[]{:S(2)}) collective-permute-start(f32[64,256]{1,0:T(8,128)S(1)} %slice.91), channel_id=1, source_target_pairs={{0,16},{2,18},{4,20},{6,22},{8,24},{10,26},{12,28},{14,30},{16,0},... | collective-permute-start | bytes 196616 | tf_op jit(solution)/shard_map/ppermute | solution.py:20
  44.0 2.3 %collective-permute-done.7 = f32[64,256]{1,0:T(8,128)S(1)} collective-permute-done((f32[64,256]{1,0:T(8,128)S(1)}, f32[64,256]{1,0:T(8,128)S(1)}, u32[]{:S(2)}, u32[]{:S(2)}) %collective-permute-start.7) | collective-permute-done | bytes 65568 | tf_op jit(solution)/shard_map/ppermute | solution.py:20
  46.2 1.6 %collective-permute-start.12 = (f32[64,256]{1,0:T(8,128)S(1)}, f32[64,256]{1,0:T(8,128)S(1)}, u32[]{:S(2)}, u32[]{:S(2)}) collective-permute-start(f32[64,256]{1,0:T(8,128)S(1)} %slice_add_fusion.7.refs_0_), channel_id=1, source_target_pairs={{0,1},{1,0},{2,3},{3,2},{4,5},{5,4},{6,7},{7,6},{8,9},{9,8},{10,11... | collective-permute-start | bytes 196616 | tf_op jit(solution)/shard_map/ppermute | solution.py:448
  48.2 1.6 %collective-permute-start.13 = (f32[64,256]{1,0:T(8,128)S(1)}, f32[64,256]{1,0:T(8,128)S(1)}, u32[]{:S(2)}, u32[]{:S(2)}) collective-permute-start(f32[64,256]{1,0:T(8,128)S(1)} %slice_add_fusion.6.refs_2_), channel_id=1, source_target_pairs={{0,1},{1,0},{2,3},{3,2},{4,5},{5,4},{6,7},{7,6},{8,9},{9,8},{10,11... | collective-permute-start | bytes 196616 | tf_op jit(solution)/shard_map/ppermute | solution.py:448
  50.6 1.9 %collective-permute-done.13.refs_3_ = f32[64,256]{1,0:T(8,128)S(1)} collective-permute-done((f32[64,256]{1,0:T(8,128)S(1)}, f32[64,256]{1,0:T(8,128)S(1)}, u32[]{:S(2)}, u32[]{:S(2)}) %collective-permute-start.13) | collective-permute-done | bytes 65568 | tf_op jit(solution)/shard_map/ppermute | solution.py:448
  55.7 3.7 %collective-permute-done.22 = f32[2,80,128]{2,1,0:T(8,128)S(1)} collective-permute-done((f32[2,80,128]{2,1,0:T(8,128)S(1)}, f32[2,80,128]{2,1,0:T(8,128)S(1)}, u32[]{:S(2)}, u32[]{:S(2)}) %collective-permute-start.22) | collective-permute-done | bytes 81952 | tf_op jit(solution)/shard_map/ppermute | solution.py:20
  60.0 1.5 %collective-permute-start.16 = (f32[1,80,128]{2,1,0:T(8,128)S(1)}, f32[1,80,128]{2,1,0:T(8,128)S(1)}, u32[]{:S(2)}, u32[]{:S(2)}) collective-permute-start(f32[1,80,128]{2,1,0:T(8,128)S(1)} %slice.95), channel_id=1, source_target_pairs={{0,8},{2,10},{4,12},{6,14},{8,0},{10,2},{12,4},{14,6},{16,24},{18,... | collective-permute-start | bytes 122888 | tf_op jit(solution)/shard_map/ppermute | solution.py:20
  61.6 1.9 %collective-permute-done.23 = f32[1,80,128]{2,1,0:T(8,128)S(1)} collective-permute-done((f32[1,80,128]{2,1,0:T(8,128)S(1)}, f32[1,80,128]{2,1,0:T(8,128)S(1)}, u32[]{:S(2)}, u32[]{:S(2)}) %collective-permute-start.23) | collective-permute-done | bytes 40992 | tf_op jit(solution)/shard_map/ppermute | solution.py:20
  64.6 2.0 %collective-permute-start.17 = (f32[1,80,128]{2,1,0:T(8,128)S(1)}, f32[1,80,128]{2,1,0:T(8,128)S(1)}, u32[]{:S(2)}, u32[]{:S(2)}) collective-permute-start(f32[1,80,128]{2,1,0:T(8,128)S(1)} %slice_add_fusion.9), channel_id=1, source_target_pairs={{0,16},{2,18},{4,20},{6,22},{8,24},{10,26},{12,28},{14,30},{16,0},... | collective-permute-start | bytes 122888 | tf_op jit(solution)/shard_map/ppermute | solution.py:20
  66.6 2.0 %collective-permute-done.24 = f32[1,80,128]{2,1,0:T(8,128)S(1)} collective-permute-done((f32[1,80,128]{2,1,0:T(8,128)S(1)}, f32[1,80,128]{2,1,0:T(8,128)S(1)}, u32[]{:S(2)}, u32[]{:S(2)}) %collective-permute-start.24) | collective-permute-done | bytes 40992 | tf_op jit(solution)/shard_map/ppermute | solution.py:20
  69.6 2.0 %collective-permute-start.18 = (f32[1,80,128]{2,1,0:T(8,128)S(1)}, f32[1,80,128]{2,1,0:T(8,128)S(1)}, u32[]{:S(2)}, u32[]{:S(2)}) collective-permute-start(f32[1,80,128]{2,1,0:T(8,128)S(1)} %add.60), channel_id=1, source_target_pairs={{0,8},{2,10},{4,12},{6,14},{8,0},{10,2},{12,4},{14,6},{16,24},{18,... | collective-permute-start | bytes 122888 | tf_op jit(solution)/shard_map/ppermute | solution.py:20
  74.7 2.5 %collective-permute-done.26 = f32[2,80,128]{2,1,0:T(8,128)S(1)} collective-permute-done((f32[2,80,128]{2,1,0:T(8,128)S(1)}, f32[2,80,128]{2,1,0:T(8,128)S(1)}, u32[]{:S(2)}, u32[]{:S(2)}) %collective-permute-start.26) | collective-permute-done | bytes 81952 | tf_op jit(solution)/shard_map/ppermute | solution.py:20
  79.6 13.1 %shard_map.65 = f32[512,256]{1,0:T(8,128)} custom-call(f32[4,80,128]{2,1,0:T(8,128)S(1)} %pad_maximum_fusion.refs_0_, f32[4,80,128]{2,1,0:T(8,128)S(1)} %collective-permute-done.20.refs_1_, f32[4,80,128]{2,1,0:T(8,128)S(1)} %pad_maximum_fusion.1.refs_2_, f32[4,80,128]{2,1,0:T(8,128)S(1)} %collective-permute-done.27.refs_3_), custom_call_target="tpu_custom_call" | custom-call | tf_op jit(solution)/shard_map/pallas_call | solution.py:382
  (79 shorter events, 20.9 us)
Async XLA Ops:
  2.8 7.5 %collective-permute-start.1 = (s32[256]{0:T(256)S(1)}, s32[256]{0:T(256)S(1)}, u32[]{:S(2)}, u32[]{:S(2)}) collective-permute-start(s32[256]{0:T(256)S(1)} %pad_add_fusion.2), channel_id=1, source_target_pairs={{0,4},{2,6},{4,0},{6,2},{8,12},{10,14},{12,8},{14,10},{16,20},{18,... | collective-permute-start | bytes 3080 | tf_op jit(solution)/shard_map/ppermute | solution.py:20
  10.3 4.3 %collective-permute-start.2 = (s32[512]{0:T(512)S(1)}, s32[512]{0:T(512)S(1)}, u32[]{:S(2)}, u32[]{:S(2)}) collective-permute-start(s32[512]{0:T(512)S(1)} %pad_add_fusion.1), channel_id=1, source_target_pairs={{0,8},{2,10},{4,12},{6,14},{8,0},{10,2},{12,4},{14,6},{16,24},{18,... | collective-permute-start | bytes 6152 | tf_op jit(solution)/shard_map/ppermute | solution.py:20
  14.7 4.6 %collective-permute-start.3 = (s32[1024]{0:T(1024)S(1)}, s32[1024]{0:T(1024)S(1)}, u32[]{:S(2)}, u32[]{:S(2)}) collective-permute-start(s32[1024]{0:T(1024)S(1)} %pad_add_fusion), channel_id=1, source_target_pairs={{0,16},{2,18},{4,20},{6,22},{8,24},{10,26},{12,28},{14,30},{16,0},... | collective-permute-start | bytes 12296 | tf_op jit(solution)/shard_map/ppermute | solution.py:20
  22.2 3.7 %collective-permute-start.4 = (f32[512,256]{1,0:T(8,128)S(1)}, f32[512,256]{1,0:T(8,128)S(1)}, u32[]{:S(2)}, u32[]{:S(2)}) collective-permute-start(f32[512,256]{1,0:T(8,128)S(1)} %get-tuple-element.35), channel_id=1, source_target_pairs={{0,2},{2,0},{4,6},{6,4},{8,10},{10,8},{12,14},{14,12},{16,18},{18,... | collective-permute-start | bytes 1572872 | tf_op jit(solution)/shard_map/ppermute | solution.py:20
  25.3 2.1 %collective-permute-start.8 = (f32[512,256]{1,0:T(8,128)S(1)}, f32[512,256]{1,0:T(8,128)S(1)}, u32[]{:S(2)}, u32[]{:S(2)}) collective-permute-start(f32[512,256]{1,0:T(8,128)S(1)} %get-tuple-element.37), channel_id=1, source_target_pairs={{0,2},{2,0},{4,6},{6,4},{8,10},{10,8},{12,14},{14,12},{16,18},{18,... | collective-permute-start | bytes 1572872 | tf_op jit(solution)/shard_map/ppermute | solution.py:20
  26.0 8.3 %collective-permute-start.5 = (f32[256,256]{1,0:T(8,128)S(1)}, f32[256,256]{1,0:T(8,128)S(1)}, u32[]{:S(2)}, u32[]{:S(2)}) collective-permute-start(f32[256,256]{1,0:T(8,128)S(1)} %slice.81), channel_id=1, source_target_pairs={{0,4},{2,6},{4,0},{6,2},{8,12},{10,14},{12,8},{14,10},{16,20},{18,... | collective-permute-start | bytes 786440 | tf_op jit(solution)/shard_map/ppermute | solution.py:20
  27.5 8.7 %collective-permute-start.9 = (f32[256,256]{1,0:T(8,128)S(1)}, f32[256,256]{1,0:T(8,128)S(1)}, u32[]{:S(2)}, u32[]{:S(2)}) collective-permute-start(f32[256,256]{1,0:T(8,128)S(1)} %slice.87), channel_id=1, source_target_pairs={{0,8},{2,10},{4,12},{6,14},{8,0},{10,2},{12,4},{14,6},{16,24},{18,... | collective-permute-start | bytes 786440 | tf_op jit(solution)/shard_map/ppermute | solution.py:20
  34.4 5.0 %collective-permute-start.6 = (f32[128,256]{1,0:T(8,128)S(1)}, f32[128,256]{1,0:T(8,128)S(1)}, u32[]{:S(2)}, u32[]{:S(2)}) collective-permute-start(f32[128,256]{1,0:T(8,128)S(1)} %slice.83), channel_id=1, source_target_pairs={{0,8},{2,10},{4,12},{6,14},{8,0},{10,2},{12,4},{14,6},{16,24},{18,... | collective-permute-start | bytes 393224 | tf_op jit(solution)/shard_map/ppermute | solution.py:20
  36.2 6.0 %collective-permute-start.10 = (f32[128,256]{1,0:T(8,128)S(1)}, f32[128,256]{1,0:T(8,128)S(1)}, u32[]{:S(2)}, u32[]{:S(2)}) collective-permute-start(f32[128,256]{1,0:T(8,128)S(1)} %slice.89), channel_id=1, source_target_pairs={{0,4},{2,6},{4,0},{6,2},{8,12},{10,14},{12,8},{14,10},{16,20},{18,... | collective-permute-start | bytes 393224 | tf_op jit(solution)/shard_map/ppermute | solution.py:20
  39.4 6.8 %collective-permute-start.7 = (f32[64,256]{1,0:T(8,128)S(1)}, f32[64,256]{1,0:T(8,128)S(1)}, u32[]{:S(2)}, u32[]{:S(2)}) collective-permute-start(f32[64,256]{1,0:T(8,128)S(1)} %slice.85), channel_id=1, source_target_pairs={{0,16},{2,18},{4,20},{6,22},{8,24},{10,26},{12,28},{14,30},{16,0},... | collective-permute-start | bytes 196616 | tf_op jit(solution)/shard_map/ppermute | solution.py:20
  42.2 5.9 %collective-permute-start.11 = (f32[64,256]{1,0:T(8,128)S(1)}, f32[64,256]{1,0:T(8,128)S(1)}, u32[]{:S(2)}, u32[]{:S(2)}) collective-permute-start(f32[64,256]{1,0:T(8,128)S(1)} %slice.91), channel_id=1, source_target_pairs={{0,16},{2,18},{4,20},{6,22},{8,24},{10,26},{12,28},{14,30},{16,0},... | collective-permute-start | bytes 196616 | tf_op jit(solution)/shard_map/ppermute | solution.py:20
  46.2 4.3 %collective-permute-start.12 = (f32[64,256]{1,0:T(8,128)S(1)}, f32[64,256]{1,0:T(8,128)S(1)}, u32[]{:S(2)}, u32[]{:S(2)}) collective-permute-start(f32[64,256]{1,0:T(8,128)S(1)} %slice_add_fusion.7.refs_0_), channel_id=1, source_target_pairs={{0,1},{1,0},{2,3},{3,2},{4,5},{5,4},{6,7},{7,6},{8,9},{9,8},{10,11... | collective-permute-start | bytes 196616 | tf_op jit(solution)/shard_map/ppermute | solution.py:448
  48.2 4.3 %collective-permute-start.13 = (f32[64,256]{1,0:T(8,128)S(1)}, f32[64,256]{1,0:T(8,128)S(1)}, u32[]{:S(2)}, u32[]{:S(2)}) collective-permute-start(f32[64,256]{1,0:T(8,128)S(1)} %slice_add_fusion.6.refs_2_), channel_id=1, source_target_pairs={{0,1},{1,0},{2,3},{3,2},{4,5},{5,4},{6,7},{7,6},{8,9},{9,8},{10,11... | collective-permute-start | bytes 196616 | tf_op jit(solution)/shard_map/ppermute | solution.py:448
  54.8 4.6 %collective-permute-start.22 = (f32[2,80,128]{2,1,0:T(8,128)S(1)}, f32[2,80,128]{2,1,0:T(8,128)S(1)}, u32[]{:S(2)}, u32[]{:S(2)}) collective-permute-start(f32[2,80,128]{2,1,0:T(8,128)S(1)} %slice.97), channel_id=1, source_target_pairs={{0,8},{2,10},{4,12},{6,14},{8,0},{10,2},{12,4},{14,6},{16,24},{18,... | collective-permute-start | bytes 245768 | tf_op jit(solution)/shard_map/ppermute | solution.py:20
  55.1 4.9 %collective-permute-start.15 = (f32[2,80,128]{2,1,0:T(8,128)S(1)}, f32[2,80,128]{2,1,0:T(8,128)S(1)}, u32[]{:S(2)}, u32[]{:S(2)}) collective-permute-start(f32[2,80,128]{2,1,0:T(8,128)S(1)} %slice.93), channel_id=1, source_target_pairs={{0,4},{2,6},{4,0},{6,2},{8,12},{10,14},{12,8},{14,10},{16,20},{18,... | collective-permute-start | bytes 245768 | tf_op jit(solution)/shard_map/ppermute | solution.py:20
  59.4 4.1 %collective-permute-start.23 = (f32[1,80,128]{2,1,0:T(8,128)S(1)}, f32[1,80,128]{2,1,0:T(8,128)S(1)}, u32[]{:S(2)}, u32[]{:S(2)}) collective-permute-start(f32[1,80,128]{2,1,0:T(8,128)S(1)} %slice.99), channel_id=1, source_target_pairs={{0,4},{2,6},{4,0},{6,2},{8,12},{10,14},{12,8},{14,10},{16,20},{18,... | collective-permute-start | bytes 122888 | tf_op jit(solution)/shard_map/ppermute | solution.py:20
  60.0 4.6 %collective-permute-start.16 = (f32[1,80,128]{2,1,0:T(8,128)S(1)}, f32[1,80,128]{2,1,0:T(8,128)S(1)}, u32[]{:S(2)}, u32[]{:S(2)}) collective-permute-start(f32[1,80,128]{2,1,0:T(8,128)S(1)} %slice.95), channel_id=1, source_target_pairs={{0,8},{2,10},{4,12},{6,14},{8,0},{10,2},{12,4},{14,6},{16,24},{18,... | collective-permute-start | bytes 122888 | tf_op jit(solution)/shard_map/ppermute | solution.py:20
  63.5 5.1 %collective-permute-start.24 = (f32[1,80,128]{2,1,0:T(8,128)S(1)}, f32[1,80,128]{2,1,0:T(8,128)S(1)}, u32[]{:S(2)}, u32[]{:S(2)}) collective-permute-start(f32[1,80,128]{2,1,0:T(8,128)S(1)} %slice_add_fusion.8), channel_id=1, source_target_pairs={{0,16},{2,18},{4,20},{6,22},{8,24},{10,26},{12,28},{14,30},{16,0},... | collective-permute-start | bytes 122888 | tf_op jit(solution)/shard_map/ppermute | solution.py:20
  64.6 5.0 %collective-permute-start.17 = (f32[1,80,128]{2,1,0:T(8,128)S(1)}, f32[1,80,128]{2,1,0:T(8,128)S(1)}, u32[]{:S(2)}, u32[]{:S(2)}) collective-permute-start(f32[1,80,128]{2,1,0:T(8,128)S(1)} %slice_add_fusion.9), channel_id=1, source_target_pairs={{0,16},{2,18},{4,20},{6,22},{8,24},{10,26},{12,28},{14,30},{16,0},... | collective-permute-start | bytes 122888 | tf_op jit(solution)/shard_map/ppermute | solution.py:20
  68.6 4.1 %collective-permute-start.25 = (f32[1,80,128]{2,1,0:T(8,128)S(1)}, f32[1,80,128]{2,1,0:T(8,128)S(1)}, u32[]{:S(2)}, u32[]{:S(2)}) collective-permute-start(f32[1,80,128]{2,1,0:T(8,128)S(1)} %add.64), channel_id=1, source_target_pairs={{0,4},{2,6},{4,0},{6,2},{8,12},{10,14},{12,8},{14,10},{16,20},{18,... | collective-permute-start | bytes 122888 | tf_op jit(solution)/shard_map/ppermute | solution.py:20
  69.6 4.0 %collective-permute-start.18 = (f32[1,80,128]{2,1,0:T(8,128)S(1)}, f32[1,80,128]{2,1,0:T(8,128)S(1)}, u32[]{:S(2)}, u32[]{:S(2)}) collective-permute-start(f32[1,80,128]{2,1,0:T(8,128)S(1)} %add.60), channel_id=1, source_target_pairs={{0,8},{2,10},{4,12},{6,14},{8,0},{10,2},{12,4},{14,6},{16,24},{18,... | collective-permute-start | bytes 122888 | tf_op jit(solution)/shard_map/ppermute | solution.py:20
  72.7 4.4 %collective-permute-start.26 = (f32[2,80,128]{2,1,0:T(8,128)S(1)}, f32[2,80,128]{2,1,0:T(8,128)S(1)}, u32[]{:S(2)}, u32[]{:S(2)}) collective-permute-start(f32[2,80,128]{2,1,0:T(8,128)S(1)} %pad_maximum_fusion.4), channel_id=1, source_target_pairs={{0,8},{2,10},{4,12},{6,14},{8,0},{10,2},{12,4},{14,6},{16,24},{18,... | collective-permute-start | bytes 245768 | tf_op jit(solution)/shard_map/ppermute | solution.py:20
  73.6 4.4 %collective-permute-start.19 = (f32[2,80,128]{2,1,0:T(8,128)S(1)}, f32[2,80,128]{2,1,0:T(8,128)S(1)}, u32[]{:S(2)}, u32[]{:S(2)}) collective-permute-start(f32[2,80,128]{2,1,0:T(8,128)S(1)} %pad_maximum_fusion.3), channel_id=1, source_target_pairs={{0,4},{2,6},{4,0},{6,2},{8,12},{10,14},{12,8},{14,10},{16,20},{18,... | collective-permute-start | bytes 245768 | tf_op jit(solution)/shard_map/ppermute | solution.py:20
  77.2 1.7 %collective-permute-start.27 = (f32[4,80,128]{2,1,0:T(8,128)S(1)}, f32[4,80,128]{2,1,0:T(8,128)S(1)}, u32[]{:S(2)}, u32[]{:S(2)}) collective-permute-start(f32[4,80,128]{2,1,0:T(8,128)S(1)} %pad_maximum_fusion.1.refs_2_), channel_id=1, source_target_pairs={{0,2},{2,0},{4,6},{6,4},{8,10},{10,8},{12,14},{14,12},{16,18},{18,... | collective-permute-start | bytes 491528 | tf_op jit(solution)/shard_map/ppermute | solution.py:20
  (4 other events, 6.0 us)

commit v8 on v7

--- a/solution.py
+++ b/solution.py
@@ -198,9 +198,13 @@
     return (0, 1, 2) if group == 0 else (0, 2, 1)
 
 
-def block_groups(tiles):
-    pairs = [(i, j) for i in range(tiles) for j in range(i, tiles)]
-    return [pairs[:len(pairs) // 2], pairs[len(pairs) // 2:]]
+def own_pairs(tiles):
+    return [(i, j) for i in range(tiles) for j in range(i, tiles)]
+
+
+def cross_pairs(tiles, peers):
+    total = tiles * peers
+    return [(i, j) for i in range(total) for j in range(i, total) if i // tiles != j // tiles]
 
 
 def strip_starts(group, low_bit):
@@ -214,42 +218,37 @@
     return starts
 
 
-def gram_kernel(*refs, scale, peers, groups):
-    outs = 2 * len(groups)
-    pieces, out_refs, (full_ref, gram_ref) = refs[:-outs - 2], refs[-outs - 2:-2], refs[-2:]
+def gram_kernel(*refs, scale, peers, pairs, group):
+    pieces, (keep_ref, send_ref, full_ref, gram_ref) = refs[:-4], refs[-4:]
     total = full_ref.shape[1]
     width = total // peers
-    column = lax.axis_index("cols")
     at = 0
     for run in range(len(pieces) // peers):
         count = pieces[run * peers].shape[0]
         for peer in range(peers):
-            first = pl.multiple_of((column ^ peer) * width, width)
+            first = pl.multiple_of((lax.axis_index("cols") ^ peer) * width, width) if peers > 1 else 0
             full_ref[at:at + count, pl.ds(first, width)] = pieces[run * peers + peer][...]
         at += count
-    for upper in range(total // LANES):
+    for upper in sorted({i for i, _ in pairs}):
         here = slice(upper * LANES, (upper + 1) * LANES)
-        rows = lax.dot_general(full_ref[:, here], full_ref[:, upper * LANES:], (((0,), (0,)), ((), ())),
+        left = min(j for i, j in pairs if i == upper) * LANES
+        rows = lax.dot_general(full_ref[:, here], full_ref[:, left:], (((0,), (0,)), ((), ())),
                                precision=lax.Precision.HIGHEST, preferred_element_type=jnp.float32)
-        gram_ref[here, upper * LANES:] = rows * scale
+        gram_ref[here, left:] = rows * scale
     height = LANES // STRIPS
-    for group, pairs in enumerate(groups):
-        for low_bit in range(2):
-            for slot, strip in enumerate(strip_starts(group, low_bit)):
-                for block, (upper, right) in enumerate(pairs):
-                    out_refs[2 * group + low_bit][slot, block * height:(block + 1) * height, :] = gram_ref[
-                        pl.ds(upper * LANES + strip, height), right * LANES:(right + 1) * LANES]
-
-
-def partial_gram(pieces, rows, peers, scale):
+    for low_bit, out_ref in ((0, keep_ref), (1, send_ref)):
+        for slot, strip in enumerate(strip_starts(group, low_bit)):
+            for block, (upper, right) in enumerate(pairs):
+                out_ref[slot, block * height:(block + 1) * height, :] = gram_ref[
+                    pl.ds(upper * LANES + strip, height), right * LANES:(right + 1) * LANES]
+
+
+def partial_gram(pieces, rows, peers, pairs, group, scale):
     total = pieces[0].shape[1] * peers
-    groups = block_groups(total // LANES)
-    shapes = []
-    for pairs in groups:
-        shapes += [jax.ShapeDtypeStruct((STRIPS // 2, len(pairs) * (LANES // STRIPS), LANES), jnp.float32)] * 2
-    return pl.pallas_call(
-        functools.partial(gram_kernel, scale=scale, peers=peers, groups=groups),
-        out_shape=shapes,
+    half = jax.ShapeDtypeStruct((STRIPS // 2, len(pairs) * (LANES // STRIPS), LANES), jnp.float32)
+    return pl.pallas_call(
+        functools.partial(gram_kernel, scale=scale, peers=peers, pairs=pairs, group=group),
+        out_shape=[half, half],
         scratch_shapes=[pltpu.VMEM((rows, total), jnp.float32), pltpu.VMEM((total, total), jnp.float32)],
         compiler_params=pltpu.CompilerParams(vmem_limit_bytes=16 << 20),
     )(*pieces)
@@ -353,16 +352,25 @@
     return jnp.where(col >= row, factored[:, :LANES], 0.0), factored[:, LANES:]
 
 
-def factor_kernel(*refs, groups):
+def factor_kernel(*refs, peers):
     strip_refs, (out_ref, gram_ref, factor_ref, column_ref, lead_ref, below_ref) = refs[:-6], refs[-6:]
     tiles = gram_ref.shape[0] // LANES
+    panel_tiles = tiles // peers
     height = LANES // STRIPS
-    for group, pairs in enumerate(groups):
-        for low_bit in range(2):
-            for slot, strip in enumerate(strip_starts(group, low_bit)):
-                for block, (upper, right) in enumerate(pairs):
-                    gram_ref[pl.ds(upper * LANES + strip, height), right * LANES:(right + 1) * LANES] = strip_refs[
-                        2 * group + low_bit][slot, block * height:(block + 1) * height, :]
+    own = own_pairs(panel_tiles)
+    for low_bit in range(2):
+        for slot, strip in enumerate(strip_starts(0, low_bit)):
+            for peer in range(peers):
+                base = (lax.axis_index("cols") ^ peer) * (panel_tiles * LANES)
+                for block, (upper, right) in enumerate(own):
+                    at = (peer * len(own) + block) * height
+                    gram_ref[pl.ds(pl.multiple_of(base + upper * LANES + strip, height), height),
+                             pl.ds(pl.multiple_of(base + right * LANES, LANES), LANES)] = strip_refs[low_bit][
+                        slot, at:at + height, :]
+        for slot, strip in enumerate(strip_starts(1, low_bit)):
+            for block, (upper, right) in enumerate(cross_pairs(panel_tiles, peers)):
+                gram_ref[pl.ds(upper * LANES + strip, height), right * LANES:(right + 1) * LANES] = strip_refs[
+                    2 + low_bit][slot, block * height:(block + 1) * height, :]
     factor_ref[...] = jnp.zeros_like(factor_ref)
     for at in range(tiles):
         here = slice(at * LANES, (at + 1) * LANES)
@@ -378,9 +386,10 @@
     out_ref[...] = factor_ref[:, pl.ds(first, width)]
 
 
-def factor_panel(strips, total, width):
-    return pl.pallas_call(
-        functools.partial(factor_kernel, groups=block_groups(total // LANES)),
+def factor_panel(strips, peers, width):
+    total = width * peers
+    return pl.pallas_call(
+        functools.partial(factor_kernel, peers=peers),
         out_shape=jax.ShapeDtypeStruct((total, width), jnp.float32),
         scratch_shapes=[pltpu.VMEM((total, total), jnp.float32)] * 2 + [
             pltpu.VMEM((LANES * SUB, LANES), jnp.float32), pltpu.VMEM((2 * LANES, LANES), jnp.float32),
@@ -389,7 +398,7 @@
     )(*strips)
 
 
-def summed_strips(keep, send, group, bits):
+def summed_strips(keep, send, group, bits, peers):
     core, *order = strip_bits(group)
     gram = keep + swapped(send, "rows", core)
     for bit in order:
@@ -397,6 +406,9 @@
         gram = gram[:half] + swapped(gram[half:], "rows", bit)
     for bit in range(len(order) + 1, bits):
         gram = gram + swapped(gram, "rows", bit)
+    others = [lax.ppermute(gram, "cols", [(i, i ^ peer) for i in range(lax.axis_size("cols"))])
+              for peer in range(1, peers)]
+    gram = jnp.concatenate([gram, *others], axis=1)
     for bit in reversed(order):
         gram = jnp.concatenate([gram, swapped(gram, "rows", bit)])
     return [gram, swapped(gram, "rows", core)]
@@ -437,21 +449,22 @@
         picks = jnp.concatenate([picks, other])
     first = pick_count // 2
     cross = list(range(1, bits))
-    sketch = []
+    parts = []
     pieces = []
     for start, count, order in ((0, first, cross), (first, pick_count - first, cross[1:2] + cross[:1] + cross[2:])):
         keep, send = pick_rows(picks, mixed, start, count, order, groups)
         part = reduce_run(keep, send, order)
-        sketch.append(part)
+        parts.append(part)
         pieces.append(part)
         for peer in range(1, peers):
             pieces.append(lax.ppermute(part, "cols", [(i, i ^ peer) for i in range(peers)]))
-    sketch = jnp.concatenate(sketch)
-    parts = partial_gram(pieces, pick_count, peers, 1.0 / (pick_count * groups))
-    strips = []
-    for group in range(len(parts) // 2):
-        strips += summed_strips(parts[2 * group], parts[2 * group + 1], group, bits)
-    r_panel = factor_panel(strips, panel_width * peers, panel_width)
+    sketch = jnp.concatenate(parts)
+    tiles = panel_width // LANES
+    scale = 1.0 / (pick_count * groups)
+    own = partial_gram(parts, pick_count, 1, own_pairs(tiles), 0, scale)
+    cross = partial_gram(pieces, pick_count, peers, cross_pairs(tiles, peers), 1, scale)
+    strips = summed_strips(*own, 0, bits, peers) + summed_strips(*cross, 1, bits, 1)
+    r_panel = factor_panel(strips, peers, panel_width)
     return (sketch, r_panel)
 
 

time: 92.9 us -> 97.3 us (1.047)
  waiting for transfers between devices: 31.3 us -> 38.2 us
  starting transfers between devices: 29 us -> 26.4 us
    ppermute x26, waiting for transfers between devices: 28.5 us -> 33.4 us  [swapped(): lax.ppermute(value, axis, [(i, i ^ 1 << bit) for i in range(lax.axis_size...]
    ppermute x26, starting transfers between devices: 25.9 us -> 22.8 us  [swapped(): lax.ppermute(value, axis, [(i, i ^ 1 << bit) for i in range(lax.axis_size...]
    ppermute x0 -> x1, waiting for transfers between devices: none -> 1.67 us  [summed_strips(): lax.ppermute(gram, 'cols', [(i, i ^ peer) for i in range(lax.axis_size('c...]
    ppermute x0 -> x1, starting transfers between devices: none -> 1.49 us  [summed_strips(): lax.ppermute(gram, 'cols', [(i, i ^ peer) for i in range(lax.axis_size('c...]
    ppermute x2, starting transfers between devices: 3.15 us -> 2.09 us  [body(): lax.ppermute(part, 'cols', [(i, i ^ peer) for i in range(peers)])]
    pallas_call x2 -> x3, Pallas kernels: 13.9 us -> 14 us  [the longest x1 13.2 us: factor_panel(): pl.pallas_call(functools.partial(factor_kernel, peers=peers), out_shape=j...]
  transfers between devices with their start and end apart: 28 -> 29, of which waited for: 21 -> 20; matrix products, arithmetic and copies ran while one was open for 2% -> 2% of each run, Pallas kernels for 13% -> 13%
where the time goes in v8:
time: 97.3 us; the launch traced here: 97.1 us
  waiting for transfers between devices  38.2 us (39%)
  Pallas kernels  28.9 us (30%)
  starting transfers between devices  26.4 us (27%)
  other arithmetic  2.55 us (3%)
    ppermute x26, waiting for transfers between devices, swapped(): lax.ppermute(value, axis, [(i, i ^ 1 << bit) for i in range(lax.axis_size...  33.4 us
    ppermute x26, starting transfers between devices, swapped(): lax.ppermute(value, axis, [(i, i ^ 1 << bit) for i in range(lax.axis_size...  22.8 us
    pallas_call x1, Pallas kernels, factor_panel(): pl.pallas_call(functools.partial(factor_kernel, peers=peers), out_shape=j...  13.2 us
    pallas_call x2, Pallas kernels, pick_rows(): pl.pallas_call(functools.partial(pick_kernel, start=start, count=count, o...  5.99 us
    pallas_call x1, Pallas kernels, mix_first(): pl.pallas_call(functools.partial(mix_first_kernel, quarter=rows // 4), in...  4.72 us
    ppermute x2, waiting for transfers between devices, body(): lax.ppermute(part, 'cols', [(i, i ^ peer) for i in range(peers)])  3.19 us
    pallas_call x1, Pallas kernels, mix_next(): pl.pallas_call(functools.partial(mix_next_kernel, quarter=rest.shape[0] /...  2.69 us
    ppermute x2, starting transfers between devices, body(): lax.ppermute(part, 'cols', [(i, i ^ peer) for i in range(peers)])  2.09 us
  transfers between devices with their start and end apart: 29, of which 20 were waited for; matrix products, arithmetic and copies ran while one was open for 2% of the time, Pallas kernels for 13%

profile of v8, /device:TPU:0, one launch (start us, length us, event | category | flops | bytes accessed | tf_op | source)
XLA Modules:
  0.0 97.1 jit_solution(16367857939859414451)
XLA Ops:
  2.8 2.8 %collective-permute-start.1 = (s32[256]{0:T(256)S(1)}, s32[256]{0:T(256)S(1)}, u32[]{:S(2)}, u32[]{:S(2)}) collective-permute-start(s32[256]{0:T(256)S(1)} %pad_add_fusion.2), channel_id=1, source_target_pairs={{0,4},{2,6},{4,0},{6,2},{8,12},{10,14},{12,8},{14,10},{16,20},{18,... | collective-permute-start | bytes 3080 | tf_op jit(solution)/shard_map/ppermute | solution.py:20
  5.6 4.7 %shard_map.59 = (f32[4096,256]{1,0:T(8,128)S(1)}, f32[4096,256]{1,0:T(8,128)S(1)}) custom-call(f32[8192,256]{1,0:T(8,128)} %slab_ref.1, f32[64,128]{1,0:T(8,128)S(1)} %fusion.sign_ref), custom_call_target="tpu_custom_call" | custom-call | tf_op jit(solution)/shard_map/pallas_call | solution.py:127
  10.3 1.6 %collective-permute-start.2 = (s32[512]{0:T(512)S(1)}, s32[512]{0:T(512)S(1)}, u32[]{:S(2)}, u32[]{:S(2)}) collective-permute-start(s32[512]{0:T(512)S(1)} %pad_add_fusion.1), channel_id=1, source_target_pairs={{0,8},{2,10},{4,12},{6,14},{8,0},{10,2},{12,4},{14,6},{16,24},{18,... | collective-permute-start | bytes 6152 | tf_op jit(solution)/shard_map/ppermute | solution.py:20
  12.0 2.7 %shard_map.60.high_ref = f32[4096,256]{1,0:T(8,128)S(1)} custom-call(f32[4096,256]{1,0:T(8,128)S(1)} %get-tuple-element.28.rest_ref, f32[64,128]{1,0:T(8,128)S(1)} %fusion.sign_ref), custom_call_target="tpu_custom_call" | custom-call | tf_op jit(solution)/shard_map/pallas_call | solution.py:142
  14.7 2.7 %collective-permute-start.3 = (s32[1024]{0:T(1024)S(1)}, s32[1024]{0:T(1024)S(1)}, u32[]{:S(2)}, u32[]{:S(2)}) collective-permute-start(s32[1024]{0:T(1024)S(1)} %pad_add_fusion), channel_id=1, source_target_pairs={{0,16},{2,18},{4,20},{6,22},{8,24},{10,26},{12,28},{14,30},{16,0},... | collective-permute-start | bytes 12296 | tf_op jit(solution)/shard_map/ppermute | solution.py:20
  19.2 2.9 %shard_map.62 = (f32[512,256]{1,0:T(8,128)S(1)}, f32[512,256]{1,0:T(8,128)S(1)}) custom-call(s32[2048]{0:T(1024)S(1)} %constant_dynamic-update-slice_fusion.pick_ref, f32[8192,256]{1,0:T(8,128)S(1)} %shard_map.61.mixed_ref), custom_call_target="tpu_custom_call" | custom-call | tf_op jit(solution)/shard_map/pallas_call | solution.py:187
  22.2 3.1 %shard_map.63 = (f32[512,256]{1,0:T(8,128)S(1)}, f32[512,256]{1,0:T(8,128)S(1)}) custom-call(s32[2048]{0:T(1024)S(1)} %constant_dynamic-update-slice_fusion.pick_ref, f32[8192,256]{1,0:T(8,128)S(1)} %shard_map.61.mixed_ref), custom_call_target="tpu_custom_call" | custom-call | tf_op jit(solution)/shard_map/pallas_call | solution.py:187
  28.4 5.9 %collective-permute-done.5 = f32[256,256]{1,0:T(8,128)S(1)} collective-permute-done((f32[256,256]{1,0:T(8,128)S(1)}, f32[256,256]{1,0:T(8,128)S(1)}, u32[]{:S(2)}, u32[]{:S(2)}) %collective-permute-start.5) | collective-permute-done | bytes 262176 | tf_op jit(solution)/shard_map/ppermute | solution.py:20
  36.8 2.5 %collective-permute-done.6 = f32[128,256]{1,0:T(8,128)S(1)} collective-permute-done((f32[128,256]{1,0:T(8,128)S(1)}, f32[128,256]{1,0:T(8,128)S(1)}, u32[]{:S(2)}, u32[]{:S(2)}) %collective-permute-start.6) | collective-permute-done | bytes 131104 | tf_op jit(solution)/shard_map/ppermute | solution.py:20
  39.4 2.8 %collective-permute-start.7 = (f32[64,256]{1,0:T(8,128)S(1)}, f32[64,256]{1,0:T(8,128)S(1)}, u32[]{:S(2)}, u32[]{:S(2)}) collective-permute-start(f32[64,256]{1,0:T(8,128)S(1)} %slice.85), channel_id=1, source_target_pairs={{0,16},{2,18},{4,20},{6,22},{8,24},{10,26},{12,28},{14,30},{16,0},... | collective-permute-start | bytes 196616 | tf_op jit(solution)/shard_map/ppermute | solution.py:20
  42.2 1.7 %collective-permute-start.11 = (f32[64,256]{1,0:T(8,128)S(1)}, f32[64,256]{1,0:T(8,128)S(1)}, u32[]{:S(2)}, u32[]{:S(2)}) collective-permute-start(f32[64,256]{1,0:T(8,128)S(1)} %slice.91), channel_id=1, source_target_pairs={{0,16},{2,18},{4,20},{6,22},{8,24},{10,26},{12,28},{14,30},{16,0},... | collective-permute-start | bytes 196616 | tf_op jit(solution)/shard_map/ppermute | solution.py:20
  44.0 2.3 %collective-permute-done.7 = f32[64,256]{1,0:T(8,128)S(1)} collective-permute-done((f32[64,256]{1,0:T(8,128)S(1)}, f32[64,256]{1,0:T(8,128)S(1)}, u32[]{:S(2)}, u32[]{:S(2)}) %collective-permute-start.7) | collective-permute-done | bytes 65568 | tf_op jit(solution)/shard_map/ppermute | solution.py:20
  46.2 1.9 %collective-permute-done.11 = f32[64,256]{1,0:T(8,128)S(1)} collective-permute-done((f32[64,256]{1,0:T(8,128)S(1)}, f32[64,256]{1,0:T(8,128)S(1)}, u32[]{:S(2)}, u32[]{:S(2)}) %collective-permute-start.11) | collective-permute-done | bytes 65568 | tf_op jit(solution)/shard_map/ppermute | solution.py:20
  48.7 1.6 %collective-permute-start.20 = (f32[64,256]{1,0:T(8,128)S(1)}, f32[64,256]{1,0:T(8,128)S(1)}, u32[]{:S(2)}, u32[]{:S(2)}) collective-permute-start(f32[64,256]{1,0:T(8,128)S(1)} %slice_add_fusion.6.refs_0_), channel_id=1, source_target_pairs={{0,1},{1,0},{2,3},{3,2},{4,5},{5,4},{6,7},{7,6},{8,9},{9,8},{10,11... | collective-permute-start | bytes 196616 | tf_op jit(solution)/shard_map/ppermute | solution.py:460
  51.4 2.0 %collective-permute-done.20.refs_1_ = f32[64,256]{1,0:T(8,128)S(1)} collective-permute-done((f32[64,256]{1,0:T(8,128)S(1)}, f32[64,256]{1,0:T(8,128)S(1)}, u32[]{:S(2)}, u32[]{:S(2)}) %collective-permute-start.20) | collective-permute-done | bytes 65568 | tf_op jit(solution)/shard_map/ppermute | solution.py:460
  57.3 1.7 %collective-permute-done.14 = f32[1,48,128]{2,1,0:T(8,128)S(1)} collective-permute-done((f32[1,48,128]{2,1,0:T(8,128)S(1)}, f32[1,48,128]{2,1,0:T(8,128)S(1)}, u32[]{:S(2)}, u32[]{:S(2)}) %collective-permute-start.14) | collective-permute-done | bytes 24608 | tf_op jit(solution)/shard_map/ppermute | solution.py:20
  60.1 3.7 %collective-permute-done.15 = f32[1,48,128]{2,1,0:T(8,128)S(1)} collective-permute-done((f32[1,48,128]{2,1,0:T(8,128)S(1)}, f32[1,48,128]{2,1,0:T(8,128)S(1)}, u32[]{:S(2)}, u32[]{:S(2)}) %collective-permute-start.15) | collective-permute-done | bytes 24608 | tf_op jit(solution)/shard_map/ppermute | solution.py:20
  65.9 1.7 %collective-permute-done.16 = f32[1,48,128]{2,1,0:T(8,128)S(1)} collective-permute-done((f32[1,48,128]{2,1,0:T(8,128)S(1)}, f32[1,48,128]{2,1,0:T(8,128)S(1)}, u32[]{:S(2)}, u32[]{:S(2)}) %collective-permute-start.16) | collective-permute-done | bytes 24608 | tf_op jit(solution)/shard_map/ppermute | solution.py:409
  67.7 1.6 %collective-permute-done.24 = f32[1,64,128]{2,1,0:T(8,128)S(1)} collective-permute-done((f32[1,64,128]{2,1,0:T(8,128)S(1)}, f32[1,64,128]{2,1,0:T(8,128)S(1)}, u32[]{:S(2)}, u32[]{:S(2)}) %collective-permute-start.24) | collective-permute-done | bytes 32800 | tf_op jit(solution)/shard_map/ppermute | solution.py:20
  70.5 3.8 %collective-permute-done.25 = f32[1,64,128]{2,1,0:T(8,128)S(1)} collective-permute-done((f32[1,64,128]{2,1,0:T(8,128)S(1)}, f32[1,64,128]{2,1,0:T(8,128)S(1)}, u32[]{:S(2)}, u32[]{:S(2)}) %collective-permute-start.25) | collective-permute-done | bytes 32800 | tf_op jit(solution)/shard_map/ppermute | solution.py:20
  74.9 1.6 %collective-permute-start.18 = (f32[2,96,128]{2,1,0:T(8,128)S(1)}, f32[2,96,128]{2,1,0:T(8,128)S(1)}, u32[]{:S(2)}, u32[]{:S(2)}) collective-permute-start(f32[2,96,128]{2,1,0:T(8,128)S(1)} %pad_maximum_fusion.3), channel_id=1, source_target_pairs={{0,4},{2,6},{4,0},{6,2},{8,12},{10,14},{12,8},{14,10},{16,20},{18,... | collective-permute-start | bytes 294920 | tf_op jit(solution)/shard_map/ppermute | solution.py:20
  76.4 1.8 %collective-permute-done.26 = f32[1,64,128]{2,1,0:T(8,128)S(1)} collective-permute-done((f32[1,64,128]{2,1,0:T(8,128)S(1)}, f32[1,64,128]{2,1,0:T(8,128)S(1)}, u32[]{:S(2)}, u32[]{:S(2)}) %collective-permute-start.26) | collective-permute-done | bytes 32800 | tf_op jit(solution)/shard_map/ppermute | solution.py:20
  79.6 2.9 %collective-permute-done.27 = f32[2,64,128]{2,1,0:T(8,128)S(1)} collective-permute-done((f32[2,64,128]{2,1,0:T(8,128)S(1)}, f32[2,64,128]{2,1,0:T(8,128)S(1)}, u32[]{:S(2)}, u32[]{:S(2)}) %collective-permute-start.27) | collective-permute-done | bytes 65568 | tf_op jit(solution)/shard_map/ppermute | solution.py:20
  83.9 13.2 %shard_map.66 = f32[512,256]{1,0:T(8,128)} custom-call(f32[4,96,128]{2,1,0:T(8,128)S(1)} %pad_maximum_fusion.refs_0_, f32[4,96,128]{2,1,0:T(8,128)S(1)} %collective-permute-done.19.refs_1_, f32[4,64,128]{2,1,0:T(8,128)S(1)} %pad_maximum_fusion.2.refs_2_, f32[4,64,128]{2,1,0:T(8,128)S(1)} %collective-permute-done.28.refs_3_), custom_call_target="tpu_custom_call" | custom-call | tf_op jit(solution)/shard_map/pallas_call | solution.py:391
  (83 shorter events, 23.1 us)
Async XLA Ops:
  2.8 7.5 %collective-permute-start.1 = (s32[256]{0:T(256)S(1)}, s32[256]{0:T(256)S(1)}, u32[]{:S(2)}, u32[]{:S(2)}) collective-permute-start(s32[256]{0:T(256)S(1)} %pad_add_fusion.2), channel_id=1, source_target_pairs={{0,4},{2,6},{4,0},{6,2},{8,12},{10,14},{12,8},{14,10},{16,20},{18,... | collective-permute-start | bytes 3080 | tf_op jit(solution)/shard_map/ppermute | solution.py:20
  10.3 4.3 %collective-permute-start.2 = (s32[512]{0:T(512)S(1)}, s32[512]{0:T(512)S(1)}, u32[]{:S(2)}, u32[]{:S(2)}) collective-permute-start(s32[512]{0:T(512)S(1)} %pad_add_fusion.1), channel_id=1, source_target_pairs={{0,8},{2,10},{4,12},{6,14},{8,0},{10,2},{12,4},{14,6},{16,24},{18,... | collective-permute-start | bytes 6152 | tf_op jit(solution)/shard_map/ppermute | solution.py:20
  14.7 4.6 %collective-permute-start.3 = (s32[1024]{0:T(1024)S(1)}, s32[1024]{0:T(1024)S(1)}, u32[]{:S(2)}, u32[]{:S(2)}) collective-permute-start(s32[1024]{0:T(1024)S(1)} %pad_add_fusion), channel_id=1, source_target_pairs={{0,16},{2,18},{4,20},{6,22},{8,24},{10,26},{12,28},{14,30},{16,0},... | collective-permute-start | bytes 12296 | tf_op jit(solution)/shard_map/ppermute | solution.py:20
  22.2 3.7 %collective-permute-start.4 = (f32[512,256]{1,0:T(8,128)S(1)}, f32[512,256]{1,0:T(8,128)S(1)}, u32[]{:S(2)}, u32[]{:S(2)}) collective-permute-start(f32[512,256]{1,0:T(8,128)S(1)} %get-tuple-element.35), channel_id=1, source_target_pairs={{0,2},{2,0},{4,6},{6,4},{8,10},{10,8},{12,14},{14,12},{16,18},{18,... | collective-permute-start | bytes 1572872 | tf_op jit(solution)/shard_map/ppermute | solution.py:20
  26.0 8.3 %collective-permute-start.5 = (f32[256,256]{1,0:T(8,128)S(1)}, f32[256,256]{1,0:T(8,128)S(1)}, u32[]{:S(2)}, u32[]{:S(2)}) collective-permute-start(f32[256,256]{1,0:T(8,128)S(1)} %slice.81), channel_id=1, source_target_pairs={{0,4},{2,6},{4,0},{6,2},{8,12},{10,14},{12,8},{14,10},{16,20},{18,... | collective-permute-start | bytes 786440 | tf_op jit(solution)/shard_map/ppermute | solution.py:20
  27.5 8.7 %collective-permute-start.9 = (f32[256,256]{1,0:T(8,128)S(1)}, f32[256,256]{1,0:T(8,128)S(1)}, u32[]{:S(2)}, u32[]{:S(2)}) collective-permute-start(f32[256,256]{1,0:T(8,128)S(1)} %slice.87), channel_id=1, source_target_pairs={{0,8},{2,10},{4,12},{6,14},{8,0},{10,2},{12,4},{14,6},{16,24},{18,... | collective-permute-start | bytes 786440 | tf_op jit(solution)/shard_map/ppermute | solution.py:20
  34.4 5.0 %collective-permute-start.6 = (f32[128,256]{1,0:T(8,128)S(1)}, f32[128,256]{1,0:T(8,128)S(1)}, u32[]{:S(2)}, u32[]{:S(2)}) collective-permute-start(f32[128,256]{1,0:T(8,128)S(1)} %slice.83), channel_id=1, source_target_pairs={{0,8},{2,10},{4,12},{6,14},{8,0},{10,2},{12,4},{14,6},{16,24},{18,... | collective-permute-start | bytes 393224 | tf_op jit(solution)/shard_map/ppermute | solution.py:20
  36.2 6.0 %collective-permute-start.10 = (f32[128,256]{1,0:T(8,128)S(1)}, f32[128,256]{1,0:T(8,128)S(1)}, u32[]{:S(2)}, u32[]{:S(2)}) collective-permute-start(f32[128,256]{1,0:T(8,128)S(1)} %slice.89), channel_id=1, source_target_pairs={{0,4},{2,6},{4,0},{6,2},{8,12},{10,14},{12,8},{14,10},{16,20},{18,... | collective-permute-start | bytes 393224 | tf_op jit(solution)/shard_map/ppermute | solution.py:20
  39.4 6.8 %collective-permute-start.7 = (f32[64,256]{1,0:T(8,128)S(1)}, f32[64,256]{1,0:T(8,128)S(1)}, u32[]{:S(2)}, u32[]{:S(2)}) collective-permute-start(f32[64,256]{1,0:T(8,128)S(1)} %slice.85), channel_id=1, source_target_pairs={{0,16},{2,18},{4,20},{6,22},{8,24},{10,26},{12,28},{14,30},{16,0},... | collective-permute-start | bytes 196616 | tf_op jit(solution)/shard_map/ppermute | solution.py:20
  42.2 5.9 %collective-permute-start.11 = (f32[64,256]{1,0:T(8,128)S(1)}, f32[64,256]{1,0:T(8,128)S(1)}, u32[]{:S(2)}, u32[]{:S(2)}) collective-permute-start(f32[64,256]{1,0:T(8,128)S(1)} %slice.91), channel_id=1, source_target_pairs={{0,16},{2,18},{4,20},{6,22},{8,24},{10,26},{12,28},{14,30},{16,0},... | collective-permute-start | bytes 196616 | tf_op jit(solution)/shard_map/ppermute | solution.py:20
  48.7 4.7 %collective-permute-start.20 = (f32[64,256]{1,0:T(8,128)S(1)}, f32[64,256]{1,0:T(8,128)S(1)}, u32[]{:S(2)}, u32[]{:S(2)}) collective-permute-start(f32[64,256]{1,0:T(8,128)S(1)} %slice_add_fusion.6.refs_0_), channel_id=1, source_target_pairs={{0,1},{1,0},{2,3},{3,2},{4,5},{5,4},{6,7},{7,6},{8,9},{9,8},{10,11... | collective-permute-start | bytes 196616 | tf_op jit(solution)/shard_map/ppermute | solution.py:460
  50.2 4.4 %collective-permute-start.21 = (f32[64,256]{1,0:T(8,128)S(1)}, f32[64,256]{1,0:T(8,128)S(1)}, u32[]{:S(2)}, u32[]{:S(2)}) collective-permute-start(f32[64,256]{1,0:T(8,128)S(1)} %slice_add_fusion.5.refs_1_.refs_2_), channel_id=1, source_target_pairs={{0,1},{1,0},{2,3},{3,2},{4,5},{5,4},{6,7},{7,6},{8,9},{9,8},{10,11... | collective-permute-start | bytes 196616 | tf_op jit(solution)/shard_map/ppermute | solution.py:460
  50.8 4.3 %collective-permute-start.13 = (f32[2,48,128]{2,1,0:T(8,128)S(1)}, f32[2,48,128]{2,1,0:T(8,128)S(1)}, u32[]{:S(2)}, u32[]{:S(2)}) collective-permute-start(f32[2,48,128]{2,1,0:T(8,128)S(1)} %slice.93), channel_id=1, source_target_pairs={{0,4},{2,6},{4,0},{6,2},{8,12},{10,14},{12,8},{14,10},{16,20},{18,... | collective-permute-start | bytes 147464 | tf_op jit(solution)/shard_map/ppermute | solution.py:20
  55.1 3.9 %collective-permute-start.14 = (f32[1,48,128]{2,1,0:T(8,128)S(1)}, f32[1,48,128]{2,1,0:T(8,128)S(1)}, u32[]{:S(2)}, u32[]{:S(2)}) collective-permute-start(f32[1,48,128]{2,1,0:T(8,128)S(1)} %slice.95), channel_id=1, source_target_pairs={{0,8},{2,10},{4,12},{6,14},{8,0},{10,2},{12,4},{14,6},{16,24},{18,... | collective-permute-start | bytes 73736 | tf_op jit(solution)/shard_map/ppermute | solution.py:20
  56.5 8.8 %collective-permute-start.23 = (f32[2,64,128]{2,1,0:T(8,128)S(1)}, f32[2,64,128]{2,1,0:T(8,128)S(1)}, u32[]{:S(2)}, u32[]{:S(2)}) collective-permute-start(f32[2,64,128]{2,1,0:T(8,128)S(1)} %slice.97), channel_id=1, source_target_pairs={{0,8},{2,10},{4,12},{6,14},{8,0},{10,2},{12,4},{14,6},{16,24},{18,... | collective-permute-start | bytes 196616 | tf_op jit(solution)/shard_map/ppermute | solution.py:20
  59.0 4.7 %collective-permute-start.15 = (f32[1,48,128]{2,1,0:T(8,128)S(1)}, f32[1,48,128]{2,1,0:T(8,128)S(1)}, u32[]{:S(2)}, u32[]{:S(2)}) collective-permute-start(f32[1,48,128]{2,1,0:T(8,128)S(1)} %slice_add_fusion.9), channel_id=1, source_target_pairs={{0,16},{2,18},{4,20},{6,22},{8,24},{10,26},{12,28},{14,30},{16,0},... | collective-permute-start | bytes 73736 | tf_op jit(solution)/shard_map/ppermute | solution.py:20
  63.8 3.8 %collective-permute-start.16 = (f32[1,48,128]{2,1,0:T(8,128)S(1)}, f32[1,48,128]{2,1,0:T(8,128)S(1)}, u32[]{:S(2)}, u32[]{:S(2)}) collective-permute-start(f32[1,48,128]{2,1,0:T(8,128)S(1)} %add.60), channel_id=1, source_target_pairs={{0,1},{1,0},{2,3},{3,2},{4,5},{5,4},{6,7},{7,6},{8,9},{9,8},{10,11... | collective-permute-start | bytes 73736 | tf_op jit(solution)/shard_map/ppermute | solution.py:409
  65.3 4.0 %collective-permute-start.24 = (f32[1,64,128]{2,1,0:T(8,128)S(1)}, f32[1,64,128]{2,1,0:T(8,128)S(1)}, u32[]{:S(2)}, u32[]{:S(2)}) collective-permute-start(f32[1,64,128]{2,1,0:T(8,128)S(1)} %slice.99), channel_id=1, source_target_pairs={{0,4},{2,6},{4,0},{6,2},{8,12},{10,14},{12,8},{14,10},{16,20},{18,... | collective-permute-start | bytes 98312 | tf_op jit(solution)/shard_map/ppermute | solution.py:20
  67.6 7.3 %collective-permute-start.17 = (f32[1,96,128]{2,1,0:T(8,128)S(1)}, f32[1,96,128]{2,1,0:T(8,128)S(1)}, u32[]{:S(2)}, u32[]{:S(2)}) collective-permute-start(f32[1,96,128]{2,1,0:T(8,128)S(1)} %pad_maximum_fusion.5), channel_id=1, source_target_pairs={{0,8},{2,10},{4,12},{6,14},{8,0},{10,2},{12,4},{14,6},{16,24},{18,... | collective-permute-start | bytes 147464 | tf_op jit(solution)/shard_map/ppermute | solution.py:20
  69.3 5.0 %collective-permute-start.25 = (f32[1,64,128]{2,1,0:T(8,128)S(1)}, f32[1,64,128]{2,1,0:T(8,128)S(1)}, u32[]{:S(2)}, u32[]{:S(2)}) collective-permute-start(f32[1,64,128]{2,1,0:T(8,128)S(1)} %slice_add_fusion.8), channel_id=1, source_target_pairs={{0,16},{2,18},{4,20},{6,22},{8,24},{10,26},{12,28},{14,30},{16,0},... | collective-permute-start | bytes 98312 | tf_op jit(solution)/shard_map/ppermute | solution.py:20
  74.3 3.9 %collective-permute-start.26 = (f32[1,64,128]{2,1,0:T(8,128)S(1)}, f32[1,64,128]{2,1,0:T(8,128)S(1)}, u32[]{:S(2)}, u32[]{:S(2)}) collective-permute-start(f32[1,64,128]{2,1,0:T(8,128)S(1)} %add.64), channel_id=1, source_target_pairs={{0,4},{2,6},{4,0},{6,2},{8,12},{10,14},{12,8},{14,10},{16,20},{18,... | collective-permute-start | bytes 98312 | tf_op jit(solution)/shard_map/ppermute | solution.py:20
  74.9 4.7 %collective-permute-start.18 = (f32[2,96,128]{2,1,0:T(8,128)S(1)}, f32[2,96,128]{2,1,0:T(8,128)S(1)}, u32[]{:S(2)}, u32[]{:S(2)}) collective-permute-start(f32[2,96,128]{2,1,0:T(8,128)S(1)} %pad_maximum_fusion.3), channel_id=1, source_target_pairs={{0,4},{2,6},{4,0},{6,2},{8,12},{10,14},{12,8},{14,10},{16,20},{18,... | collective-permute-start | bytes 294920 | tf_op jit(solution)/shard_map/ppermute | solution.py:20
  78.2 4.3 %collective-permute-start.27 = (f32[2,64,128]{2,1,0:T(8,128)S(1)}, f32[2,64,128]{2,1,0:T(8,128)S(1)}, u32[]{:S(2)}, u32[]{:S(2)}) collective-permute-start(f32[2,64,128]{2,1,0:T(8,128)S(1)} %pad_maximum_fusion.4), channel_id=1, source_target_pairs={{0,8},{2,10},{4,12},{6,14},{8,0},{10,2},{12,4},{14,6},{16,24},{18,... | collective-permute-start | bytes 196616 | tf_op jit(solution)/shard_map/ppermute | solution.py:20
  79.6 4.4 %collective-permute-start.19 = (f32[4,96,128]{2,1,0:T(8,128)S(1)}, f32[4,96,128]{2,1,0:T(8,128)S(1)}, u32[]{:S(2)}, u32[]{:S(2)}) collective-permute-start(f32[4,96,128]{2,1,0:T(8,128)S(1)} %pad_maximum_fusion.refs_0_), channel_id=1, source_target_pairs={{0,2},{2,0},{4,6},{6,4},{8,10},{10,8},{12,14},{14,12},{16,18},{18,... | collective-permute-start | bytes 589832 | tf_op jit(solution)/shard_map/ppermute | solution.py:20
  (5 other events, 8.6 us)

commit v9 on v7

--- a/solution.py
+++ b/solution.py
@@ -160,18 +160,18 @@
     )(low, high)
 
 
-def pick_kernel(pick_ref, mixed_ref, keep_ref, send_ref, *, start, count, order, pick_count, groups, norm_scale):
+def pick_kernel(pick_ref, mixed_ref, *out_refs, jobs, pick_count, groups, norm_scale):
     device = lax.axis_index("rows")
     sub_row = lax.broadcasted_iota(jnp.int32, (SUB, mixed_ref.shape[1]), 0)
-    octets = count // SUB
-    for out_ref, low_bit in ((send_ref, 1), (keep_ref, 0)):
+
+    def pick(out_ref, start, count, order, low_bit):
         @pl.loop(0, groups // 2)
         def _(pair):
             offset = low_bit
             for place, bit in enumerate(reversed(order)):
                 offset = offset | ((pair >> place) & 1) << bit
             scale = parity_sign((device ^ offset) & device).astype(jnp.float32) * norm_scale
-            for octet in range(octets):
+            for octet in range(count // SUB):
                 rows = None
                 for sub in range(SUB):
                     index = pick_ref[offset * pick_count + start + octet * SUB + sub]
@@ -180,16 +180,18 @@
                 out_at = pl.multiple_of(pair * count + octet * SUB, SUB)
                 out_ref[pl.ds(out_at, SUB), :] = rows * scale
 
-
-def pick_rows(picks, mixed, start, count, order, groups):
+    for out_ref, job in zip(out_refs, jobs):
+        pick(out_ref, *job)
+
+
+def pick_rows(picks, mixed, jobs, groups):
     norm_scale = 1.0 / math.sqrt(mixed.shape[0] * groups)
-    half = jax.ShapeDtypeStruct((groups // 2 * count, mixed.shape[1]), jnp.float32)
-    return pl.pallas_call(
-        functools.partial(pick_kernel, start=start, count=count, order=order, pick_count=picks.shape[0] // groups,
+    return pl.pallas_call(
+        functools.partial(pick_kernel, jobs=jobs, pick_count=picks.shape[0] // groups,
                           groups=groups, norm_scale=norm_scale),
         in_specs=[pl.BlockSpec(memory_space=pltpu.SMEM), pl.BlockSpec(memory_space=pltpu.VMEM)],
-        out_specs=[pl.BlockSpec(memory_space=pltpu.VMEM)] * 2,
-        out_shape=[half, half],
+        out_specs=[pl.BlockSpec(memory_space=pltpu.VMEM)] * len(jobs),
+        out_shape=[jax.ShapeDtypeStruct((groups // 2 * job[1], mixed.shape[1]), jnp.float32) for job in jobs],
         compiler_params=pltpu.CompilerParams(vmem_limit_bytes=32 << 20),
     )(picks, mixed)
 
@@ -285,18 +287,19 @@
     return jnp.broadcast_to(value[:, lane:lane + 1], (value.shape[0], LANES))
 
 
-def factor_tile(diagonal, column_ref, lead_ref, below_ref):
+def factor_tile(diagonal, column_ref, lead_ref, below_ref, inverted):
     row = lax.broadcasted_iota(jnp.int32, (LANES, LANES), 0)
     col = lax.broadcasted_iota(jnp.int32, (LANES, LANES), 1)
     identity = (row == col).astype(jnp.float32)
-    whole = jnp.concatenate([diagonal, identity], axis=1)
+    whole = jnp.concatenate([diagonal, identity], axis=1) if inverted else diagonal
+    copies = whole.shape[1] // LANES
     slabs = LANES // SUB
     tile = [whole[SUB * t:SUB * t + SUB] for t in range(slabs)]
     sub_row = lax.broadcasted_iota(jnp.int32, tile[0].shape, 0)
     done = []
 
     def widen(value):
-        return jnp.concatenate([value, value], axis=1)
+        return jnp.concatenate([value] * copies, axis=1)
 
     def splats(slab, at):
         return [lane_splat(tile[slab][:, :LANES], SUB * at + j) for j in range(SUB)]
@@ -307,7 +310,7 @@
         direct = range(at + 1, min(slabs, at + 1 + AHEAD))
         for j in range(SUB):
             column_ref[(at * SUB + j) * SUB:(at * SUB + j + 1) * SUB, :] = own[j]
-        for half in range(2):
+        for half in range(copies):
             lead_ref[half * LANES + at * SUB:half * LANES + (at + 1) * SUB, :] = lead[:, half * LANES:(half + 1) * LANES]
         pivot = {(i, j): column_ref[pl.ds((at * SUB + j) * SUB + i, SUB, stride=0), :]
                  for j in range(SUB) for i in range(j + 1)}
@@ -316,7 +319,7 @@
             own = splats(at + 1, at + 1)
         if at + 2 < slabs:
             near = splats(at + 2, at + 1)
-        rows = [jnp.concatenate([lead_ref[pl.ds(half * LANES + at * SUB + m, SUB, stride=0), :] for half in range(2)],
+        rows = [jnp.concatenate([lead_ref[pl.ds(half * LANES + at * SUB + m, SUB, stride=0), :] for half in range(copies)],
                                 axis=1) for m in range(SUB)]
         panel = jnp.zeros_like(lead)
         for m in range(SUB):
@@ -350,7 +353,7 @@
             for u in range(at + 1 + AHEAD, slabs):
                 tile[u] = tile[u] - update[SUB * u:SUB * u + SUB]
     factored = jnp.concatenate(done, axis=0)
-    return jnp.where(col >= row, factored[:, :LANES], 0.0), factored[:, LANES:]
+    return jnp.where(col >= row, factored[:, :LANES], 0.0), factored[:, LANES:] if inverted else None
 
 
 def factor_kernel(*refs, groups):
@@ -366,7 +369,7 @@
     factor_ref[...] = jnp.zeros_like(factor_ref)
     for at in range(tiles):
         here = slice(at * LANES, (at + 1) * LANES)
-        factor, inverse = factor_tile(gram_ref[here, here], column_ref, lead_ref, below_ref)
+        factor, inverse = factor_tile(gram_ref[here, here], column_ref, lead_ref, below_ref, at < tiles - 1)
         factor_ref[here, here] = factor
         if at < tiles - 1:
             rest = (at + 1) * LANES
@@ -439,8 +442,12 @@
     cross = list(range(1, bits))
     sketch = []
     pieces = []
-    for start, count, order in ((0, first, cross), (first, pick_count - first, cross[1:2] + cross[:1] + cross[2:])):
-        keep, send = pick_rows(picks, mixed, start, count, order, groups)
+    job_a = (0, first, cross)
+    job_b = (first, pick_count - first, cross[1:2] + cross[:1] + cross[2:])
+    send_a, = pick_rows(picks, mixed, [job_a + (1,)], groups)
+    send_a, mixed = lax.optimization_barrier((send_a, mixed))
+    keep_a, send_b, keep_b = pick_rows(picks, mixed, [job_a + (0,), job_b + (1,), job_b + (0,)], groups)
+    for keep, send, order in ((keep_a, send_a, job_a[2]), (keep_b, send_b, job_b[2])):
         part = reduce_run(keep, send, order)
         sketch.append(part)
         pieces.append(part)

time: 92.9 us -> 92.7 us (level)
  transfers between devices with their start and end apart: 28 -> 28, of which waited for: 21 -> 21; matrix products, arithmetic and copies ran while one was open for 2% -> 2% of each run, Pallas kernels for 13% -> 14%
where the time goes in v9:
time: 92.7 us; the launch traced here: 92.5 us
  waiting for transfers between devices  31.3 us (34%)
  starting transfers between devices  29 us (31%)
  Pallas kernels  28.7 us (31%)
  other arithmetic  2.57 us (3%)
    ppermute x26, waiting for transfers between devices, swapped(): lax.ppermute(value, axis, [(i, i ^ 1 << bit) for i in range(lax.axis_size...  28.5 us
    ppermute x26, starting transfers between devices, swapped(): lax.ppermute(value, axis, [(i, i ^ 1 << bit) for i in range(lax.axis_size...  25.9 us
    pallas_call x1, Pallas kernels, factor_panel(): pl.pallas_call(functools.partial(factor_kernel, groups=block_groups(total...  13 us
    pallas_call x2, Pallas kernels, pick_rows(): pl.pallas_call(functools.partial(pick_kernel, jobs=jobs, pick_count=picks...  6 us
    pallas_call x1, Pallas kernels, mix_first(): pl.pallas_call(functools.partial(mix_first_kernel, quarter=rows // 4), in...  4.72 us
    ppermute x2, starting transfers between devices, body(): lax.ppermute(part, 'cols', [(i, i ^ peer) for i in range(peers)])  3.15 us
    ppermute x2, waiting for transfers between devices, body(): lax.ppermute(part, 'cols', [(i, i ^ peer) for i in range(peers)])  2.77 us
    pallas_call x1, Pallas kernels, mix_next(): pl.pallas_call(functools.partial(mix_next_kernel, quarter=rest.shape[0] /...  2.69 us
  transfers between devices with their start and end apart: 28, of which 21 were waited for; matrix products, arithmetic and copies ran while one was open for 2% of the time, Pallas kernels for 14%

profile of v9, /device:TPU:0, one launch (start us, length us, event | category | flops | bytes accessed | tf_op | source)
XLA Modules:
  0.0 92.5 jit_solution(1333152760296924879)
XLA Ops:
  2.8 2.8 %collective-permute-start.1 = (s32[256]{0:T(256)S(1)}, s32[256]{0:T(256)S(1)}, u32[]{:S(2)}, u32[]{:S(2)}) collective-permute-start(s32[256]{0:T(256)S(1)} %pad_add_fusion.2), channel_id=1, source_target_pairs={{0,4},{2,6},{4,0},{6,2},{8,12},{10,14},{12,8},{14,10},{16,20},{18,... | collective-permute-start | bytes 3080 | tf_op jit(solution)/shard_map/ppermute | solution.py:20
  5.6 4.7 %shard_map.59 = (f32[4096,256]{1,0:T(8,128)S(1)}, f32[4096,256]{1,0:T(8,128)S(1)}) custom-call(f32[8192,256]{1,0:T(8,128)} %slab_ref.1, f32[64,128]{1,0:T(8,128)S(1)} %fusion.sign_ref), custom_call_target="tpu_custom_call" | custom-call | tf_op jit(solution)/shard_map/pallas_call | solution.py:127
  10.3 1.6 %collective-permute-start.2 = (s32[512]{0:T(512)S(1)}, s32[512]{0:T(512)S(1)}, u32[]{:S(2)}, u32[]{:S(2)}) collective-permute-start(s32[512]{0:T(512)S(1)} %pad_add_fusion.1), channel_id=1, source_target_pairs={{0,8},{2,10},{4,12},{6,14},{8,0},{10,2},{12,4},{14,6},{16,24},{18,... | collective-permute-start | bytes 6152 | tf_op jit(solution)/shard_map/ppermute | solution.py:20
  12.0 2.7 %shard_map.60.high_ref = f32[4096,256]{1,0:T(8,128)S(1)} custom-call(f32[4096,256]{1,0:T(8,128)S(1)} %get-tuple-element.29.rest_ref, f32[64,128]{1,0:T(8,128)S(1)} %fusion.sign_ref), custom_call_target="tpu_custom_call" | custom-call | tf_op jit(solution)/shard_map/pallas_call | solution.py:142
  14.7 2.7 %collective-permute-start.3 = (s32[1024]{0:T(1024)S(1)}, s32[1024]{0:T(1024)S(1)}, u32[]{:S(2)}, u32[]{:S(2)}) collective-permute-start(s32[1024]{0:T(1024)S(1)} %pad_add_fusion), channel_id=1, source_target_pairs={{0,16},{2,18},{4,20},{6,22},{8,24},{10,26},{12,28},{14,30},{16,0},... | collective-permute-start | bytes 12296 | tf_op jit(solution)/shard_map/ppermute | solution.py:20
  17.3 1.5 %shard_map.61.mixed_ref = f32[8192,256]{1,0:T(8,128)S(1)} custom-call(f32[4096,256]{1,0:T(8,128)S(1)} %get-tuple-element.31.low_ref, f32[4096,256]{1,0:T(8,128)S(1)} %shard_map.60.high_ref), custom_call_target="tpu_custom_call" | custom-call | tf_op jit(solution)/shard_map/pallas_call | solution.py:154
  19.2 1.8 %shard_map.62 = f32[512,256]{1,0:T(8,128)S(1)} custom-call(s32[2048]{0:T(1024)S(1)} %constant_dynamic-update-slice_fusion.pick_ref, f32[8192,256]{1,0:T(8,128)S(1)} %shard_map.61.mixed_ref), custom_call_target="tpu_custom_call" | custom-call | tf_op jit(solution)/shard_map/pallas_call | solution.py:189
  21.1 4.2 %shard_map.63 = (f32[512,256]{1,0:T(8,128)S(1)}, f32[512,256]{1,0:T(8,128)S(1)}, f32[512,256]{1,0:T(8,128)S(1)}) custom-call(s32[2048]{0:T(1024)S(1)} %constant_dynamic-update-slice_fusion.pick_ref, f32[8192,256]{1,0:T(8,128)S(1)} %shard_map.61.mixed_ref), custom_call_target="tpu_custom_call" | custom-call | tf_op jit(solution)/shard_map/pallas_call | solution.py:189
  28.4 5.9 %collective-permute-done.5 = f32[256,256]{1,0:T(8,128)S(1)} collective-permute-done((f32[256,256]{1,0:T(8,128)S(1)}, f32[256,256]{1,0:T(8,128)S(1)}, u32[]{:S(2)}, u32[]{:S(2)}) %collective-permute-start.5) | collective-permute-done | bytes 262176 | tf_op jit(solution)/shard_map/ppermute | solution.py:20
  36.8 2.6 %collective-permute-done.6 = f32[128,256]{1,0:T(8,128)S(1)} collective-permute-done((f32[128,256]{1,0:T(8,128)S(1)}, f32[128,256]{1,0:T(8,128)S(1)}, u32[]{:S(2)}, u32[]{:S(2)}) %collective-permute-start.6) | collective-permute-done | bytes 131104 | tf_op jit(solution)/shard_map/ppermute | solution.py:20
  39.4 2.8 %collective-permute-start.7 = (f32[64,256]{1,0:T(8,128)S(1)}, f32[64,256]{1,0:T(8,128)S(1)}, u32[]{:S(2)}, u32[]{:S(2)}) collective-permute-start(f32[64,256]{1,0:T(8,128)S(1)} %slice.85), channel_id=1, source_target_pairs={{0,16},{2,18},{4,20},{6,22},{8,24},{10,26},{12,28},{14,30},{16,0},... | collective-permute-start | bytes 196616 | tf_op jit(solution)/shard_map/ppermute | solution.py:20
  42.3 1.7 %collective-permute-start.11 = (f32[64,256]{1,0:T(8,128)S(1)}, f32[64,256]{1,0:T(8,128)S(1)}, u32[]{:S(2)}, u32[]{:S(2)}) collective-permute-start(f32[64,256]{1,0:T(8,128)S(1)} %slice.91), channel_id=1, source_target_pairs={{0,16},{2,18},{4,20},{6,22},{8,24},{10,26},{12,28},{14,30},{16,0},... | collective-permute-start | bytes 196616 | tf_op jit(solution)/shard_map/ppermute | solution.py:20
  44.0 2.3 %collective-permute-done.7 = f32[64,256]{1,0:T(8,128)S(1)} collective-permute-done((f32[64,256]{1,0:T(8,128)S(1)}, f32[64,256]{1,0:T(8,128)S(1)}, u32[]{:S(2)}, u32[]{:S(2)}) %collective-permute-start.7) | collective-permute-done | bytes 65568 | tf_op jit(solution)/shard_map/ppermute | solution.py:20
  46.3 1.6 %collective-permute-start.12 = (f32[64,256]{1,0:T(8,128)S(1)}, f32[64,256]{1,0:T(8,128)S(1)}, u32[]{:S(2)}, u32[]{:S(2)}) collective-permute-start(f32[64,256]{1,0:T(8,128)S(1)} %slice_add_fusion.7.refs_0_), channel_id=1, source_target_pairs={{0,1},{1,0},{2,3},{3,2},{4,5},{5,4},{6,7},{7,6},{8,9},{9,8},{10,11... | collective-permute-start | bytes 196616 | tf_op jit(solution)/shard_map/ppermute | solution.py:455
  48.2 1.6 %collective-permute-start.13 = (f32[64,256]{1,0:T(8,128)S(1)}, f32[64,256]{1,0:T(8,128)S(1)}, u32[]{:S(2)}, u32[]{:S(2)}) collective-permute-start(f32[64,256]{1,0:T(8,128)S(1)} %slice_add_fusion.6.refs_2_), channel_id=1, source_target_pairs={{0,1},{1,0},{2,3},{3,2},{4,5},{5,4},{6,7},{7,6},{8,9},{9,8},{10,11... | collective-permute-start | bytes 196616 | tf_op jit(solution)/shard_map/ppermute | solution.py:455
  50.6 1.9 %collective-permute-done.13.refs_3_ = f32[64,256]{1,0:T(8,128)S(1)} collective-permute-done((f32[64,256]{1,0:T(8,128)S(1)}, f32[64,256]{1,0:T(8,128)S(1)}, u32[]{:S(2)}, u32[]{:S(2)}) %collective-permute-start.13) | collective-permute-done | bytes 65568 | tf_op jit(solution)/shard_map/ppermute | solution.py:455
  55.7 3.7 %collective-permute-done.22 = f32[2,80,128]{2,1,0:T(8,128)S(1)} collective-permute-done((f32[2,80,128]{2,1,0:T(8,128)S(1)}, f32[2,80,128]{2,1,0:T(8,128)S(1)}, u32[]{:S(2)}, u32[]{:S(2)}) %collective-permute-start.22) | collective-permute-done | bytes 81952 | tf_op jit(solution)/shard_map/ppermute | solution.py:20
  60.0 1.5 %collective-permute-start.16 = (f32[1,80,128]{2,1,0:T(8,128)S(1)}, f32[1,80,128]{2,1,0:T(8,128)S(1)}, u32[]{:S(2)}, u32[]{:S(2)}) collective-permute-start(f32[1,80,128]{2,1,0:T(8,128)S(1)} %slice.95), channel_id=1, source_target_pairs={{0,8},{2,10},{4,12},{6,14},{8,0},{10,2},{12,4},{14,6},{16,24},{18,... | collective-permute-start | bytes 122888 | tf_op jit(solution)/shard_map/ppermute | solution.py:20
  61.6 1.9 %collective-permute-done.23 = f32[1,80,128]{2,1,0:T(8,128)S(1)} collective-permute-done((f32[1,80,128]{2,1,0:T(8,128)S(1)}, f32[1,80,128]{2,1,0:T(8,128)S(1)}, u32[]{:S(2)}, u32[]{:S(2)}) %collective-permute-start.23) | collective-permute-done | bytes 40992 | tf_op jit(solution)/shard_map/ppermute | solution.py:20
  64.6 2.0 %collective-permute-start.17 = (f32[1,80,128]{2,1,0:T(8,128)S(1)}, f32[1,80,128]{2,1,0:T(8,128)S(1)}, u32[]{:S(2)}, u32[]{:S(2)}) collective-permute-start(f32[1,80,128]{2,1,0:T(8,128)S(1)} %slice_add_fusion.9), channel_id=1, source_target_pairs={{0,16},{2,18},{4,20},{6,22},{8,24},{10,26},{12,28},{14,30},{16,0},... | collective-permute-start | bytes 122888 | tf_op jit(solution)/shard_map/ppermute | solution.py:20
  66.6 2.0 %collective-permute-done.24 = f32[1,80,128]{2,1,0:T(8,128)S(1)} collective-permute-done((f32[1,80,128]{2,1,0:T(8,128)S(1)}, f32[1,80,128]{2,1,0:T(8,128)S(1)}, u32[]{:S(2)}, u32[]{:S(2)}) %collective-permute-start.24) | collective-permute-done | bytes 40992 | tf_op jit(solution)/shard_map/ppermute | solution.py:20
  69.6 2.0 %collective-permute-start.18 = (f32[1,80,128]{2,1,0:T(8,128)S(1)}, f32[1,80,128]{2,1,0:T(8,128)S(1)}, u32[]{:S(2)}, u32[]{:S(2)}) collective-permute-start(f32[1,80,128]{2,1,0:T(8,128)S(1)} %add.60), channel_id=1, source_target_pairs={{0,8},{2,10},{4,12},{6,14},{8,0},{10,2},{12,4},{14,6},{16,24},{18,... | collective-permute-start | bytes 122888 | tf_op jit(solution)/shard_map/ppermute | solution.py:20
  74.7 2.5 %collective-permute-done.26 = f32[2,80,128]{2,1,0:T(8,128)S(1)} collective-permute-done((f32[2,80,128]{2,1,0:T(8,128)S(1)}, f32[2,80,128]{2,1,0:T(8,128)S(1)}, u32[]{:S(2)}, u32[]{:S(2)}) %collective-permute-start.26) | collective-permute-done | bytes 81952 | tf_op jit(solution)/shard_map/ppermute | solution.py:20
  79.6 13.0 %shard_map.65 = f32[512,256]{1,0:T(8,128)} custom-call(f32[4,80,128]{2,1,0:T(8,128)S(1)} %pad_maximum_fusion.refs_0_, f32[4,80,128]{2,1,0:T(8,128)S(1)} %collective-permute-done.20.refs_1_, f32[4,80,128]{2,1,0:T(8,128)S(1)} %pad_maximum_fusion.1.refs_2_, f32[4,80,128]{2,1,0:T(8,128)S(1)} %collective-permute-done.27.refs_3_), custom_call_target="tpu_custom_call" | custom-call | tf_op jit(solution)/shard_map/pallas_call | solution.py:385
  (79 shorter events, 20.9 us)
Async XLA Ops:
  2.8 7.5 %collective-permute-start.1 = (s32[256]{0:T(256)S(1)}, s32[256]{0:T(256)S(1)}, u32[]{:S(2)}, u32[]{:S(2)}) collective-permute-start(s32[256]{0:T(256)S(1)} %pad_add_fusion.2), channel_id=1, source_target_pairs={{0,4},{2,6},{4,0},{6,2},{8,12},{10,14},{12,8},{14,10},{16,20},{18,... | collective-permute-start | bytes 3080 | tf_op jit(solution)/shard_map/ppermute | solution.py:20
  10.3 4.3 %collective-permute-start.2 = (s32[512]{0:T(512)S(1)}, s32[512]{0:T(512)S(1)}, u32[]{:S(2)}, u32[]{:S(2)}) collective-permute-start(s32[512]{0:T(512)S(1)} %pad_add_fusion.1), channel_id=1, source_target_pairs={{0,8},{2,10},{4,12},{6,14},{8,0},{10,2},{12,4},{14,6},{16,24},{18,... | collective-permute-start | bytes 6152 | tf_op jit(solution)/shard_map/ppermute | solution.py:20
  14.7 4.6 %collective-permute-start.3 = (s32[1024]{0:T(1024)S(1)}, s32[1024]{0:T(1024)S(1)}, u32[]{:S(2)}, u32[]{:S(2)}) collective-permute-start(s32[1024]{0:T(1024)S(1)} %pad_add_fusion), channel_id=1, source_target_pairs={{0,16},{2,18},{4,20},{6,22},{8,24},{10,26},{12,28},{14,30},{16,0},... | collective-permute-start | bytes 12296 | tf_op jit(solution)/shard_map/ppermute | solution.py:20
  21.1 4.9 %collective-permute-start.4 = (f32[512,256]{1,0:T(8,128)S(1)}, f32[512,256]{1,0:T(8,128)S(1)}, u32[]{:S(2)}, u32[]{:S(2)}) collective-permute-start(f32[512,256]{1,0:T(8,128)S(1)} %shard_map.62), channel_id=1, source_target_pairs={{0,2},{2,0},{4,6},{6,4},{8,10},{10,8},{12,14},{14,12},{16,18},{18,... | collective-permute-start | bytes 1572872 | tf_op jit(solution)/shard_map/ppermute | solution.py:20
  25.3 2.1 %collective-permute-start.8 = (f32[512,256]{1,0:T(8,128)S(1)}, f32[512,256]{1,0:T(8,128)S(1)}, u32[]{:S(2)}, u32[]{:S(2)}) collective-permute-start(f32[512,256]{1,0:T(8,128)S(1)} %get-tuple-element.39), channel_id=1, source_target_pairs={{0,2},{2,0},{4,6},{6,4},{8,10},{10,8},{12,14},{14,12},{16,18},{18,... | collective-permute-start | bytes 1572872 | tf_op jit(solution)/shard_map/ppermute | solution.py:20
  26.0 8.3 %collective-permute-start.5 = (f32[256,256]{1,0:T(8,128)S(1)}, f32[256,256]{1,0:T(8,128)S(1)}, u32[]{:S(2)}, u32[]{:S(2)}) collective-permute-start(f32[256,256]{1,0:T(8,128)S(1)} %slice.81), channel_id=1, source_target_pairs={{0,4},{2,6},{4,0},{6,2},{8,12},{10,14},{12,8},{14,10},{16,20},{18,... | collective-permute-start | bytes 786440 | tf_op jit(solution)/shard_map/ppermute | solution.py:20
  27.5 8.7 %collective-permute-start.9 = (f32[256,256]{1,0:T(8,128)S(1)}, f32[256,256]{1,0:T(8,128)S(1)}, u32[]{:S(2)}, u32[]{:S(2)}) collective-permute-start(f32[256,256]{1,0:T(8,128)S(1)} %slice.87), channel_id=1, source_target_pairs={{0,8},{2,10},{4,12},{6,14},{8,0},{10,2},{12,4},{14,6},{16,24},{18,... | collective-permute-start | bytes 786440 | tf_op jit(solution)/shard_map/ppermute | solution.py:20
  34.4 5.0 %collective-permute-start.6 = (f32[128,256]{1,0:T(8,128)S(1)}, f32[128,256]{1,0:T(8,128)S(1)}, u32[]{:S(2)}, u32[]{:S(2)}) collective-permute-start(f32[128,256]{1,0:T(8,128)S(1)} %slice.83), channel_id=1, source_target_pairs={{0,8},{2,10},{4,12},{6,14},{8,0},{10,2},{12,4},{14,6},{16,24},{18,... | collective-permute-start | bytes 393224 | tf_op jit(solution)/shard_map/ppermute | solution.py:20
  36.2 6.0 %collective-permute-start.10 = (f32[128,256]{1,0:T(8,128)S(1)}, f32[128,256]{1,0:T(8,128)S(1)}, u32[]{:S(2)}, u32[]{:S(2)}) collective-permute-start(f32[128,256]{1,0:T(8,128)S(1)} %slice.89), channel_id=1, source_target_pairs={{0,4},{2,6},{4,0},{6,2},{8,12},{10,14},{12,8},{14,10},{16,20},{18,... | collective-permute-start | bytes 393224 | tf_op jit(solution)/shard_map/ppermute | solution.py:20
  39.4 6.8 %collective-permute-start.7 = (f32[64,256]{1,0:T(8,128)S(1)}, f32[64,256]{1,0:T(8,128)S(1)}, u32[]{:S(2)}, u32[]{:S(2)}) collective-permute-start(f32[64,256]{1,0:T(8,128)S(1)} %slice.85), channel_id=1, source_target_pairs={{0,16},{2,18},{4,20},{6,22},{8,24},{10,26},{12,28},{14,30},{16,0},... | collective-permute-start | bytes 196616 | tf_op jit(solution)/shard_map/ppermute | solution.py:20
  42.3 5.9 %collective-permute-start.11 = (f32[64,256]{1,0:T(8,128)S(1)}, f32[64,256]{1,0:T(8,128)S(1)}, u32[]{:S(2)}, u32[]{:S(2)}) collective-permute-start(f32[64,256]{1,0:T(8,128)S(1)} %slice.91), channel_id=1, source_target_pairs={{0,16},{2,18},{4,20},{6,22},{8,24},{10,26},{12,28},{14,30},{16,0},... | collective-permute-start | bytes 196616 | tf_op jit(solution)/shard_map/ppermute | solution.py:20
  46.3 4.3 %collective-permute-start.12 = (f32[64,256]{1,0:T(8,128)S(1)}, f32[64,256]{1,0:T(8,128)S(1)}, u32[]{:S(2)}, u32[]{:S(2)}) collective-permute-start(f32[64,256]{1,0:T(8,128)S(1)} %slice_add_fusion.7.refs_0_), channel_id=1, source_target_pairs={{0,1},{1,0},{2,3},{3,2},{4,5},{5,4},{6,7},{7,6},{8,9},{9,8},{10,11... | collective-permute-start | bytes 196616 | tf_op jit(solution)/shard_map/ppermute | solution.py:455
  48.2 4.3 %collective-permute-start.13 = (f32[64,256]{1,0:T(8,128)S(1)}, f32[64,256]{1,0:T(8,128)S(1)}, u32[]{:S(2)}, u32[]{:S(2)}) collective-permute-start(f32[64,256]{1,0:T(8,128)S(1)} %slice_add_fusion.6.refs_2_), channel_id=1, source_target_pairs={{0,1},{1,0},{2,3},{3,2},{4,5},{5,4},{6,7},{7,6},{8,9},{9,8},{10,11... | collective-permute-start | bytes 196616 | tf_op jit(solution)/shard_map/ppermute | solution.py:455
  54.8 4.6 %collective-permute-start.22 = (f32[2,80,128]{2,1,0:T(8,128)S(1)}, f32[2,80,128]{2,1,0:T(8,128)S(1)}, u32[]{:S(2)}, u32[]{:S(2)}) collective-permute-start(f32[2,80,128]{2,1,0:T(8,128)S(1)} %slice.97), channel_id=1, source_target_pairs={{0,8},{2,10},{4,12},{6,14},{8,0},{10,2},{12,4},{14,6},{16,24},{18,... | collective-permute-start | bytes 245768 | tf_op jit(solution)/shard_map/ppermute | solution.py:20
  55.1 4.9 %collective-permute-start.15 = (f32[2,80,128]{2,1,0:T(8,128)S(1)}, f32[2,80,128]{2,1,0:T(8,128)S(1)}, u32[]{:S(2)}, u32[]{:S(2)}) collective-permute-start(f32[2,80,128]{2,1,0:T(8,128)S(1)} %slice.93), channel_id=1, source_target_pairs={{0,4},{2,6},{4,0},{6,2},{8,12},{10,14},{12,8},{14,10},{16,20},{18,... | collective-permute-start | bytes 245768 | tf_op jit(solution)/shard_map/ppermute | solution.py:20
  59.4 4.1 %collective-permute-start.23 = (f32[1,80,128]{2,1,0:T(8,128)S(1)}, f32[1,80,128]{2,1,0:T(8,128)S(1)}, u32[]{:S(2)}, u32[]{:S(2)}) collective-permute-start(f32[1,80,128]{2,1,0:T(8,128)S(1)} %slice.99), channel_id=1, source_target_pairs={{0,4},{2,6},{4,0},{6,2},{8,12},{10,14},{12,8},{14,10},{16,20},{18,... | collective-permute-start | bytes 122888 | tf_op jit(solution)/shard_map/ppermute | solution.py:20
  60.0 4.6 %collective-permute-start.16 = (f32[1,80,128]{2,1,0:T(8,128)S(1)}, f32[1,80,128]{2,1,0:T(8,128)S(1)}, u32[]{:S(2)}, u32[]{:S(2)}) collective-permute-start(f32[1,80,128]{2,1,0:T(8,128)S(1)} %slice.95), channel_id=1, source_target_pairs={{0,8},{2,10},{4,12},{6,14},{8,0},{10,2},{12,4},{14,6},{16,24},{18,... | collective-permute-start | bytes 122888 | tf_op jit(solution)/shard_map/ppermute | solution.py:20
  63.5 5.1 %collective-permute-start.24 = (f32[1,80,128]{2,1,0:T(8,128)S(1)}, f32[1,80,128]{2,1,0:T(8,128)S(1)}, u32[]{:S(2)}, u32[]{:S(2)}) collective-permute-start(f32[1,80,128]{2,1,0:T(8,128)S(1)} %slice_add_fusion.8), channel_id=1, source_target_pairs={{0,16},{2,18},{4,20},{6,22},{8,24},{10,26},{12,28},{14,30},{16,0},... | collective-permute-start | bytes 122888 | tf_op jit(solution)/shard_map/ppermute | solution.py:20
  64.6 5.0 %collective-permute-start.17 = (f32[1,80,128]{2,1,0:T(8,128)S(1)}, f32[1,80,128]{2,1,0:T(8,128)S(1)}, u32[]{:S(2)}, u32[]{:S(2)}) collective-permute-start(f32[1,80,128]{2,1,0:T(8,128)S(1)} %slice_add_fusion.9), channel_id=1, source_target_pairs={{0,16},{2,18},{4,20},{6,22},{8,24},{10,26},{12,28},{14,30},{16,0},... | collective-permute-start | bytes 122888 | tf_op jit(solution)/shard_map/ppermute | solution.py:20
  68.6 4.1 %collective-permute-start.25 = (f32[1,80,128]{2,1,0:T(8,128)S(1)}, f32[1,80,128]{2,1,0:T(8,128)S(1)}, u32[]{:S(2)}, u32[]{:S(2)}) collective-permute-start(f32[1,80,128]{2,1,0:T(8,128)S(1)} %add.64), channel_id=1, source_target_pairs={{0,4},{2,6},{4,0},{6,2},{8,12},{10,14},{12,8},{14,10},{16,20},{18,... | collective-permute-start | bytes 122888 | tf_op jit(solution)/shard_map/ppermute | solution.py:20
  69.6 4.0 %collective-permute-start.18 = (f32[1,80,128]{2,1,0:T(8,128)S(1)}, f32[1,80,128]{2,1,0:T(8,128)S(1)}, u32[]{:S(2)}, u32[]{:S(2)}) collective-permute-start(f32[1,80,128]{2,1,0:T(8,128)S(1)} %add.60), channel_id=1, source_target_pairs={{0,8},{2,10},{4,12},{6,14},{8,0},{10,2},{12,4},{14,6},{16,24},{18,... | collective-permute-start | bytes 122888 | tf_op jit(solution)/shard_map/ppermute | solution.py:20
  72.7 4.4 %collective-permute-start.26 = (f32[2,80,128]{2,1,0:T(8,128)S(1)}, f32[2,80,128]{2,1,0:T(8,128)S(1)}, u32[]{:S(2)}, u32[]{:S(2)}) collective-permute-start(f32[2,80,128]{2,1,0:T(8,128)S(1)} %pad_maximum_fusion.4), channel_id=1, source_target_pairs={{0,8},{2,10},{4,12},{6,14},{8,0},{10,2},{12,4},{14,6},{16,24},{18,... | collective-permute-start | bytes 245768 | tf_op jit(solution)/shard_map/ppermute | solution.py:20
  73.7 4.4 %collective-permute-start.19 = (f32[2,80,128]{2,1,0:T(8,128)S(1)}, f32[2,80,128]{2,1,0:T(8,128)S(1)}, u32[]{:S(2)}, u32[]{:S(2)}) collective-permute-start(f32[2,80,128]{2,1,0:T(8,128)S(1)} %pad_maximum_fusion.3), channel_id=1, source_target_pairs={{0,4},{2,6},{4,0},{6,2},{8,12},{10,14},{12,8},{14,10},{16,20},{18,... | collective-permute-start | bytes 245768 | tf_op jit(solution)/shard_map/ppermute | solution.py:20
  77.2 1.7 %collective-permute-start.27 = (f32[4,80,128]{2,1,0:T(8,128)S(1)}, f32[4,80,128]{2,1,0:T(8,128)S(1)}, u32[]{:S(2)}, u32[]{:S(2)}) collective-permute-start(f32[4,80,128]{2,1,0:T(8,128)S(1)} %pad_maximum_fusion.1.refs_2_), channel_id=1, source_target_pairs={{0,2},{2,0},{4,6},{6,4},{8,10},{10,8},{12,14},{14,12},{16,18},{18,... | collective-permute-start | bytes 491528 | tf_op jit(solution)/shard_map/ppermute | solution.py:20
  (4 other events, 6.0 us)
